TPU v7x, 256 devices: a whole 4x4x8 slice. The times are simulated.
256 devices in a mesh: pb: 64 (over x, z_hi, y), ka: 4 (over z_lo, core).
Axes of the slice: x: 4, y: 4, z: 8 (z_hi: 4, z_lo: 2; z = z_hi * 2 + z_lo), core: 2. Of those that a mesh axis runs over, the one named last changes fastest.
Arguments:
- coupling: bfloat16 [2, 320, 4800, 320], P(None, 'ka', 'pb'), may hold values from -0.019897461 to 0.019897461
- kpoints: int32 [3, 16], replicated, may hold values from 0 to 99
- qpoints: int32 [3, 256], replicated, may hold values from 0 to 99
- electron_cells: int32 [3, 320], replicated, may hold values from -6 to 6
- phonon_cells: int32 [3, 320], replicated, may hold values from -6 to 6
- phonon_modes: bfloat16 [256, 2, 120, 120], P('pb'), may hold values from -0.375 to 0.375
- band_vectors: bfloat16 [256, 16, 2, 40, 40], P('pb', 'ka'), may hold values from -0.625 to 0.625
- energies_kq: float32 [256, 16, 40], P('pb', 'ka'), may hold values from -0.5 to 0.5
- occupations_kq: float32 [256, 16, 40], P('pb', 'ka'), may hold values from 0 to 1
- energy_k: float32 [16], P('ka'), may hold values from -0.5 to 0.5
- occupation_k: float32 [16], P('ka'), may hold values from 0 to 1
- frequencies: float32 [256, 120], P('pb'), may hold values from 0.02 to 0.2
- bose_factors: float32 [256, 120], P('pb'), may hold values from 0.1 to 5
Outputs:
- electron_width: float32 [16, 120], P('ka')
- phonon_width: float32 [256, 120], P('pb')
All inputs are finite; a program needn't handle non-finite values.
Results may differ from a plain program's by a relative error of at most 0.0066.
Values may be sent and summed in bfloat16 or wider, within the bound.
No kernel may reach another device: no remote copies, remote signals or barrier semaphores. Data moves between devices by JAX's collectives and lax.ppermute only.
A program may use at most 128 MiB of HBM per device.

v0:
```python
import math

import jax
import jax.numpy as jnp
from jax import lax
from jax.sharding import PartitionSpec as P

NB = 40
MODES = 120
NG = 100


smearing = 0.05


def split_up(shard, dim, count):
    dims = shard.shape
    pieces = shard.reshape(*dims[:dim], count, dims[dim] // count, *dims[dim + 1 :])
    return jnp.moveaxis(pieces, dim, 0)


def sum_at_owner(shard, axis, dim):
    pieces = split_up(shard, dim, lax.axis_size(axis))
    arrived = lax.all_to_all(pieces, axis, split_axis=0, concat_axis=0, tiled=True)
    return arrived.sum(axis=0)


def in_one_piece(arrays, axis, split_dim, concat_dim, along):
    both = jnp.concatenate(arrays, axis=along)
    filled, at, done = (
        lax.all_to_all(both, axis, split_axis=split_dim, concat_axis=concat_dim, tiled=True),
        0,
        [],
    )
    for a in arrays:
        done.append(lax.slice_in_dim(filled, at, at + a.shape[along], axis=along))
        at += a.shape[along]
    return tuple(done)


def sent_to_all(shard, axis):
    count = lax.axis_size(axis)
    return lax.all_to_all(
        jnp.broadcast_to(shard[None], (count, *shard.shape)), axis, 0, 0, tiled=True
    )


def of_everyone(shard, axis):
    return sent_to_all(shard, axis).sum(axis=0)


def phase_table(points, cells):
    product = (
        points[0][:, None] * cells[0][None, :]
        + points[1][:, None] * cells[1][None, :]
        + points[2][:, None] * cells[2][None, :]
    )
    angle = jnp.mod(product, NG).astype(jnp.float32) * (2.0 * math.pi / NG)
    return (jnp.cos(angle).astype(jnp.bfloat16), jnp.sin(angle).astype(jnp.bfloat16))


def gaussian(offset):
    return jnp.exp(-0.5 * (offset / smearing) ** 2) / (smearing * math.sqrt(2.0 * math.pi))


def contract_last(left, right):
    return lax.dot_general(
        left, right, (((1,), (1,)), ((), ())), preferred_element_type=jnp.float32
    )


def mixed(form, left, right):
    return jnp.einsum(form, left, right, preferred_element_type=jnp.float32)


def widths(
    bloch_real, bloch_imag, modes, vectors, levels, filled, energy_k, occupation_k, omega, bose
):
    mode_real = modes[:, 0]
    mode_imag = modes[:, 1]
    moded_real = (
        mixed("kqnm,qmv->kqnv", bloch_real, mode_real)
        - mixed("kqnm,qmv->kqnv", bloch_imag, mode_imag)
    ).astype(jnp.bfloat16)
    moded_imag = (
        mixed("kqnm,qmv->kqnv", bloch_real, mode_imag)
        + mixed("kqnm,qmv->kqnv", bloch_imag, mode_real)
    ).astype(jnp.bfloat16)
    vector_real = vectors[:, :, 0]
    vector_imag = vectors[:, :, 1]
    band_real = mixed("qknb,kqnv->kqbv", vector_real, moded_real) + mixed(
        "qknb,kqnv->kqbv", vector_imag, moded_imag
    )
    band_imag = mixed("qknb,kqnv->kqbv", vector_real, moded_imag) - mixed(
        "qknb,kqnv->kqbv", vector_imag, moded_real
    )
    weight = band_real * band_real + band_imag * band_imag
    level_kq = jnp.transpose(levels, (1, 0, 2))[..., None]
    filled_kq = jnp.transpose(filled, (1, 0, 2))[..., None]
    offset = energy_k[:, None, None, None] - level_kq
    freq = omega[None, :, None, :]
    boson = bose[None, :, None, :]
    absorb = gaussian(offset + freq)
    emit = gaussian(offset - freq)
    electron = jnp.sum(
        weight * ((boson + filled_kq) * absorb + (boson + 1.0 - filled_kq) * emit), axis=(1, 2)
    )
    phonon = jnp.sum(weight * (occupation_k[:, None, None, None] - filled_kq) * absorb, axis=(0, 2))
    return (electron, phonon)


def on_device(
    coupling,
    kpoints,
    qpoints,
    electron_cells,
    phonon_cells,
    phonon_modes,
    band_vectors,
    energies_kq,
    occupations_kq,
    energy_k,
    occupation_k,
    frequencies,
    bose_factors,
):
    k_local = energy_k.shape[0]
    q_local = frequencies.shape[0]
    cells_local = coupling.shape[1]
    pairs_local = coupling.shape[2]
    phonon_count = coupling.shape[3]
    q_total = q_local * lax.axis_size("pb")
    k_total = k_local * lax.axis_size("ka")
    cos_q, sin_q = phase_table(qpoints, phonon_cells)
    cos_k, sin_k = phase_table(kpoints, electron_cells)
    real_flat = coupling[0].reshape(cells_local * pairs_local, phonon_count)
    imag_flat = coupling[1].reshape(cells_local * pairs_local, phonon_count)
    half_real = (
        (contract_last(cos_q, real_flat) - contract_last(sin_q, imag_flat))
        .astype(jnp.bfloat16)
        .reshape(q_total, cells_local, pairs_local)
    )
    half_imag = (
        (contract_last(cos_q, imag_flat) + contract_last(sin_q, real_flat))
        .astype(jnp.bfloat16)
        .reshape(q_total, cells_local, pairs_local)
    )
    cell_start = lax.axis_index("ka") * cells_local
    cos_cols = lax.dynamic_slice_in_dim(cos_k, cell_start, cells_local, 1)
    sin_cols = lax.dynamic_slice_in_dim(sin_k, cell_start, cells_local, 1)
    real_part = mixed("kr,qrp->kqp", cos_cols, half_real) - mixed(
        "kr,qrp->kqp", sin_cols, half_imag
    )
    imag_part = mixed("kr,qrp->kqp", cos_cols, half_imag) + mixed(
        "kr,qrp->kqp", sin_cols, half_real
    )
    partials = sum_at_owner(jnp.stack([real_part, imag_part], axis=1), "ka", 0)
    owned_real = partials[:, 0].astype(jnp.bfloat16)
    owned_imag = partials[:, 1].astype(jnp.bfloat16)
    bloch_real, bloch_imag = in_one_piece((owned_real, owned_imag), "pb", 1, 2, 0)
    bloch_real = bloch_real.reshape(k_local, q_local, NB, MODES)
    bloch_imag = bloch_imag.reshape(k_local, q_local, NB, MODES)
    electron, phonon = widths(
        bloch_real,
        bloch_imag,
        phonon_modes,
        band_vectors,
        energies_kq,
        occupations_kq,
        energy_k,
        occupation_k,
        frequencies,
        bose_factors,
    )
    electron_width = of_everyone(electron / (q_total * NB), "pb")
    phonon_width = of_everyone(phonon / (k_total * NB), "ka")
    return (electron_width, phonon_width)


def solution(mesh):
    in_specs = (
        P(None, "ka", "pb", None),
        P(),
        P(),
        P(),
        P(),
        P("pb", None, None, None),
        P("pb", "ka", None, None, None),
        P("pb", "ka", None),
        P("pb", "ka", None),
        P("ka"),
        P("ka"),
        P("pb", None),
        P("pb", None),
    )
    out_specs = (P("ka", None), P("pb", None))
    return jax.shard_map(
        on_device, mesh=mesh, in_specs=in_specs, out_specs=out_specs, check_vma=False
    )
```

profile of v0, /device:TPU:32, one launch (start us, length us, event | category | flops | bytes accessed | tf_op | source)
XLA Modules:
  0.0 180.0 jit_solution(16729167819854023712)
XLA Ops:
  0.6 0.8 slice_bitcast_fusion.4
  1.4 0.8 fusion.81
  2.2 0.8 slice_reduce_fusion.5
  3.1 0.8 slice_reduce_fusion.2
  3.9 6.8 %fusion.78 = (bf16[1,80,75,320]{3,1,2,0:T(8,128)(2,1)S(1)}, bf16[1,80,75,320]{3,1,2,0:T(8,128)(2,1)}) fusion(bf16[2,80,75,320]{3,1,2,0:T(8,128)(2,1)} %param.13), kind=kLoop, calls=%fused_computation.105 | loop fusion | bytes 15360000 | tf_op jit(solution)/shard_map/slice | solution.py:136
  10.7 3.2 %copy.143 = bf16[1,80,75,320]{3,2,1,0:T(8,128)(2,1)} copy(bf16[1,80,75,320]{3,1,2,0:T(8,128)(2,1)S(1)} %get-tuple-element.10) | data formatting | bytes 7680000 | tf_op jit(solution)/shard_map/slice | solution.py:136
  14.0 7.3 %reshape_squeeze.6 = bf16[6000,320]{1,0:T(8,128)(2,1)} reshape(bf16[1,80,75,320]{3,2,1,0:T(8,128)(2,1)} %copy.143) | data formatting | bytes 7680000 | tf_op jit(solution)/shard_map/reshape;squeeze | solution.py:136
  21.3 5.5 %copy.144 = bf16[1,80,75,320]{3,2,1,0:T(8,128)(2,1)} copy(bf16[1,80,75,320]{3,1,2,0:T(8,128)(2,1)} %get-tuple-element.11) | data formatting | bytes 7680000 | tf_op jit(solution)/shard_map/slice | solution.py:137
  26.8 7.3 %reshape_squeeze.7 = bf16[6000,320]{1,0:T(8,128)(2,1)} reshape(bf16[1,80,75,320]{3,2,1,0:T(8,128)(2,1)} %copy.144) | data formatting | bytes 7680000 | tf_op jit(solution)/shard_map/reshape;squeeze | solution.py:137
  34.1 5.8 %fusion.39 = f32[256,6000]{0,1:T(8,128)S(1)} fusion(bf16[6000,320]{1,0:T(8,128)(2,1)} %reshape_squeeze.7, s32[320]{0:T(512)S(1)} %get-tuple-element.8, s32[256]{0:T(256)S(1)} %bitcast.101, s32[320]{0:T(512)S(1)} %get-tuple-element.9, s32[256]{0:T(256)S(1)} %bitcast.105, s32[320]{0:T(512)S(1)} %get-tuple-element.7, s32[256]{0:T(256)S(1)} %bitcast.97), kind=kOutput, calls=%fused_computation.52 | convolution fusion | flops 984186880 | bytes 9990912 | tf_op jit(solution)/shard_map/dot_general | solution.py:67
  39.9 6.4 %fusion.1 = bf16[256,6000]{0,1:T(8,128)(2,1)} fusion(f32[256,6000]{0,1:T(8,128)S(1)} %fusion.39, bf16[6000,320]{1,0:T(8,128)(2,1)S(1)} %bitcast.93, s32[320]{0:T(512)S(1)} %get-tuple-element.8, s32[256]{0:T(256)S(1)} %bitcast.102, s32[320]{0:T(512)S(1)} %get-tuple-element.9, s32[256]{0:T(256)S(1)} %bitcast.106, s32[320]{0:T(512)S(1)} %get-tuple-element.7, ...), kind=kOutput, calls=%fused_computation.3 | convolution fusion | flops 987258880 | bytes 13062912 | tf_op jit(solution)/shard_map/dot_general | solution.py:67
  46.3 4.0 %reshape.55 = bf16[256,80,75]{0,2,1:T(8,128)(2,1)S(1)} reshape(bf16[256,6000]{0,1:T(8,128)(2,1)} %fusion.1) | data formatting | bytes 6144000 | tf_op jit(solution)/shard_map/reshape | solution.py:146
  50.5 2.1 %fusion.2 = f32[16,256,75]{1,0,2:T(8,128)} fusion(bf16[256,80,75]{0,2,1:T(8,128)(2,1)S(1)} %reshape.55, f32[16,320]{1,0:T(8,128)S(1)} %fusion.52, s32[]{:T(128)S(6)} %select_n.18), kind=kOutput, calls=%fused_computation.4 | convolution fusion | flops 49153280 | bytes 4513796 | tf_op jit(solution)/shard_map/kr,qrp->kqp/dot_general | solution.py:73
  52.6 2.1 %fusion.4 = f32[16,256,75]{1,0,2:T(8,128)} fusion(bf16[256,80,75]{0,2,1:T(8,128)(2,1)S(1)} %reshape.55, f32[16,320]{1,0:T(8,128)S(1)} %fusion.52, s32[]{:T(128)S(6)} %select_n.18), kind=kOutput, calls=%fused_computation.6 | convolution fusion | flops 49153280 | bytes 4513796 | tf_op jit(solution)/shard_map/kr,qrp->kqp/dot_general | solution.py:73
  54.7 3.3 %fusion.40 = f32[256,6000]{0,1:T(8,128)S(1)} fusion(bf16[6000,320]{1,0:T(8,128)(2,1)S(1)} %bitcast.95, s32[320]{0:T(512)S(1)} %get-tuple-element.8, s32[256]{0:T(256)S(1)} %bitcast.103, s32[320]{0:T(512)S(1)} %get-tuple-element.9, s32[256]{0:T(256)S(1)} %bitcast.107, s32[320]{0:T(512)S(1)} %get-tuple-element.7, s32[256]{0:T(256)S(1)} %bitcast.99), kind=kOutput, calls=%fused_computation.53 | convolution fusion | flops 984186880 | bytes 9990912 | tf_op jit(solution)/shard_map/dot_general | solution.py:67
  58.0 6.6 %fusion = bf16[256,6000]{0,1:T(8,128)(2,1)} fusion(f32[256,6000]{0,1:T(8,128)S(1)} %fusion.40, bf16[6000,320]{1,0:T(8,128)(2,1)S(1)} %bitcast.91, s32[320]{0:T(512)S(1)} %get-tuple-element.8, s32[256]{0:T(256)S(1)} %bitcast.104, s32[320]{0:T(512)S(1)} %get-tuple-element.9, s32[256]{0:T(256)S(1)} %bitcast.108, s32[320]{0:T(512)S(1)} %get-tuple-element.7, ...), kind=kOutput, calls=%fused_computation.2 | convolution fusion | flops 987258880 | bytes 13062912 | tf_op jit(solution)/shard_map/dot_general | solution.py:67
  64.6 3.8 %reshape.54 = bf16[256,80,75]{0,2,1:T(8,128)(2,1)S(1)} reshape(bf16[256,6000]{0,1:T(8,128)(2,1)} %fusion) | data formatting | bytes 6144000 | tf_op jit(solution)/shard_map/reshape | solution.py:141
  68.5 3.5 %fusion.13 = f32[16,256,75]{1,0,2:T(8,128)} fusion(f32[16,256,75]{1,0,2:T(8,128)} %fusion.2, bf16[256,80,75]{0,2,1:T(8,128)(2,1)S(1)} %reshape.54, f32[16,320]{1,0:T(8,128)S(1)} %fusion.52, s32[]{:T(128)S(6)} %select_n.18), kind=kOutput, calls=%fused_computation.14 | convolution fusion | flops 49460480 | bytes 5742596 | tf_op jit(solution)/shard_map/kr,qrp->kqp/dot_general | solution.py:73
  72.0 2.1 %fusion.10 = f32[16,256,75]{1,0,2:T(8,128)} fusion(f32[16,256,75]{1,0,2:T(8,128)S(1)} %copy-done, bf16[256,80,75]{0,2,1:T(8,128)(2,1)S(1)} %reshape.54, f32[16,320]{1,0:T(8,128)S(1)} %fusion.52, s32[]{:T(128)S(6)} %select_n.18), kind=kOutput, calls=%fused_computation.13 | convolution fusion | flops 49460480 | bytes 5742596 | tf_op jit(solution)/shard_map/kr,qrp->kqp/dot_general | solution.py:73
  74.1 2.0 %stack.9 = f32[4,4,1,256,75]{3,1,0,4,2:T(4,128)S(1)} reshape(f32[16,256,75]{1,0,2:T(8,128)} %fusion.10) | data formatting | bytes 2457600 | tf_op jit(solution)/shard_map/stack | solution.py:157
  76.1 1.4 stack.10
  77.5 1.9 %pad_maximum_fusion = f32[4,4,2,256,75]{3,1,0,4,2:T(4,128)S(1)} fusion(f32[4,4,1,256,75]{3,1,0,4,2:T(4,128)} %stack.10, f32[4,4,1,256,75]{3,1,0,4,2:T(4,128)S(1)} %stack.9), kind=kLoop, calls=%fused_computation.12 | loop fusion | flops 614400 | bytes 4915200 | tf_op jit(solution)/shard_map/stack | solution.py:157
  79.4 1.9 %copy.169 = f32[4,4,2,256,75]{3,1,4,2,0:T(4,128)} copy(f32[4,4,2,256,75]{3,1,0,4,2:T(4,128)S(1)} %pad_maximum_fusion) | data formatting | bytes 4915200 | tf_op jit(solution)/shard_map/stack | solution.py:157
  81.3 5.6 %all-to-all-start = ((f32[4,4,2,256,75]{3,1,4,2,0:T(4,128)}), f32[4,4,2,256,75]{3,1,4,2,0:T(4,128)S(1)}, u32[]{:S(2)}, u32[]{:S(2)}) async-start(f32[4,4,2,256,75]{3,1,4,2,0:T(4,128)} %copy.169), calls=%async_computation | async-start | bytes 4915200 | tf_op jit(solution)/shard_map/all_to_all | solution.py:24
  87.0 27.8 %all-to-all-done = f32[4,4,2,256,75]{3,1,4,2,0:T(4,128)S(1)} async-done(((f32[4,4,2,256,75]{3,1,4,2,0:T(4,128)}), f32[4,4,2,256,75]{3,1,4,2,0:T(4,128)S(1)}, u32[]{:S(2)}, u32[]{:S(2)}) %all-to-all-start) | async-done | bytes 2457632 | tf_op jit(solution)/shard_map/all_to_all | solution.py:24
  115.8 1.3 copy.152
  117.0 12.8 %all-to-all-start.1 = ((bf16[8,256,75]{2,0,1:T(8,128)(2,1)}), bf16[8,256,75]{2,0,1:T(8,128)(2,1)S(1)}, u32[]{:S(2)}, u32[]{:S(2)}) async-start(bf16[8,256,75]{2,0,1:T(8,128)(2,1)} %copy.152), calls=%async_computation.1 | async-start | bytes 1048576 | tf_op jit(solution)/shard_map/all_to_all | solution.py:31
  130.3 18.4 %all-to-all-done.1 = bf16[8,256,75]{2,0,1:T(8,128)(2,1)S(1)} async-done(((bf16[8,256,75]{2,0,1:T(8,128)(2,1)}), bf16[8,256,75]{2,0,1:T(8,128)(2,1)S(1)}, u32[]{:S(2)}, u32[]{:S(2)}) %all-to-all-start.1) | async-done | bytes 307232 | tf_op jit(solution)/shard_map/all_to_all | solution.py:31
  152.7 6.0 %all-to-all-start.3 = ((f32[4,4,120]{2,1,0:T(4,128)}), f32[4,4,120]{2,1,0:T(4,128)S(1)}, u32[]{:S(2)}, u32[]{:S(2)}) async-start(f32[4,4,120]{2,1,0:T(4,128)} %broadcast_in_dim.5), calls=%async_computation.3 | async-start | bytes 16384 | tf_op jit(solution)/shard_map/all_to_all | solution.py:43
  158.7 1.8 %all-to-all-done.3 = f32[4,4,120]{2,1,0:T(4,128)S(1)} async-done(((f32[4,4,120]{2,1,0:T(4,128)}), f32[4,4,120]{2,1,0:T(4,128)S(1)}, u32[]{:S(2)}, u32[]{:S(2)}) %all-to-all-start.3) | async-done | bytes 7712 | tf_op jit(solution)/shard_map/all_to_all | solution.py:43
  161.2 5.4 %all-to-all-start.2 = ((f32[64,4,120]{2,1,0:T(4,128)}), f32[64,4,120]{2,1,0:T(4,128)S(1)}, u32[]{:S(2)}, u32[]{:S(2)}) async-start(f32[64,4,120]{2,1,0:T(4,128)} %broadcast_in_dim.4), calls=%async_computation.2 | async-start | bytes 262144 | tf_op jit(solution)/shard_map/all_to_all | solution.py:43
  167.2 12.1 %all-to-all-done.2 = f32[64,4,120]{2,1,0:T(4,128)S(1)} async-done(((f32[64,4,120]{2,1,0:T(4,128)}), f32[64,4,120]{2,1,0:T(4,128)S(1)}, u32[]{:S(2)}, u32[]{:S(2)}) %all-to-all-start.2) | async-done | bytes 122912 | tf_op jit(solution)/shard_map/all_to_all | solution.py:43
  (67 shorter events, 7.3 us)
Async XLA Ops:
  26.8 13.1 %slice-start.2 = ((s8[4608000]{0:T(1024)(128)(4,1)}), s8[413696]{0:T(1024)(128)(4,1)S(1)}, s32[]{:S(2)}) async-start(s8[4608000]{0:T(1024)(128)(4,1)} %bitcast.92), calls=%async_computation.6 | async-start | bytes 827392
  34.1 5.8 %slice-start.3 = ((s8[4608000]{0:T(1024)(128)(4,1)}), s8[4194304]{0:T(1024)(128)(4,1)S(1)}, s32[]{:S(2)}) async-start(s8[4608000]{0:T(1024)(128)(4,1)} %bitcast.92), calls=%async_computation.7 | async-start | bytes 8388608
  50.4 4.3 %slice-start.4 = ((s8[4608000]{0:T(1024)(128)(4,1)}), s8[4194304]{0:T(1024)(128)(4,1)S(1)}, s32[]{:S(2)}) async-start(s8[4608000]{0:T(1024)(128)(4,1)} %bitcast.94), calls=%async_computation.8 | async-start | bytes 8388608
  50.5 4.2 %slice-start.5 = ((s8[4608000]{0:T(1024)(128)(4,1)}), s8[413696]{0:T(1024)(128)(4,1)S(1)}, s32[]{:S(2)}) async-start(s8[4608000]{0:T(1024)(128)(4,1)} %bitcast.94), calls=%async_computation.9 | async-start | bytes 827392
  52.6 5.4 %slice-start = ((s8[4608000]{0:T(1024)(128)(4,1)}), s8[4194304]{0:T(1024)(128)(4,1)S(1)}, s32[]{:S(2)}) async-start(s8[4608000]{0:T(1024)(128)(4,1)} %bitcast.90), calls=%async_computation.4 | async-start | bytes 8388608
  54.7 3.4 %slice-start.1 = ((s8[4608000]{0:T(1024)(128)(4,1)}), s8[413696]{0:T(1024)(128)(4,1)S(1)}, s32[]{:S(2)}) async-start(s8[4608000]{0:T(1024)(128)(4,1)} %bitcast.90), calls=%async_computation.5 | async-start | bytes 827392
  68.5 3.5 %copy-start = (f32[16,256,75]{1,0,2:T(8,128)S(1)}, f32[16,256,75]{1,0,2:T(8,128)}, u32[]{:S(2)}) copy-start(f32[16,256,75]{1,0,2:T(8,128)} %fusion.4) | copy-start | bytes 3686404
  74.1 2.0 %copy-start.1 = (f32[16,256,75]{1,0,2:T(8,128)S(1)}, f32[16,256,75]{1,0,2:T(8,128)}, u32[]{:S(2)}) copy-start(f32[16,256,75]{1,0,2:T(8,128)} %fusion.13) | copy-start | bytes 3686404
  81.3 5.6 %copy-start.5 = (f32[4,4,40]{2,1,0:T(4,128)S(1)}, f32[4,4,40]{2,1,0:T(4,128)}, u32[]{:S(2)}) copy-start(f32[4,4,40]{2,1,0:T(4,128)} %param.20) | copy-start | bytes 7684
  81.3 5.6 %copy-start.7 = (f32[4]{0:T(128)S(1)}, f32[4]{0:T(128)}, u32[]{:S(2)}) copy-start(f32[4]{0:T(128)} %param.22) | copy-start | bytes 52
  81.3 33.5 %all-to-all-start = ((f32[4,4,2,256,75]{3,1,4,2,0:T(4,128)}), f32[4,4,2,256,75]{3,1,4,2,0:T(4,128)S(1)}, u32[]{:S(2)}, u32[]{:S(2)}) async-start(f32[4,4,2,256,75]{3,1,4,2,0:T(4,128)} %copy.169), calls=%async_computation | async-start | bytes 4915200 | tf_op jit(solution)/shard_map/all_to_all | solution.py:24
  86.9 43.0 %copy-start.4 = (f32[4,4,40]{2,1,0:T(4,128)S(1)}, f32[4,4,40]{2,1,0:T(4,128)}, u32[]{:S(2)}) copy-start(f32[4,4,40]{2,1,0:T(4,128)} %param.21) | copy-start | bytes 7684
  86.9 43.0 %copy-start.8 = (f32[4]{0:T(128)S(1)}, f32[4]{0:T(128)}, u32[]{:S(2)}) copy-start(f32[4]{0:T(128)} %param.23) | copy-start | bytes 52
  86.9 43.1 %copy-start.3 = (bf16[4,4,2,40,40]{4,3,2,1,0:T(8,128)(2,1)S(1)}, bf16[4,4,2,40,40]{4,3,2,1,0:T(8,128)(2,1)}, u32[]{:S(2)}) copy-start(bf16[4,4,2,40,40]{4,3,2,1,0:T(8,128)(2,1)} %param.19) | copy-start | bytes 307204
  87.0 43.3 %copy-start.6 = (f32[4,120]{1,0:T(4,128)S(1)}, f32[4,120]{1,0:T(4,128)}, u32[]{:S(2)}) copy-start(f32[4,120]{1,0:T(4,128)} %param.25) | copy-start | bytes 5764
  115.5 33.9 %copy-start.2 = (bf16[4,2,120,120]{3,2,1,0:T(8,128)(2,1)S(1)}, bf16[4,2,120,120]{3,2,1,0:T(8,128)(2,1)}, u32[]{:S(2)}) copy-start(bf16[4,2,120,120]{3,2,1,0:T(8,128)(2,1)} %param.18) | copy-start | bytes 691204
  117.0 31.7 %all-to-all-start.1 = ((bf16[8,256,75]{2,0,1:T(8,128)(2,1)}), bf16[8,256,75]{2,0,1:T(8,128)(2,1)S(1)}, u32[]{:S(2)}, u32[]{:S(2)}) async-start(bf16[8,256,75]{2,0,1:T(8,128)(2,1)} %copy.152), calls=%async_computation.1 | async-start | bytes 1048576 | tf_op jit(solution)/shard_map/all_to_all | solution.py:31
  149.0 2.6 %copy-start.9 = (f32[4,120]{1,0:T(4,128)S(1)}, f32[4,120]{1,0:T(4,128)}, u32[]{:S(2)}) copy-start(f32[4,120]{1,0:T(4,128)} %param.24) | copy-start | bytes 5764
  152.7 7.9 %all-to-all-start.3 = ((f32[4,4,120]{2,1,0:T(4,128)}), f32[4,4,120]{2,1,0:T(4,128)S(1)}, u32[]{:S(2)}, u32[]{:S(2)}) async-start(f32[4,4,120]{2,1,0:T(4,128)} %broadcast_in_dim.5), calls=%async_computation.3 | async-start | bytes 16384 | tf_op jit(solution)/shard_map/all_to_all | solution.py:43
  161.2 18.2 %all-to-all-start.2 = ((f32[64,4,120]{2,1,0:T(4,128)}), f32[64,4,120]{2,1,0:T(4,128)S(1)}, u32[]{:S(2)}, u32[]{:S(2)}) async-start(f32[64,4,120]{2,1,0:T(4,128)} %broadcast_in_dim.4), calls=%async_computation.2 | async-start | bytes 262144 | tf_op jit(solution)/shard_map/all_to_all | solution.py:43
where the time goes:
time: 183 us; the launch traced here: 180 us
  waiting for transfers between devices  60.1 us (33%)
  local copies, waits for them, and re-layouts  50.7 us (28%)
  matrix products  34 us (19%)
  starting transfers between devices  29.9 us (16%)
  other arithmetic  4.26 us (2%)
    all_to_all x1, waiting for transfers between devices, sum_at_owner(): lax.all_to_all(pieces, axis, split_axis=0, concat_axis=0, tiled=True)  27.8 us
    dot_general x4, matrix products, contract_last(): lax.dot_general(left, right, (((1,), (1,)), ((), ())), preferred_element_...  22.2 us
    all_to_all x1, waiting for transfers between devices, in_one_piece(): lax.all_to_all(both, axis, split_axis=split_dim, concat_axis=concat_dim,...  18.4 us
    all_to_all x2, waiting for transfers between devices, sent_to_all(): lax.all_to_all(jnp.broadcast_to(shard[None], (count, *shard.shape)), axis...  13.9 us
    all_to_all x1, starting transfers between devices, in_one_piece(): lax.all_to_all(both, axis, split_axis=split_dim, concat_axis=concat_dim,...  12.8 us
    dot_general x12, matrix products, mixed(): return jnp.einsum(form, left, right, preferred_element_type=jnp.float32)  11.9 us
    all_to_all x2, starting transfers between devices, sent_to_all(): lax.all_to_all(jnp.broadcast_to(shard[None], (count, *shard.shape)), axis...  11.5 us
    slice x2, local copies, waits for them, and re-layouts, on_device(): real_flat = coupling[0].reshape(cells_local * pairs_local, phonon_count)  10.1 us
  transfers between devices with their start and end apart: 4, of which 4 were waited for; matrix products, arithmetic and copies ran while one was open for 1% of the time, Pallas kernels for 0%

commit v1 on v0

v1 whole, which is shorter than its diff:
```python
import math

import jax
import jax.numpy as jnp
from jax import lax
from jax.experimental import pallas as pl
from jax.experimental.pallas import tpu as pltpu
from jax.sharding import PartitionSpec as P

NB = 40
MODES = 120
NG = 100
SMEARING = 0.05

STRIP = 16
LANES = 128
PARTS = 8


def whole_turn_cosine(ticks):
    rest = ticks - NG * jnp.floor((ticks + 0.5) * (1.0 / NG))
    y = (jnp.abs(rest - NG // 2) - NG // 4) * (2.0 * math.pi / NG)
    z = y * y
    series = -1.0 / 39916800.0
    for term in (1.0 / 362880.0, -1.0 / 5040.0, 1.0 / 120.0, -1.0 / 6.0, 1.0):
        series = series * z + term
    return y * series


def small_dot(left, right, dims):
    return lax.dot_general(left, right, (dims, ((), ())), preferred_element_type=jnp.float32)


def product_kernel(
    kpt_ref, qpt_ref, ecell_ref, pcell_ref, g_ref, send_ref, keep_ref, table, mixer, rows
):
    step = pl.program_id(0)
    q_total = qpt_ref.shape[1]
    cells = g_ref.shape[2]
    groups = kpt_ref.shape[1] // 4
    bf16 = jnp.bfloat16

    @pl.when(step == 0)
    def _():
        mine = lax.axis_index("ka")
        kpt = kpt_ref[...].astype(jnp.float32).astype(bf16)
        qpt = qpt_ref[...].astype(jnp.float32).astype(bf16)
        ecell = ecell_ref[...].astype(jnp.float32).astype(bf16)
        pcell = pcell_ref[...].astype(jnp.float32).astype(bf16)
        source = lax.broadcasted_iota(jnp.int32, (kpt.shape[1], PARTS * groups), 0)
        row = lax.broadcasted_iota(jnp.int32, (kpt.shape[1], PARTS * groups), 1)
        wanted = jnp.bitwise_xor(row // PARTS, mine) * 4 + row % 4
        k_rows = small_dot(kpt, (source == wanted).astype(jnp.float32).astype(bf16), ((1,), (0,)))
        source = lax.broadcasted_iota(jnp.int32, (ecell.shape[1], 2 * cells), 0)
        col = lax.broadcasted_iota(jnp.int32, (ecell.shape[1], 2 * cells), 1)
        wanted = mine * cells + jnp.where(col >= cells, col - cells, col)
        e_cols = small_dot(ecell, (source == wanted).astype(jnp.float32).astype(bf16), ((1,), (0,)))
        ticks = small_dot(k_rows.astype(bf16), e_cols.astype(bf16), ((0,), (0,)))
        row = lax.broadcasted_iota(jnp.int32, ticks.shape, 0)
        col = lax.broadcasted_iota(jnp.int32, ticks.shape, 1)
        imaginary = row % PARTS >= 4
        second = col >= cells
        turn = jnp.where(imaginary, jnp.where(second, 0.0, -25.0), jnp.where(second, 25.0, 0.0))
        mixer[...] = whole_turn_cosine(ticks + turn).astype(bf16)
        ticks = small_dot(qpt, pcell, ((0,), (0,)))
        table[0:q_total, :] = whole_turn_cosine(ticks).astype(bf16)
        table[q_total : 2 * q_total, :] = whole_turn_cosine(ticks - 25.0).astype(bf16)

    mix = mixer[...]
    for j in range(STRIP):
        both = jnp.concatenate([g_ref[0, j], g_ref[1, j]], axis=0)
        value = jnp.dot(mix, both, preferred_element_type=jnp.float32)
        for t in range(rows.shape[0]):
            tile = value[:, t * LANES : (t + 1) * LANES]
            if tile.shape[1] < LANES:
                blank = jnp.zeros((tile.shape[0], LANES - tile.shape[1]), jnp.float32)
                tile = jnp.concatenate([tile, blank], axis=1)
            rows[t, pl.ds(j, PARTS * groups, stride=STRIP), :] = tile

    @pl.when(step == pl.num_programs(0) - 1)
    def _():
        empty = jnp.zeros((PARTS * groups, LANES), jnp.float32)
        for j in range(75 % STRIP, STRIP):
            for t in range(rows.shape[0]):
                rows[t, pl.ds(j, PARTS * groups, stride=STRIP), :] = empty

    every = jnp.concatenate([rows[t] for t in range(rows.shape[0])], axis=1)
    every = every[:, : table.shape[1]].astype(bf16)
    turned = small_dot(table[...], every, ((1,), (1,)))
    lane = lax.broadcasted_iota(jnp.int32, (q_total, LANES), 1)
    sign = jnp.where(lane < LANES // 2, -1.0, 1.0)
    for ref, slot, group in ((send_ref, 0, 3), (send_ref, 1, 1), (keep_ref, 0, 2), (keep_ref, 1, 0)):
        straight = turned[:q_total, group * LANES : (group + 1) * LANES]
        crossed = turned[q_total:, group * LANES : (group + 1) * LANES]
        ref[slot] = (straight + sign * pltpu.roll(crossed, LANES // 2, 1)).astype(bf16)


def products(kpoints, qpoints, electron_cells, phonon_cells, coupling):
    parts, cells, pairs, phonons = coupling.shape
    k_total = kpoints.shape[1]
    q_total = qpoints.shape[1]
    steps = pl.cdiv(pairs, STRIP)
    by_pair = jnp.transpose(coupling, (0, 2, 1, 3))
    whole = lambda a: pl.BlockSpec(a.shape, lambda i: (0, 0))
    out = jax.ShapeDtypeStruct((2, q_total, steps * LANES), jnp.bfloat16)
    out_spec = pl.BlockSpec((2, q_total, LANES), lambda i: (0, 0, i))
    return pl.pallas_call(
        product_kernel,
        grid=(steps,),
        in_specs=[
            whole(kpoints),
            whole(qpoints),
            whole(electron_cells),
            whole(phonon_cells),
            pl.BlockSpec((parts, STRIP, cells, phonons), lambda i: (0, i, 0, 0)),
        ],
        out_specs=[out_spec, out_spec],
        out_shape=[out, out],
        scratch_shapes=[
            pltpu.VMEM((2 * q_total, phonons), jnp.bfloat16),
            pltpu.VMEM((2 * k_total, 2 * cells), jnp.bfloat16),
            pltpu.VMEM((pl.cdiv(phonons, LANES), 2 * k_total * STRIP, LANES), jnp.float32),
        ],
        compiler_params=pltpu.CompilerParams(vmem_limit_bytes=48 << 20),
    )(kpoints, qpoints, electron_cells, phonon_cells, by_pair)


def table_kernel(
    level_ref, filled_ref, omega_ref, bose_ref, vector_ref, ek_ref, ok_ref,
    absorb_ref, count_ref, turned_ref, pick_ref,
):
    f32 = jnp.float32
    points = level_ref.shape[0]
    q_local = omega_ref.shape[0]
    level = jnp.transpose(level_ref[...])
    filled = jnp.transpose(filled_ref[...])
    scale = 1.0 / (SMEARING * math.sqrt(2.0 * math.pi))
    electron_scale = scale / (256 * NB)
    phonon_scale = scale / (16 * NB)
    for i in range(points):
        q, k = divmod(i, points // q_local)
        offset = ek_ref[k] - level[:, i : i + 1]
        f = filled[:, i : i + 1]
        w = omega_ref[q : q + 1, :]
        n = bose_ref[q : q + 1, :]
        up = jnp.exp(-0.5 * ((offset + w) / SMEARING) ** 2)
        down = jnp.exp(-0.5 * ((offset - w) / SMEARING) ** 2)
        absorb_ref[i] = ((n + f) * up + (n + 1.0 - f) * down) * electron_scale
        count_ref[i] = (ok_ref[k] - f) * up * phonon_scale
        for part in range(2):
            turned_ref[i, part * NB : (part + 1) * NB, :] = jnp.transpose(
                vector_ref[i, part].astype(f32)
            ).astype(jnp.bfloat16)
    lane = lax.broadcasted_iota(jnp.int32, pick_ref.shape, 0)
    col = lax.broadcasted_iota(jnp.int32, pick_ref.shape, 1)
    place = col % LANES
    wanted = (place // STRIP) * LANES + (col // LANES) * STRIP + place % STRIP
    pick_ref[...] = (lane == wanted).astype(f32).astype(jnp.bfloat16)


def tables(levels, filled, frequencies, bose, vectors, energy_k, occupation_k, width):
    q_local, k_local, bands = levels.shape
    points = q_local * k_local
    modes = frequencies.shape[1]
    vmem = pl.BlockSpec(memory_space=pltpu.VMEM)
    smem = pl.BlockSpec(memory_space=pltpu.SMEM)
    weight = jax.ShapeDtypeStruct((points, bands, modes), jnp.float32)
    return pl.pallas_call(
        table_kernel,
        in_specs=[vmem] * 5 + [smem] * 2,
        out_specs=[vmem] * 4,
        out_shape=[
            weight,
            weight,
            jax.ShapeDtypeStruct((points, 2 * bands, bands), jnp.bfloat16),
            jax.ShapeDtypeStruct((width, PARTS * LANES), jnp.bfloat16),
        ],
        compiler_params=pltpu.CompilerParams(vmem_limit_bytes=48 << 20),
    )(
        levels.reshape(points, bands),
        filled.reshape(points, bands),
        frequencies,
        bose,
        vectors.reshape(points, 2, bands, bands),
        energy_k,
        occupation_k,
    )


def width_kernel(
    block_ref, modes_ref, turned_ref, absorb_ref, count_ref, pick_ref,
    electron_ref, phonon_ref, spread, cycle, moded,
):
    f32 = jnp.float32
    bf16 = jnp.bfloat16
    q_local = modes_ref.shape[0]
    k_local = PARTS // 2
    rows = block_ref.shape[0]
    per_source = 75
    depth = 80
    sources = rows // q_local
    phases = 8
    runs = sources // phases
    block = block_ref[...]
    for part in range(PARTS):
        spread[part] = jnp.dot(
            block, pick_ref[:, part * LANES : (part + 1) * LANES], preferred_element_type=f32
        )
    electron_ref[...] = jnp.zeros(electron_ref.shape, f32)
    for q in range(q_local):
        for part in range(2):
            m = modes_ref[q, part].astype(f32)
            cycle[0:MODES, part * LANES : part * LANES + MODES] = m
            cycle[MODES : 2 * MODES, part * LANES : part * LANES + MODES] = m
        sums = [None] * 5
        for phase in range(phases):
            start = (per_source * phase) % MODES
            first = (per_source * phase) // MODES
            left = jnp.concatenate(
                [
                    spread[part, pl.ds(phase * q_local + q, runs, stride=phases * q_local), :]
                    for part in range(PARTS)
                ],
                axis=0,
            )[:, :depth].astype(bf16)
            right = cycle[pl.ds(start, depth), :]
            at = lax.broadcasted_iota(jnp.int32, right.shape, 0)
            until = min(MODES - start, per_source)
            pieces = [(first, jnp.where(at < until, right, 0.0))]
            if until < per_source:
                pieces.append(
                    (first + 1, jnp.where((at >= until) & (at < per_source), right, 0.0))
                )
            for n, piece in pieces:
                value = jnp.dot(left, piece.astype(bf16), preferred_element_type=f32)
                sums[n] = value if sums[n] is None else sums[n] + value
        half = PARTS // 2 * runs
        for n in range(5):
            real = sums[n][:half, :LANES] - sums[n][half:, LANES:]
            imag = sums[n][:half, LANES:] + sums[n][half:, :LANES]
            for k in range(k_local):
                moded[k, 0, pl.ds(n, runs, stride=5), :] = real[k * runs : (k + 1) * runs]
                moded[k, 1, pl.ds(n, runs, stride=5), :] = imag[k * runs : (k + 1) * runs]
        phonon = None
        for k in range(k_local):
            i = q * k_local + k
            right = jnp.concatenate([moded[k, 0], moded[k, 1]], axis=1).astype(bf16)
            both = jnp.dot(turned_ref[i], right, preferred_element_type=f32)
            real = both[:NB, :MODES] + both[NB:, LANES : LANES + MODES]
            imag = both[:NB, LANES : LANES + MODES] - both[NB:, :MODES]
            weight = real * real + imag * imag
            electron_ref[k : k + 1, :] += jnp.sum(weight * absorb_ref[i], axis=0, keepdims=True)
            value = jnp.sum(weight * count_ref[i], axis=0, keepdims=True)
            phonon = value if phonon is None else phonon + value
        phonon_ref[q : q + 1, :] = phonon


def widths(block, phonon_modes, turned, absorb, count, pick):
    q_local, _, modes, _ = phonon_modes.shape
    rows = block.shape[0]
    vmem = pl.BlockSpec(memory_space=pltpu.VMEM)
    return pl.pallas_call(
        width_kernel,
        in_specs=[vmem] * 6,
        out_specs=[vmem] * 2,
        out_shape=[
            jax.ShapeDtypeStruct((PARTS // 2, modes), jnp.float32),
            jax.ShapeDtypeStruct((q_local, modes), jnp.float32),
        ],
        scratch_shapes=[
            pltpu.VMEM((PARTS, rows, LANES), jnp.float32),
            pltpu.VMEM((2 * modes, 2 * LANES), jnp.float32),
            pltpu.VMEM((PARTS // 2, 2, NB, LANES), jnp.float32),
        ],
        compiler_params=pltpu.CompilerParams(vmem_limit_bytes=48 << 20),
    )(block, phonon_modes, turned, absorb, count, pick)


def sent_to_all(shard, axis):
    count = lax.axis_size(axis)
    return lax.all_to_all(
        jnp.broadcast_to(shard[None], (count, *shard.shape)), axis, 0, 0, tiled=True
    )


def added(left, right):
    return (left.astype(jnp.float32) + right.astype(jnp.float32)).astype(jnp.bfloat16)


def on_device(
    coupling,
    kpoints,
    qpoints,
    electron_cells,
    phonon_cells,
    phonon_modes,
    band_vectors,
    energies_kq,
    occupations_kq,
    energy_k,
    occupation_k,
    frequencies,
    bose_factors,
):
    q_local = frequencies.shape[0]
    send, keep = products(kpoints, qpoints, electron_cells, phonon_cells, coupling)
    q_total, width = send.shape[1:]
    members = lax.axis_size("ka")
    beside = [(i, i ^ 1) for i in range(members)]
    across = [(i, i ^ 2) for i in range(members)]
    chip = added(keep, lax.ppermute(send, "ka", beside))
    own = added(chip[1], lax.ppermute(chip[0], "ka", across))
    absorb, count, turned, pick = tables(
        energies_kq,
        occupations_kq,
        frequencies,
        bose_factors,
        band_vectors,
        energy_k,
        occupation_k,
        width,
    )
    chunks = own.reshape(q_total // q_local, q_local, width)
    arrived = lax.all_to_all(chunks, "pb", 0, 0, tiled=True)
    electron, phonon = widths(
        arrived.reshape(q_total, width), phonon_modes, turned, absorb, count, pick
    )
    electron_width = sent_to_all(electron, "pb").sum(axis=0)
    phonon_width = sent_to_all(phonon, "ka").sum(axis=0)
    return (electron_width, phonon_width)


def solution(mesh):
    in_specs = (
        P(None, "ka", "pb", None),
        P(),
        P(),
        P(),
        P(),
        P("pb", None, None, None),
        P("pb", "ka", None, None, None),
        P("pb", "ka", None),
        P("pb", "ka", None),
        P("ka"),
        P("ka"),
        P("pb", None),
        P("pb", None),
    )
    out_specs = (P("ka", None), P("pb", None))
    return jax.shard_map(
        on_device, mesh=mesh, in_specs=in_specs, out_specs=out_specs, check_vma=False
    )
```

time: 183 us -> 84.4 us (0.46)
  local copies, waits for them, and re-layouts: 50.7 us -> 4.38 us
  matrix products: 34 us -> 0 us
  waiting for transfers between devices: 60.1 us -> 37 us
  Pallas kernels: 0 us -> 13.9 us
  starting transfers between devices: 29.9 us -> 20.2 us
  blocking collectives: 0 us -> 5.17 us
  other arithmetic: 4.26 us -> 1.49 us
    dot_general x16 -> x0, matrix products: 34 us -> none  [the longest x4 22.2 us: contract_last(): lax.dot_general(left, right, (((1,), (1,)), ((), ())), preferred_element_...]
    all_to_all x2 -> x1, waiting for transfers between devices: 46.2 us -> 14.3 us  [on_device(): arrived = lax.all_to_all(chunks, 'pb', 0, 0, tiled=True)]
    another operation x5 -> x0, local copies, waits for them, and re-layouts: 19.8 us -> none  [the longest x1 7.3 us: on_device(): real_flat = coupling[0].reshape(cells_local * pairs_local, phonon_count)]
    slice x10 -> x0, local copies, waits for them, and re-layouts: 18.4 us -> none  [the longest x2 10.1 us: on_device(): real_flat = coupling[0].reshape(cells_local * pairs_local, phonon_count)]
    pallas_call x0 -> x3, Pallas kernels: none -> 13.9 us  [the longest x1 9.83 us: products(): pl.pallas_call(product_kernel, grid=(steps,), in_specs=[whole(kpoints), w...]
    ppermute x0 -> x2, waiting for transfers between devices: none -> 10.1 us  [the longest x1 8.01 us: on_device(): own = added(chip[1], lax.ppermute(chip[0], 'ka', across))]
    reshape x4 -> x2, local copies, waits for them, and re-layouts: 8.71 us -> 0.88 us  [the longest x1 0.8 us: on_device(): chunks = own.reshape(q_total // q_local, q_local, width)]
    all_to_all x2 -> x1, starting transfers between devices: 11.5 us -> 4.6 us  [sent_to_all(): lax.all_to_all(jnp.broadcast_to(shard[None], (count, *shard.shape)), axis...]
  transfers between devices with their start and end apart: 4 -> 4, of which waited for: 4 -> 4; matrix products, arithmetic and copies ran while one was open for 1% -> 1% of each run, Pallas kernels for 0% -> 2%
where the time goes in v1:
time: 84.4 us; the launch traced here: 83 us
  waiting for transfers between devices  37 us (44%)
  starting transfers between devices  20.2 us (24%)
  Pallas kernels  13.9 us (16%)
  blocking collectives  5.17 us (6%)
  local copies, waits for them, and re-layouts  4.38 us (5%)
  other arithmetic  1.49 us (2%)
  between operations  0.85 us (1%)
    all_to_all x1, waiting for transfers between devices, on_device(): arrived = lax.all_to_all(chunks, 'pb', 0, 0, tiled=True)  14.3 us
    all_to_all x1, starting transfers between devices, on_device(): arrived = lax.all_to_all(chunks, 'pb', 0, 0, tiled=True)  13.6 us
    all_to_all x1, waiting for transfers between devices, sent_to_all(): lax.all_to_all(jnp.broadcast_to(shard[None], (count, *shard.shape)), axis...  12.6 us
    pallas_call x1, Pallas kernels, products(): pl.pallas_call(product_kernel, grid=(steps,), in_specs=[whole(kpoints), w...  9.83 us
    ppermute x1, waiting for transfers between devices, on_device(): own = added(chip[1], lax.ppermute(chip[0], 'ka', across))  8.01 us
    all_to_all x1, blocking collectives, sent_to_all(): lax.all_to_all(jnp.broadcast_to(shard[None], (count, *shard.shape)), axis...  5.17 us
    all_to_all x1, starting transfers between devices, sent_to_all(): lax.all_to_all(jnp.broadcast_to(shard[None], (count, *shard.shape)), axis...  4.6 us
    unnamed x24, local copies, waits for them, and re-layouts  2.79 us
  transfers between devices with their start and end apart: 4, of which 4 were waited for; matrix products, arithmetic and copies ran while one was open for 1% of the time, Pallas kernels for 2%

profile of v1, /device:TPU:32, one launch (start us, length us, event | category | flops | bytes accessed | tf_op | source)
XLA Modules:
  0.0 83.0 jit_solution(230484154989594117)
XLA Ops:
  0.6 0.0 copy-start.4
  0.6 0.7 copy-done.4
  1.3 0.7 copy-done.5
  2.0 0.7 copy-done.6
  2.7 0.7 copy-done.7
  3.4 9.8 %shard_map.140 = (bf16[2,256,640]{2,1,0:T(8,128)(2,1)S(1)}, bf16[2,256,640]{2,1,0:T(8,128)(2,1)S(1)}) custom-call(s32[3,16]{1,0:T(4,128)S(1)} %copy-done.7, s32[3,256]{1,0:T(4,128)S(1)} %copy-done.6, s32[3,320]{1,0:T(4,128)S(1)} %copy-done.4, s32[3,320]{1,0:T(4,128)S(1)} %copy-done.5, bf16[2,75,80,320]{3,2,1,0:T(8,128)(2,1)} %bitcast.14), custom_call_target="tpu_custom_call" | custom-call | tf_op jit(solution)/shard_map/pallas_call | solution.py:107
  13.2 0.1 collective-permute-start
  13.3 2.1 %collective-permute-done = bf16[2,256,640]{2,1,0:T(8,128)(2,1)S(1)} collective-permute-done((bf16[2,256,640]{2,1,0:T(8,128)(2,1)S(1)}, bf16[2,256,640]{2,1,0:T(8,128)(2,1)S(1)}, u32[]{:S(2)}, u32[]{:S(2)}) %collective-permute-start) | collective-permute-done | bytes 655392 | tf_op jit(solution)/shard_map/ppermute | solution.py:311
  15.4 0.2 add_convert_fusion
  15.6 0.0 copy-start
  15.6 0.0 copy-start.2
  15.6 0.0 copy-start.3
  15.6 0.0 copy-start.8
  15.7 0.0 copy-start.9
  15.7 0.0 copy-start.10
  15.7 0.0 copy-start.11
  15.7 1.9 %collective-permute-start.1 = (bf16[256,640]{1,0:T(8,128)(2,1)S(1)}, bf16[256,640]{1,0:T(8,128)(2,1)S(1)}, u32[]{:S(2)}, u32[]{:S(2)}) collective-permute-start(bf16[256,640]{1,0:T(8,128)(2,1)S(1)} %slice_bitcast_fusion), channel_id=1, source_target_pairs={{0,2},{1,3},{2,0},{3,1},{4,6},{5,7},{6,4},{7,5},{8,10},{9,11},{10,... | collective-permute-start | bytes 983048 | tf_op jit(solution)/shard_map/ppermute | solution.py:312
  17.6 8.0 %collective-permute-done.1 = bf16[256,640]{1,0:T(8,128)(2,1)S(1)} collective-permute-done((bf16[256,640]{1,0:T(8,128)(2,1)S(1)}, bf16[256,640]{1,0:T(8,128)(2,1)S(1)}, u32[]{:S(2)}, u32[]{:S(2)}) %collective-permute-start.1) | collective-permute-done | bytes 327712 | tf_op jit(solution)/shard_map/ppermute | solution.py:312
  25.7 0.1 fusion
  25.7 0.0 copy-start.1
  25.8 0.8 reshape.23
  26.6 13.6 %all-to-all-start = ((bf16[64,4,640]{2,1,0:T(4,128)(2,1)}), bf16[64,4,640]{2,1,0:T(4,128)(2,1)S(1)}, u32[]{:S(2)}, u32[]{:S(2)}) async-start(bf16[64,4,640]{2,1,0:T(4,128)(2,1)} %reshape.23), calls=%async_computation | async-start | bytes 655360 | tf_op jit(solution)/shard_map/all_to_all | solution.py:324
  40.2 1.6 %shard_map.141 = (f32[16,40,120]{2,1,0:T(8,128)S(1)}, f32[16,40,120]{2,1,0:T(8,128)S(1)}, bf16[16,80,40]{2,1,0:T(8,128)(2,1)S(1)}, bf16[640,1024]{1,0:T(8,128)(2,1)S(1)}) custom-call(f32[16,40]{1,0:T(8,128)S(1)} %bitcast.12, f32[16,40]{1,0:T(8,128)S(1)} %bitcast.13, f32[4,120]{1,0:T(4,128)S(1)} %copy-done.8, f32[4,120]{1,0:T(4,128)S(1)} %copy-done.9, ...), custom_call_target="tpu_custom_call" | custom-call | tf_op jit(solution)/shard_map/pallas_call | solution.py:168
  41.8 14.3 %all-to-all-done = bf16[64,4,640]{2,1,0:T(4,128)(2,1)S(1)} async-done(((bf16[64,4,640]{2,1,0:T(4,128)(2,1)}), bf16[64,4,640]{2,1,0:T(4,128)(2,1)S(1)}, u32[]{:S(2)}, u32[]{:S(2)}) %all-to-all-start) | async-done | bytes 327712 | tf_op jit(solution)/shard_map/all_to_all | solution.py:324
  56.1 0.1 reshape.24.block_ref
  56.2 2.4 %shard_map.142 = (f32[4,120]{1,0:T(4,128)S(1)}, f32[4,120]{1,0:T(4,128)S(1)}) custom-call(bf16[256,640]{1,0:T(8,128)(2,1)S(1)} %reshape.24.block_ref, bf16[4,2,120,120]{3,2,1,0:T(8,128)(2,1)S(1)} %copy-done.1, bf16[16,80,40]{2,1,0:T(8,128)(2,1)S(1)} %get-tuple-element.12.turned_ref, f32[16,40,120]{2,1,0:T(8,128)S(1)} %get-tuple-element.13.absorb_ref, ...), custom_call_target="tpu_custom_call" | custom-call | tf_op jit(solution)/shard_map/pallas_call | solution.py:262
  58.7 5.2 %all_to_all.15 = f32[4,4,120]{2,1,0:T(4,128)S(1)} all-to-all(f32[4,4,120]{2,1,0:T(4,128)S(1)} %broadcast_in_dim.5), channel_id=1, replica_groups=mesh['pb'=64,'ka'=4] {'ka'}, dimensions={0} | all-to-all | bytes 15360 | tf_op jit(solution)/shard_map/all_to_all | solution.py:281
  63.8 0.7 broadcast_in_dim.4
  64.5 4.6 %all-to-all-start.1 = ((f32[64,4,120]{2,1,0:T(4,128)}), f32[64,4,120]{2,1,0:T(4,128)S(1)}, u32[]{:S(2)}, u32[]{:S(2)}) async-start(f32[64,4,120]{2,1,0:T(4,128)} %broadcast_in_dim.4), calls=%async_computation.1 | async-start | bytes 262144 | tf_op jit(solution)/shard_map/all_to_all | solution.py:281
  69.1 0.6 reduce_sum.19
  69.7 12.6 %all-to-all-done.1 = f32[64,4,120]{2,1,0:T(4,128)S(1)} async-done(((f32[64,4,120]{2,1,0:T(4,128)}), f32[64,4,120]{2,1,0:T(4,128)S(1)}, u32[]{:S(2)}, u32[]{:S(2)}) %all-to-all-start.1) | async-done | bytes 122912 | tf_op jit(solution)/shard_map/all_to_all | solution.py:281
  82.3 0.7 reduce_sum.18
  (13 shorter events, 0.1 us)
Async XLA Ops:
  0.6 0.7 copy-start.4
  1.3 0.7 copy-start.5
  2.0 0.7 copy-start.6
  2.7 0.7 copy-start.7
  13.2 2.2 %collective-permute-start = (bf16[2,256,640]{2,1,0:T(8,128)(2,1)S(1)}, bf16[2,256,640]{2,1,0:T(8,128)(2,1)S(1)}, u32[]{:S(2)}, u32[]{:S(2)}) collective-permute-start(bf16[2,256,640]{2,1,0:T(8,128)(2,1)S(1)} %get-tuple-element.11), channel_id=1, source_target_pairs={{0,1},{1,0},{2,3},{3,2},{4,5},{5,4},{6,7},{7,6},{8,9},{9,8},{10,11... | collective-permute-start | bytes 1966088 | tf_op jit(solution)/shard_map/ppermute | solution.py:311
  15.6 24.5 %copy-start = (bf16[4,4,2,40,40]{4,3,2,1,0:T(8,128)(2,1)S(1)}, bf16[4,4,2,40,40]{4,3,2,1,0:T(8,128)(2,1)}, u32[]{:S(2)}) copy-start(bf16[4,4,2,40,40]{4,3,2,1,0:T(8,128)(2,1)} %param.19) | copy-start | bytes 307204
  15.6 24.5 %copy-start.2 = (f32[4,4,40]{2,1,0:T(4,128)S(1)}, f32[4,4,40]{2,1,0:T(4,128)}, u32[]{:S(2)}) copy-start(f32[4,4,40]{2,1,0:T(4,128)} %param.20) | copy-start | bytes 7684
  15.6 24.5 %copy-start.3 = (f32[4,4,40]{2,1,0:T(4,128)S(1)}, f32[4,4,40]{2,1,0:T(4,128)}, u32[]{:S(2)}) copy-start(f32[4,4,40]{2,1,0:T(4,128)} %param.21) | copy-start | bytes 7684
  15.6 24.5 %copy-start.8 = (f32[4,120]{1,0:T(4,128)S(1)}, f32[4,120]{1,0:T(4,128)}, u32[]{:S(2)}) copy-start(f32[4,120]{1,0:T(4,128)} %omega_ref.1) | copy-start | bytes 5764
  15.7 24.5 %copy-start.9 = (f32[4,120]{1,0:T(4,128)S(1)}, f32[4,120]{1,0:T(4,128)}, u32[]{:S(2)}) copy-start(f32[4,120]{1,0:T(4,128)} %bose_ref.1) | copy-start | bytes 5764
  15.7 24.5 %copy-start.10 = (f32[4]{0:T(128)S(1)}, f32[4]{0:T(128)}, u32[]{:S(2)}) copy-start(f32[4]{0:T(128)} %ek_ref.1) | copy-start | bytes 52
  15.7 24.5 %copy-start.11 = (f32[4]{0:T(128)S(1)}, f32[4]{0:T(128)}, u32[]{:S(2)}) copy-start(f32[4]{0:T(128)} %ok_ref.1) | copy-start | bytes 52
  15.7 10.0 %collective-permute-start.1 = (bf16[256,640]{1,0:T(8,128)(2,1)S(1)}, bf16[256,640]{1,0:T(8,128)(2,1)S(1)}, u32[]{:S(2)}, u32[]{:S(2)}) collective-permute-start(bf16[256,640]{1,0:T(8,128)(2,1)S(1)} %slice_bitcast_fusion), channel_id=1, source_target_pairs={{0,2},{1,3},{2,0},{3,1},{4,6},{5,7},{6,4},{7,5},{8,10},{9,11},{10,... | collective-permute-start | bytes 983048 | tf_op jit(solution)/shard_map/ppermute | solution.py:312
  25.7 30.5 %copy-start.1 = (bf16[4,2,120,120]{3,2,1,0:T(8,128)(2,1)S(1)}, bf16[4,2,120,120]{3,2,1,0:T(8,128)(2,1)}, u32[]{:S(2)}) copy-start(bf16[4,2,120,120]{3,2,1,0:T(8,128)(2,1)} %modes_ref.1) | copy-start | bytes 691204
  26.6 29.6 %all-to-all-start = ((bf16[64,4,640]{2,1,0:T(4,128)(2,1)}), bf16[64,4,640]{2,1,0:T(4,128)(2,1)S(1)}, u32[]{:S(2)}, u32[]{:S(2)}) async-start(bf16[64,4,640]{2,1,0:T(4,128)(2,1)} %reshape.23), calls=%async_computation | async-start | bytes 655360 | tf_op jit(solution)/shard_map/all_to_all | solution.py:324
  64.5 17.8 %all-to-all-start.1 = ((f32[64,4,120]{2,1,0:T(4,128)}), f32[64,4,120]{2,1,0:T(4,128)S(1)}, u32[]{:S(2)}, u32[]{:S(2)}) async-start(f32[64,4,120]{2,1,0:T(4,128)} %broadcast_in_dim.4), calls=%async_computation.1 | async-start | bytes 262144 | tf_op jit(solution)/shard_map/all_to_all | solution.py:281

commit v2 on v1

--- a/solution.py
+++ b/solution.py
@@ -189,7 +189,7 @@
 
 def width_kernel(
     block_ref, modes_ref, turned_ref, absorb_ref, count_ref, pick_ref,
-    electron_ref, phonon_ref, spread, cycle, moded,
+    copies_ref, phonon_ref, spread, cycle, moded,
 ):
     f32 = jnp.float32
     bf16 = jnp.bfloat16
@@ -206,7 +206,7 @@
         spread[part] = jnp.dot(
             block, pick_ref[:, part * LANES : (part + 1) * LANES], preferred_element_type=f32
         )
-    electron_ref[...] = jnp.zeros(electron_ref.shape, f32)
+    electron = [None] * k_local
     for q in range(q_local):
         for part in range(2):
             m = modes_ref[q, part].astype(f32)
@@ -249,13 +249,15 @@
             real = both[:NB, :MODES] + both[NB:, LANES : LANES + MODES]
             imag = both[:NB, LANES : LANES + MODES] - both[NB:, :MODES]
             weight = real * real + imag * imag
-            electron_ref[k : k + 1, :] += jnp.sum(weight * absorb_ref[i], axis=0, keepdims=True)
+            value = jnp.sum(weight * absorb_ref[i], axis=0, keepdims=True)
+            electron[k] = value if electron[k] is None else electron[k] + value
             value = jnp.sum(weight * count_ref[i], axis=0, keepdims=True)
             phonon = value if phonon is None else phonon + value
         phonon_ref[q : q + 1, :] = phonon
-
-
-def widths(block, phonon_modes, turned, absorb, count, pick):
+    copies_ref[...] = jnp.broadcast_to(jnp.concatenate(electron, axis=0)[None], copies_ref.shape)
+
+
+def widths(block, phonon_modes, turned, absorb, count, pick, members):
     q_local, _, modes, _ = phonon_modes.shape
     rows = block.shape[0]
     vmem = pl.BlockSpec(memory_space=pltpu.VMEM)
@@ -264,7 +266,7 @@
         in_specs=[vmem] * 6,
         out_specs=[vmem] * 2,
         out_shape=[
-            jax.ShapeDtypeStruct((PARTS // 2, modes), jnp.float32),
+            jax.ShapeDtypeStruct((members, PARTS // 2, modes), jnp.float32),
             jax.ShapeDtypeStruct((q_local, modes), jnp.float32),
         ],
         scratch_shapes=[
@@ -276,11 +278,42 @@
     )(block, phonon_modes, turned, absorb, count, pick)
 
 
-def sent_to_all(shard, axis):
-    count = lax.axis_size(axis)
-    return lax.all_to_all(
-        jnp.broadcast_to(shard[None], (count, *shard.shape)), axis, 0, 0, tiled=True
-    )
+def final_kernel(electron_ref, own_ref, first_ref, second_ref, third_ref, electron_out, phonon_out):
+    electron_out[...] = jnp.sum(electron_ref[...], axis=0)
+    phonon_out[...] = (own_ref[...] + first_ref[...]) + (second_ref[...] + third_ref[...])
+
+
+def final_sums(electrons, phonons):
+    vmem = pl.BlockSpec(memory_space=pltpu.VMEM)
+    return pl.pallas_call(
+        final_kernel,
+        in_specs=[vmem] * 5,
+        out_specs=[vmem] * 2,
+        out_shape=[
+            jax.ShapeDtypeStruct(electrons.shape[1:], jnp.float32),
+            jax.ShapeDtypeStruct(phonons[0].shape, jnp.float32),
+        ],
+    )(electrons, *phonons)
+
+
+def chunk_kernel(mine_ref, other_ref, out_ref):
+    total = (mine_ref[...].astype(jnp.float32) + other_ref[...].astype(jnp.float32)).astype(
+        jnp.bfloat16
+    )
+    depth = out_ref.shape[1]
+    for i in range(out_ref.shape[0]):
+        out_ref[i] = total[i * depth : (i + 1) * depth]
+
+
+def added_chunks(mine, other, depth):
+    rows, width = mine.shape
+    vmem = pl.BlockSpec(memory_space=pltpu.VMEM)
+    return pl.pallas_call(
+        chunk_kernel,
+        in_specs=[vmem] * 2,
+        out_specs=vmem,
+        out_shape=jax.ShapeDtypeStruct((rows // depth, depth, width), jnp.bfloat16),
+    )(mine, other)
 
 
 def added(left, right):
@@ -309,8 +342,8 @@
     beside = [(i, i ^ 1) for i in range(members)]
     across = [(i, i ^ 2) for i in range(members)]
     chip = added(keep, lax.ppermute(send, "ka", beside))
-    own = added(chip[1], lax.ppermute(chip[0], "ka", across))
-    absorb, count, turned, pick = tables(
+    theirs = lax.ppermute(chip[0], "ka", across)
+    prepared = tables(
         energies_kq,
         occupations_kq,
         frequencies,
@@ -320,14 +353,25 @@
         occupation_k,
         width,
     )
-    chunks = own.reshape(q_total // q_local, q_local, width)
+    chunks = added_chunks(chip[1], theirs, q_local)
+    chunks, prepared, phonon_modes = lax.optimization_barrier((chunks, prepared, phonon_modes))
     arrived = lax.all_to_all(chunks, "pb", 0, 0, tiled=True)
-    electron, phonon = widths(
-        arrived.reshape(q_total, width), phonon_modes, turned, absorb, count, pick
-    )
-    electron_width = sent_to_all(electron, "pb").sum(axis=0)
-    phonon_width = sent_to_all(phonon, "ka").sum(axis=0)
-    return (electron_width, phonon_width)
+    absorb, count, turned, pick = prepared
+    copies, phonon = widths(
+        arrived.reshape(q_total, width),
+        phonon_modes,
+        turned,
+        absorb,
+        count,
+        pick,
+        q_total // q_local,
+    )
+    phonons = [phonon] + [
+        lax.ppermute(phonon, "ka", [(i, i ^ flip) for i in range(members)])
+        for flip in range(1, members)
+    ]
+    electrons = lax.all_to_all(copies, "pb", 0, 0, tiled=True)
+    return tuple(final_sums(electrons, phonons))
 
 
 def solution(mesh):

time: 84.4 us -> 81.6 us (0.967); the launches traced: 83 us -> 81.2 us
  blocking collectives: 5.17 us -> 29.6 us
  waiting for transfers between devices: 37 us -> 19.1 us
  starting transfers between devices: 20.2 us -> 8.5 us
  Pallas kernels: 13.9 us -> 18 us
  other arithmetic: 1.49 us -> 0.16 us
    all_to_all x1, blocking collectives: 5.17 us -> 29.6 us  [on_device(): arrived = lax.all_to_all(chunks, 'pb', 0, 0, tiled=True)]
    all_to_all x2 -> x1, waiting for transfers between devices: 26.9 us -> 8.83 us  [on_device(): electrons = lax.all_to_all(copies, 'pb', 0, 0, tiled=True)]
    all_to_all x2 -> x1, starting transfers between devices: 18.2 us -> 4.61 us  [on_device(): electrons = lax.all_to_all(copies, 'pb', 0, 0, tiled=True)]
    pallas_call x0 -> x2, Pallas kernels: none -> 3.47 us  [the longest x1 1.91 us: added_chunks(): pl.pallas_call(chunk_kernel, in_specs=[vmem] * 2, out_specs=vmem, out_sha...]
    ppermute x1 -> x4, starting transfers between devices: 1.94 us -> 3.8 us  [the longest x3 1.94 us: on_device(): lax.ppermute(phonon, 'ka', [(i, i ^ flip) for i in range(members)])]
    unnamed x24 -> x36, local copies, waits for them, and re-layouts: 2.79 us -> 4.18 us
    reduce_sum x2 -> x0, other arithmetic: 1.25 us -> none  [the longest x1 0.65 us: on_device(): electron_width = sent_to_all(electron, 'pb').sum(axis=0)]
    ppermute x1 -> x4, waiting for transfers between devices: 8.01 us -> 8.14 us  [the longest x1 6.31 us: on_device(): theirs = lax.ppermute(chip[0], 'ka', across)]
  transfers between devices with their start and end apart: 4 -> 6, of which waited for: 4 -> 5; matrix products, arithmetic and copies ran while one was open for 1% -> 0% of each run, Pallas kernels for 2% -> 2%
where the time goes in v2:
time: 81.6 us; the launch traced here: 81.2 us
  blocking collectives  29.6 us (36%)
  waiting for transfers between devices  19.1 us (23%)
  Pallas kernels  18 us (22%)
  starting transfers between devices  8.5 us (10%)
  local copies, waits for them, and re-layouts  5.05 us (6%)
    all_to_all x1, blocking collectives, on_device(): arrived = lax.all_to_all(chunks, 'pb', 0, 0, tiled=True)  29.6 us
    pallas_call x1, Pallas kernels, products(): pl.pallas_call(product_kernel, grid=(steps,), in_specs=[whole(kpoints), w...  9.83 us
    all_to_all x1, waiting for transfers between devices, on_device(): electrons = lax.all_to_all(copies, 'pb', 0, 0, tiled=True)  8.83 us
    ppermute x1, waiting for transfers between devices, on_device(): theirs = lax.ppermute(chip[0], 'ka', across)  6.31 us
    all_to_all x1, starting transfers between devices, on_device(): electrons = lax.all_to_all(copies, 'pb', 0, 0, tiled=True)  4.61 us
    unnamed x36, local copies, waits for them, and re-layouts  4.18 us
    pallas_call x1, Pallas kernels, widths(): pl.pallas_call(width_kernel, in_specs=[vmem] * 6, out_specs=[vmem] * 2, o...  3.11 us
    ppermute x1, waiting for transfers between devices, on_device(): chip = added(keep, lax.ppermute(send, 'ka', beside))  2.08 us
  transfers between devices with their start and end apart: 6, of which 5 were waited for; matrix products, arithmetic and copies ran while one was open for 0% of the time, Pallas kernels for 2%

profile of v2, /device:TPU:32, one launch (start us, length us, event | category | flops | bytes accessed | tf_op | source)
XLA Modules:
  0.0 81.2 jit_solution(2723327538438377623)
XLA Ops:
  0.6 0.7 copy-done.4
  1.3 0.7 copy-done.5
  2.0 0.7 copy-done.6
  2.7 0.7 copy-done.7
  3.4 9.8 %shard_map.140 = (bf16[2,256,640]{2,1,0:T(8,128)(2,1)S(1)}, bf16[2,256,640]{2,1,0:T(8,128)(2,1)S(1)}) custom-call(s32[3,16]{1,0:T(4,128)S(1)} %copy-done.7, s32[3,256]{1,0:T(4,128)S(1)} %copy-done.6, s32[3,320]{1,0:T(4,128)S(1)} %copy-done.4, s32[3,320]{1,0:T(4,128)S(1)} %copy-done.5, bf16[2,75,80,320]{3,2,1,0:T(8,128)(2,1)} %bitcast.11), custom_call_target="tpu_custom_call" | custom-call | tf_op jit(solution)/shard_map/pallas_call | solution.py:107
  13.2 0.1 collective-permute-start
  13.3 2.1 %collective-permute-done = bf16[2,256,640]{2,1,0:T(8,128)(2,1)S(1)} collective-permute-done((bf16[2,256,640]{2,1,0:T(8,128)(2,1)S(1)}, bf16[2,256,640]{2,1,0:T(8,128)(2,1)S(1)}, u32[]{:S(2)}, u32[]{:S(2)}) %collective-permute-start) | collective-permute-done | bytes 655392 | tf_op jit(solution)/shard_map/ppermute | solution.py:344
  15.4 0.0 copy-start.9
  15.4 0.0 copy-start.11
  15.4 0.0 copy-start.12
  15.5 0.2 add_convert_fusion
  15.6 0.8 slice_bitcast_fusion
  16.4 1.9 %collective-permute-start.1 = (bf16[256,640]{1,0:T(8,128)(2,1)S(1)}, bf16[256,640]{1,0:T(8,128)(2,1)S(1)}, u32[]{:S(2)}, u32[]{:S(2)}) collective-permute-start(bf16[256,640]{1,0:T(8,128)(2,1)S(1)} %get-tuple-element.30), channel_id=1, source_target_pairs={{0,2},{1,3},{2,0},{3,1},{4,6},{5,7},{6,4},{7,5},{8,10},{9,11},{10,... | collective-permute-start | bytes 983048 | tf_op jit(solution)/shard_map/ppermute | solution.py:345
  18.3 0.0 copy-done
  18.3 0.0 copy-start.1
  18.3 1.6 %shard_map.142 = (f32[16,40,120]{2,1,0:T(8,128)S(1)}, f32[16,40,120]{2,1,0:T(8,128)S(1)}, bf16[16,80,40]{2,1,0:T(8,128)(2,1)S(1)}, bf16[640,1024]{1,0:T(8,128)(2,1)S(1)}) custom-call(f32[16,40]{1,0:T(8,128)S(1)} %bitcast.9, f32[16,40]{1,0:T(8,128)S(1)} %bitcast.10, f32[4,120]{1,0:T(4,128)S(1)} %copy-done.8, f32[4,120]{1,0:T(4,128)S(1)} %copy-done.9, ...), custom_call_target="tpu_custom_call" | custom-call | tf_op jit(solution)/shard_map/pallas_call | solution.py:168
  20.0 6.3 %collective-permute-done.1.other_ref = bf16[256,640]{1,0:T(8,128)(2,1)S(1)} collective-permute-done((bf16[256,640]{1,0:T(8,128)(2,1)S(1)}, bf16[256,640]{1,0:T(8,128)(2,1)S(1)}, u32[]{:S(2)}, u32[]{:S(2)}) %collective-permute-start.1) | collective-permute-done | bytes 327712 | tf_op jit(solution)/shard_map/ppermute | solution.py:345
  26.3 0.7 copy-done.14
  27.0 1.9 %shard_map.141 = bf16[64,4,640]{2,1,0:T(4,128)(2,1)} custom-call(bf16[256,640]{1,0:T(8,128)(2,1)} %get-tuple-element.31.mine_ref, bf16[256,640]{1,0:T(8,128)(2,1)} %copy-done.14), custom_call_target="tpu_custom_call" | custom-call | tf_op jit(solution)/shard_map/pallas_call | solution.py:311
  28.9 29.6 %all_to_all.10 = bf16[64,4,640]{2,1,0:T(4,128)(2,1)S(1)} all-to-all(bf16[64,4,640]{2,1,0:T(4,128)(2,1)} %shard_map.141), channel_id=1, replica_groups=mesh['pb'=64,'ka'=4] {'pb'}, dimensions={0} | all-to-all | bytes 655360 | tf_op jit(solution)/shard_map/all_to_all | solution.py:358
  58.5 0.1 reshape.19.block_ref
  58.6 3.1 %shard_map.143 = (f32[64,4,120]{2,1,0:T(4,128)}, f32[4,120]{1,0:T(4,128)S(1)}) custom-call(bf16[256,640]{1,0:T(8,128)(2,1)S(1)} %reshape.19.block_ref, bf16[4,2,120,120]{3,2,1,0:T(8,128)(2,1)S(1)} %copy-done.1, bf16[16,80,40]{2,1,0:T(8,128)(2,1)S(1)} %get-tuple-element.24.turned_ref, f32[16,40,120]{2,1,0:T(8,128)S(1)} %get-tuple-element.25.absorb_ref, ...), custom_call_target="tpu_custom_call" | custom-call | tf_op jit(solution)/shard_map/pallas_call | solution.py:264
  61.7 4.6 %all-to-all-start.1 = ((f32[64,4,120]{2,1,0:T(4,128)}), f32[64,4,120]{2,1,0:T(4,128)S(1)}, u32[]{:S(2)}, u32[]{:S(2)}) async-start(f32[64,4,120]{2,1,0:T(4,128)} %get-tuple-element.28), calls=%async_computation.1 | async-start | bytes 262144 | tf_op jit(solution)/shard_map/all_to_all | solution.py:373
  66.3 0.1 collective-permute-start.4
  66.4 1.1 %collective-permute-start.3 = (f32[4,120]{1,0:T(4,128)S(1)}, f32[4,120]{1,0:T(4,128)S(1)}, u32[]{:S(2)}, u32[]{:S(2)}) collective-permute-start(f32[4,120]{1,0:T(4,128)S(1)} %get-tuple-element.29.own_ref), channel_id=1, source_target_pairs={{0,2},{1,3},{2,0},{3,1},{4,6},{5,7},{6,4},{7,5},{8,10},{9,11},{10,... | collective-permute-start | bytes 5768 | tf_op jit(solution)/shard_map/ppermute | solution.py:370
  67.5 0.8 collective-permute-start.2
  68.2 1.2 %collective-permute-done.4.third_ref = f32[4,120]{1,0:T(4,128)S(1)} collective-permute-done((f32[4,120]{1,0:T(4,128)S(1)}, f32[4,120]{1,0:T(4,128)S(1)}, u32[]{:S(2)}, u32[]{:S(2)}) %collective-permute-start.4) | collective-permute-done | bytes 1952 | tf_op jit(solution)/shard_map/ppermute | solution.py:370
  69.4 0.6 collective-permute-done.3.second_ref
  70.1 0.0 collective-permute-done.2.first_ref
  70.1 8.8 %all-to-all-done.1.electron_ref = f32[64,4,120]{2,1,0:T(4,128)S(1)} async-done(((f32[64,4,120]{2,1,0:T(4,128)}), f32[64,4,120]{2,1,0:T(4,128)S(1)}, u32[]{:S(2)}, u32[]{:S(2)}) %all-to-all-start.1) | async-done | bytes 122912 | tf_op jit(solution)/shard_map/all_to_all | solution.py:373
  78.9 0.7 copy-done.13
  79.6 1.6 %shard_map.144 = (f32[4,120]{1,0:T(4,128)}, f32[4,120]{1,0:T(4,128)}) custom-call(f32[64,4,120]{2,1,0:T(4,128)} %copy-done.13, f32[4,120]{1,0:T(4,128)} %copy-done.10, f32[4,120]{1,0:T(4,128)} %copy-done.17, f32[4,120]{1,0:T(4,128)} %copy-done.16, f32[4,120]{1,0:T(4,128)} %copy-done.15), custom_call_target="tpu_custom_call" | custom-call | tf_op jit(solution)/shard_map/pallas_call | solution.py:288
  (25 shorter events, 0.0 us)
Async XLA Ops:
  0.6 0.7 copy-start.4
  1.3 0.7 copy-start.5
  2.0 0.7 copy-start.6
  2.7 0.7 copy-start.7
  13.2 2.2 %collective-permute-start = (bf16[2,256,640]{2,1,0:T(8,128)(2,1)S(1)}, bf16[2,256,640]{2,1,0:T(8,128)(2,1)S(1)}, u32[]{:S(2)}, u32[]{:S(2)}) collective-permute-start(bf16[2,256,640]{2,1,0:T(8,128)(2,1)S(1)} %get-tuple-element.17), channel_id=1, source_target_pairs={{0,1},{1,0},{2,3},{3,2},{4,5},{5,4},{6,7},{7,6},{8,9},{9,8},{10,11... | collective-permute-start | bytes 1966088 | tf_op jit(solution)/shard_map/ppermute | solution.py:344
  15.4 2.9 %copy-start = (bf16[4,4,2,40,40]{4,3,2,1,0:T(8,128)(2,1)S(1)}, bf16[4,4,2,40,40]{4,3,2,1,0:T(8,128)(2,1)}, u32[]{:S(2)}) copy-start(bf16[4,4,2,40,40]{4,3,2,1,0:T(8,128)(2,1)} %param.19) | copy-start | bytes 307204
  15.4 2.9 %copy-start.2 = (f32[4,4,40]{2,1,0:T(4,128)S(1)}, f32[4,4,40]{2,1,0:T(4,128)}, u32[]{:S(2)}) copy-start(f32[4,4,40]{2,1,0:T(4,128)} %param.20) | copy-start | bytes 7684
  15.4 2.9 %copy-start.3 = (f32[4,4,40]{2,1,0:T(4,128)S(1)}, f32[4,4,40]{2,1,0:T(4,128)}, u32[]{:S(2)}) copy-start(f32[4,4,40]{2,1,0:T(4,128)} %param.21) | copy-start | bytes 7684
  15.4 2.9 %copy-start.8 = (f32[4,120]{1,0:T(4,128)S(1)}, f32[4,120]{1,0:T(4,128)}, u32[]{:S(2)}) copy-start(f32[4,120]{1,0:T(4,128)} %omega_ref.1) | copy-start | bytes 5764
  15.4 2.9 %copy-start.9 = (f32[4,120]{1,0:T(4,128)S(1)}, f32[4,120]{1,0:T(4,128)}, u32[]{:S(2)}) copy-start(f32[4,120]{1,0:T(4,128)} %bose_ref.1) | copy-start | bytes 5764
  15.4 2.9 %copy-start.11 = (f32[4]{0:T(128)S(1)}, f32[4]{0:T(128)}, u32[]{:S(2)}) copy-start(f32[4]{0:T(128)} %ek_ref.1) | copy-start | bytes 52
  15.4 2.9 %copy-start.12 = (f32[4]{0:T(128)S(1)}, f32[4]{0:T(128)}, u32[]{:S(2)}) copy-start(f32[4]{0:T(128)} %ok_ref.1) | copy-start | bytes 52
  16.4 9.9 %collective-permute-start.1 = (bf16[256,640]{1,0:T(8,128)(2,1)S(1)}, bf16[256,640]{1,0:T(8,128)(2,1)S(1)}, u32[]{:S(2)}, u32[]{:S(2)}) collective-permute-start(bf16[256,640]{1,0:T(8,128)(2,1)S(1)} %get-tuple-element.30), channel_id=1, source_target_pairs={{0,2},{1,3},{2,0},{3,1},{4,6},{5,7},{6,4},{7,5},{8,10},{9,11},{10,... | collective-permute-start | bytes 983048 | tf_op jit(solution)/shard_map/ppermute | solution.py:345
  18.3 40.2 %copy-start.1 = (bf16[4,2,120,120]{3,2,1,0:T(8,128)(2,1)S(1)}, bf16[4,2,120,120]{3,2,1,0:T(8,128)(2,1)}, u32[]{:S(2)}) copy-start(bf16[4,2,120,120]{3,2,1,0:T(8,128)(2,1)} %modes_ref) | copy-start | bytes 691204
  26.3 0.7 copy-start.14
  61.7 17.2 %copy-start.10 = (f32[4,120]{1,0:T(4,128)}, f32[4,120]{1,0:T(4,128)S(1)}, u32[]{:S(2)}) copy-start(f32[4,120]{1,0:T(4,128)S(1)} %get-tuple-element.29.own_ref) | copy-start | bytes 5764
  61.7 17.2 %all-to-all-start.1 = ((f32[64,4,120]{2,1,0:T(4,128)}), f32[64,4,120]{2,1,0:T(4,128)S(1)}, u32[]{:S(2)}, u32[]{:S(2)}) async-start(f32[64,4,120]{2,1,0:T(4,128)} %get-tuple-element.28), calls=%async_computation.1 | async-start | bytes 262144 | tf_op jit(solution)/shard_map/all_to_all | solution.py:373
  66.3 3.1 %collective-permute-start.4 = (f32[4,120]{1,0:T(4,128)S(1)}, f32[4,120]{1,0:T(4,128)S(1)}, u32[]{:S(2)}, u32[]{:S(2)}) collective-permute-start(f32[4,120]{1,0:T(4,128)S(1)} %get-tuple-element.29.own_ref), channel_id=1, source_target_pairs={{0,3},{1,2},{2,1},{3,0},{4,7},{5,6},{6,5},{7,4},{8,11},{9,10},{10,... | collective-permute-start | bytes 5768 | tf_op jit(solution)/shard_map/ppermute | solution.py:370
  66.4 3.7 %collective-permute-start.3 = (f32[4,120]{1,0:T(4,128)S(1)}, f32[4,120]{1,0:T(4,128)S(1)}, u32[]{:S(2)}, u32[]{:S(2)}) collective-permute-start(f32[4,120]{1,0:T(4,128)S(1)} %get-tuple-element.29.own_ref), channel_id=1, source_target_pairs={{0,2},{1,3},{2,0},{3,1},{4,6},{5,7},{6,4},{7,5},{8,10},{9,11},{10,... | collective-permute-start | bytes 5768 | tf_op jit(solution)/shard_map/ppermute | solution.py:370
  67.5 2.6 %collective-permute-start.2 = (f32[4,120]{1,0:T(4,128)S(1)}, f32[4,120]{1,0:T(4,128)S(1)}, u32[]{:S(2)}, u32[]{:S(2)}) collective-permute-start(f32[4,120]{1,0:T(4,128)S(1)} %get-tuple-element.29.own_ref), channel_id=1, source_target_pairs={{0,1},{1,0},{2,3},{3,2},{4,5},{5,4},{6,7},{7,6},{8,9},{9,8},{10,11... | collective-permute-start | bytes 5768 | tf_op jit(solution)/shard_map/ppermute | solution.py:370
  69.4 9.5 %copy-start.15 = (f32[4,120]{1,0:T(4,128)}, f32[4,120]{1,0:T(4,128)S(1)}, u32[]{:S(2)}) copy-start(f32[4,120]{1,0:T(4,128)S(1)} %collective-permute-done.4.third_ref) | copy-start | bytes 5764
  70.1 8.8 %copy-start.16 = (f32[4,120]{1,0:T(4,128)}, f32[4,120]{1,0:T(4,128)S(1)}, u32[]{:S(2)}) copy-start(f32[4,120]{1,0:T(4,128)S(1)} %collective-permute-done.3.second_ref) | copy-start | bytes 5764
  70.1 8.8 %copy-start.17 = (f32[4,120]{1,0:T(4,128)}, f32[4,120]{1,0:T(4,128)S(1)}, u32[]{:S(2)}) copy-start(f32[4,120]{1,0:T(4,128)S(1)} %collective-permute-done.2.first_ref) | copy-start | bytes 5764
  78.9 0.7 copy-start.13

commit v3 on v2

--- a/solution.py
+++ b/solution.py
@@ -32,67 +32,101 @@
 
 
 def product_kernel(
-    kpt_ref, qpt_ref, ecell_ref, pcell_ref, g_ref, send_ref, keep_ref, table, mixer, rows
+    kpt_hbm, qpt_hbm, ecell_hbm, pcell_hbm, g_hbm, send_ref, keep_ref,
+    kpt_ref, qpt_ref, ecell_ref, pcell_ref, g_ref, table, rows, small_sem, strip_sem,
 ):
-    step = pl.program_id(0)
     q_total = qpt_ref.shape[1]
     cells = g_ref.shape[2]
+    pairs = g_hbm.shape[1]
+    phonons = g_hbm.shape[3]
     groups = kpt_ref.shape[1] // 4
+    pitch = table.shape[1] // 2
+    f32 = jnp.float32
     bf16 = jnp.bfloat16
-
-    @pl.when(step == 0)
-    def _():
-        mine = lax.axis_index("ka")
-        kpt = kpt_ref[...].astype(jnp.float32).astype(bf16)
-        qpt = qpt_ref[...].astype(jnp.float32).astype(bf16)
-        ecell = ecell_ref[...].astype(jnp.float32).astype(bf16)
-        pcell = pcell_ref[...].astype(jnp.float32).astype(bf16)
-        source = lax.broadcasted_iota(jnp.int32, (kpt.shape[1], PARTS * groups), 0)
-        row = lax.broadcasted_iota(jnp.int32, (kpt.shape[1], PARTS * groups), 1)
-        wanted = jnp.bitwise_xor(row // PARTS, mine) * 4 + row % 4
-        k_rows = small_dot(kpt, (source == wanted).astype(jnp.float32).astype(bf16), ((1,), (0,)))
-        source = lax.broadcasted_iota(jnp.int32, (ecell.shape[1], 2 * cells), 0)
-        col = lax.broadcasted_iota(jnp.int32, (ecell.shape[1], 2 * cells), 1)
-        wanted = mine * cells + jnp.where(col >= cells, col - cells, col)
-        e_cols = small_dot(ecell, (source == wanted).astype(jnp.float32).astype(bf16), ((1,), (0,)))
-        ticks = small_dot(k_rows.astype(bf16), e_cols.astype(bf16), ((0,), (0,)))
-        row = lax.broadcasted_iota(jnp.int32, ticks.shape, 0)
-        col = lax.broadcasted_iota(jnp.int32, ticks.shape, 1)
-        imaginary = row % PARTS >= 4
-        second = col >= cells
-        turn = jnp.where(imaginary, jnp.where(second, 0.0, -25.0), jnp.where(second, 25.0, 0.0))
-        mixer[...] = whole_turn_cosine(ticks + turn).astype(bf16)
-        ticks = small_dot(qpt, pcell, ((0,), (0,)))
-        table[0:q_total, :] = whole_turn_cosine(ticks).astype(bf16)
-        table[q_total : 2 * q_total, :] = whole_turn_cosine(ticks - 25.0).astype(bf16)
-
-    mix = mixer[...]
-    for j in range(STRIP):
-        both = jnp.concatenate([g_ref[0, j], g_ref[1, j]], axis=0)
-        value = jnp.dot(mix, both, preferred_element_type=jnp.float32)
-        for t in range(rows.shape[0]):
-            tile = value[:, t * LANES : (t + 1) * LANES]
-            if tile.shape[1] < LANES:
-                blank = jnp.zeros((tile.shape[0], LANES - tile.shape[1]), jnp.float32)
-                tile = jnp.concatenate([tile, blank], axis=1)
-            rows[t, pl.ds(j, PARTS * groups, stride=STRIP), :] = tile
-
-    @pl.when(step == pl.num_programs(0) - 1)
-    def _():
-        empty = jnp.zeros((PARTS * groups, LANES), jnp.float32)
-        for j in range(75 % STRIP, STRIP):
-            for t in range(rows.shape[0]):
-                rows[t, pl.ds(j, PARTS * groups, stride=STRIP), :] = empty
-
-    every = jnp.concatenate([rows[t] for t in range(rows.shape[0])], axis=1)
-    every = every[:, : table.shape[1]].astype(bf16)
-    turned = small_dot(table[...], every, ((1,), (1,)))
-    lane = lax.broadcasted_iota(jnp.int32, (q_total, LANES), 1)
-    sign = jnp.where(lane < LANES // 2, -1.0, 1.0)
-    for ref, slot, group in ((send_ref, 0, 3), (send_ref, 1, 1), (keep_ref, 0, 2), (keep_ref, 1, 0)):
-        straight = turned[:q_total, group * LANES : (group + 1) * LANES]
-        crossed = turned[q_total:, group * LANES : (group + 1) * LANES]
-        ref[slot] = (straight + sign * pltpu.roll(crossed, LANES // 2, 1)).astype(bf16)
+    small = [
+        pltpu.make_async_copy(source, target, small_sem.at[i])
+        for i, (source, target) in enumerate(
+            ((kpt_hbm, kpt_ref), (ecell_hbm, ecell_ref), (qpt_hbm, qpt_ref), (pcell_hbm, pcell_ref))
+        )
+    ]
+    for copy in small:
+        copy.start()
+    strips = []
+    for first in range(0, pairs, STRIP):
+        part = pl.ds(first, min(STRIP, pairs - first))
+        strips.append(
+            pltpu.make_async_copy(g_hbm.at[:, part], g_ref.at[:, part], strip_sem.at[len(strips)])
+        )
+        strips[-1].start()
+    blank = jnp.zeros((table.shape[0], pitch - phonons), bf16)
+    for part in range(2):
+        table[:, part * pitch + phonons : (part + 1) * pitch] = blank
+        for slot in range(2):
+            for g in range(0, rows.shape[1], table.shape[0]):
+                rows[slot, g : g + table.shape[0], part * pitch + phonons : (part + 1) * pitch] = blank
+    for copy in small:
+        copy.wait()
+    mine = lax.axis_index("ka")
+    kpt = kpt_ref[...].astype(f32).astype(bf16)
+    qpt = qpt_ref[...].astype(f32).astype(bf16)
+    ecell = ecell_ref[...].astype(f32).astype(bf16)
+    pcell = pcell_ref[...].astype(f32).astype(bf16)
+    height = 2 * PARTS * groups
+    source = lax.broadcasted_iota(jnp.int32, (kpt.shape[1], height), 0)
+    row = lax.broadcasted_iota(jnp.int32, (kpt.shape[1], height), 1)
+    wanted = jnp.bitwise_xor((row // PARTS) % groups, mine) * 4 + row % 4
+    k_rows = small_dot(kpt, (source == wanted).astype(f32).astype(bf16), ((1,), (0,)))
+    source = lax.broadcasted_iota(jnp.int32, (ecell.shape[1], 2 * cells), 0)
+    col = lax.broadcasted_iota(jnp.int32, (ecell.shape[1], 2 * cells), 1)
+    wanted = mine * cells + jnp.where(col >= cells, col - cells, col)
+    e_cols = small_dot(ecell, (source == wanted).astype(f32).astype(bf16), ((1,), (0,)))
+    ticks = small_dot(k_rows.astype(bf16), e_cols.astype(bf16), ((0,), (0,)))
+    row = lax.broadcasted_iota(jnp.int32, ticks.shape, 0)
+    col = lax.broadcasted_iota(jnp.int32, ticks.shape, 1)
+    turn = jnp.where(row >= height // 2, 25.0, 0.0)
+    turn = turn - jnp.where(row % PARTS >= 4, 25.0, 0.0)
+    turn = turn + jnp.where(col >= cells, 25.0, 0.0)
+    mix = whole_turn_cosine(ticks + turn).astype(bf16)
+    ticks = small_dot(qpt, pcell, ((0,), (0,)))
+    table[:, 0:phonons] = whole_turn_cosine(ticks).astype(bf16)
+    table[:, pitch : pitch + phonons] = whole_turn_cosine(ticks - 25.0).astype(bf16)
+
+    def mixed_rows(s):
+        values = []
+        for j in range(STRIP):
+            pair = s * STRIP + j
+            if pair < pairs:
+                both = jnp.concatenate([g_ref[0, pair], g_ref[1, pair]], axis=0)
+                values.append(jnp.dot(mix, both, preferred_element_type=f32))
+            else:
+                values.append(jnp.zeros((height, phonons), f32))
+            if j % 2 == 0:
+                continue
+            for set_ in range(2):
+                for g in range(groups):
+                    at = (set_ * groups + g) * PARTS
+                    two = jnp.concatenate(
+                        [values[j - 1][at : at + PARTS], values[j][at : at + PARTS]], axis=0
+                    )
+                    to = g * LANES + (j - 1) * PARTS
+                    rows[s % 2, to : to + 2 * PARTS, set_ * pitch : set_ * pitch + phonons] = (
+                        two.astype(bf16)
+                    )
+
+    def turned_rows(s):
+        turned = small_dot(table[...], rows[s % 2], ((1,), (1,)))
+        to = pl.ds(s * LANES, LANES)
+        for ref, slot, g in (
+            (send_ref, 0, 3), (send_ref, 1, 1), (keep_ref, 0, 2), (keep_ref, 1, 0),
+        ):
+            ref[slot, :, to] = turned[:, g * LANES : (g + 1) * LANES].astype(bf16)
+
+    for s, strip in enumerate(strips):
+        strip.wait()
+        mixed_rows(s)
+        if s > 0:
+            turned_rows(s - 1)
+    turned_rows(len(strips) - 1)
 
 
 def products(kpoints, qpoints, electron_cells, phonon_cells, coupling):
@@ -100,29 +134,28 @@
     k_total = kpoints.shape[1]
     q_total = qpoints.shape[1]
     steps = pl.cdiv(pairs, STRIP)
+    pitch = pl.cdiv(phonons, LANES) * LANES
     by_pair = jnp.transpose(coupling, (0, 2, 1, 3))
-    whole = lambda a: pl.BlockSpec(a.shape, lambda i: (0, 0))
     out = jax.ShapeDtypeStruct((2, q_total, steps * LANES), jnp.bfloat16)
-    out_spec = pl.BlockSpec((2, q_total, LANES), lambda i: (0, 0, i))
+    points = [
+        pltpu.with_memory_space_constraint(a, pltpu.HBM)
+        for a in (kpoints, qpoints, electron_cells, phonon_cells)
+    ]
     return pl.pallas_call(
         product_kernel,
-        grid=(steps,),
-        in_specs=[
-            whole(kpoints),
-            whole(qpoints),
-            whole(electron_cells),
-            whole(phonon_cells),
-            pl.BlockSpec((parts, STRIP, cells, phonons), lambda i: (0, i, 0, 0)),
-        ],
-        out_specs=[out_spec, out_spec],
+        in_specs=[pl.BlockSpec(memory_space=pltpu.HBM)] * 5,
+        out_specs=[pl.BlockSpec(memory_space=pltpu.VMEM)] * 2,
         out_shape=[out, out],
-        scratch_shapes=[
-            pltpu.VMEM((2 * q_total, phonons), jnp.bfloat16),
-            pltpu.VMEM((2 * k_total, 2 * cells), jnp.bfloat16),
-            pltpu.VMEM((pl.cdiv(phonons, LANES), 2 * k_total * STRIP, LANES), jnp.float32),
+        scratch_shapes=[pltpu.VMEM(a.shape, a.dtype) for a in points]
+        + [
+            pltpu.VMEM(by_pair.shape, by_pair.dtype),
+            pltpu.VMEM((q_total, 2 * pitch), jnp.bfloat16),
+            pltpu.VMEM((2, 2 * k_total * STRIP, 2 * pitch), jnp.bfloat16),
+            pltpu.SemaphoreType.DMA((4,)),
+            pltpu.SemaphoreType.DMA((steps,)),
         ],
         compiler_params=pltpu.CompilerParams(vmem_limit_bytes=48 << 20),
-    )(kpoints, qpoints, electron_cells, phonon_cells, by_pair)
+    )(*points, by_pair)
 
 
 def table_kernel(
@@ -154,7 +187,7 @@
     lane = lax.broadcasted_iota(jnp.int32, pick_ref.shape, 0)
     col = lax.broadcasted_iota(jnp.int32, pick_ref.shape, 1)
     place = col % LANES
-    wanted = (place // STRIP) * LANES + (col // LANES) * STRIP + place % STRIP
+    wanted = (place // STRIP) * LANES + (place % STRIP) * PARTS + col // LANES
     pick_ref[...] = (lane == wanted).astype(f32).astype(jnp.bfloat16)
 
 
@@ -278,44 +311,6 @@
     )(block, phonon_modes, turned, absorb, count, pick)
 
 
-def final_kernel(electron_ref, own_ref, first_ref, second_ref, third_ref, electron_out, phonon_out):
-    electron_out[...] = jnp.sum(electron_ref[...], axis=0)
-    phonon_out[...] = (own_ref[...] + first_ref[...]) + (second_ref[...] + third_ref[...])
-
-
-def final_sums(electrons, phonons):
-    vmem = pl.BlockSpec(memory_space=pltpu.VMEM)
-    return pl.pallas_call(
-        final_kernel,
-        in_specs=[vmem] * 5,
-        out_specs=[vmem] * 2,
-        out_shape=[
-            jax.ShapeDtypeStruct(electrons.shape[1:], jnp.float32),
-            jax.ShapeDtypeStruct(phonons[0].shape, jnp.float32),
-        ],
-    )(electrons, *phonons)
-
-
-def chunk_kernel(mine_ref, other_ref, out_ref):
-    total = (mine_ref[...].astype(jnp.float32) + other_ref[...].astype(jnp.float32)).astype(
-        jnp.bfloat16
-    )
-    depth = out_ref.shape[1]
-    for i in range(out_ref.shape[0]):
-        out_ref[i] = total[i * depth : (i + 1) * depth]
-
-
-def added_chunks(mine, other, depth):
-    rows, width = mine.shape
-    vmem = pl.BlockSpec(memory_space=pltpu.VMEM)
-    return pl.pallas_call(
-        chunk_kernel,
-        in_specs=[vmem] * 2,
-        out_specs=vmem,
-        out_shape=jax.ShapeDtypeStruct((rows // depth, depth, width), jnp.bfloat16),
-    )(mine, other)
-
-
 def added(left, right):
     return (left.astype(jnp.float32) + right.astype(jnp.float32)).astype(jnp.bfloat16)
 
@@ -353,7 +348,7 @@
         occupation_k,
         width,
     )
-    chunks = added_chunks(chip[1], theirs, q_local)
+    chunks = added(chip[1], theirs).reshape(q_total // q_local, q_local, width)
     chunks, prepared, phonon_modes = lax.optimization_barrier((chunks, prepared, phonon_modes))
     arrived = lax.all_to_all(chunks, "pb", 0, 0, tiled=True)
     absorb, count, turned, pick = prepared
@@ -371,7 +366,7 @@
         for flip in range(1, members)
     ]
     electrons = lax.all_to_all(copies, "pb", 0, 0, tiled=True)
-    return tuple(final_sums(electrons, phonons))
+    return (electrons.sum(axis=0), (phonons[0] + phonons[1]) + (phonons[2] + phonons[3]))
 
 
 def solution(mesh):

time: 81.6 us -> 71.8 us (0.88)
  Pallas kernels: 18 us -> 12.5 us
  local copies, waits for them, and re-layouts: 5.05 us -> 0.23 us
  other arithmetic: 0.16 us -> 1.48 us
    pallas_call x3 -> x1, Pallas kernels: 13.3 us -> 7.79 us  [products(): pl.pallas_call(product_kernel, in_specs=[pl.BlockSpec(memory_space=pltpu....]
    unnamed x36 -> x16, local copies, waits for them, and re-layouts: 4.18 us -> 0.04 us
  transfers between devices with their start and end apart: 6 -> 6, of which waited for: 5 -> 5; matrix products, arithmetic and copies ran while one was open for 0% -> 1% of each run, Pallas kernels for 2% -> 2%
where the time goes in v3:
time: 71.8 us; the launch traced here: 71.6 us
  blocking collectives  29.4 us (41%)
  waiting for transfers between devices  18.5 us (26%)
  Pallas kernels  12.5 us (17%)
  starting transfers between devices  8.68 us (12%)
  other arithmetic  1.48 us (2%)
  between operations  0.78 us (1%)
    all_to_all x1, blocking collectives, on_device(): arrived = lax.all_to_all(chunks, 'pb', 0, 0, tiled=True)  29.4 us
    all_to_all x1, waiting for transfers between devices, on_device(): electrons = lax.all_to_all(copies, 'pb', 0, 0, tiled=True)  8.25 us
    pallas_call x1, Pallas kernels, products(): pl.pallas_call(product_kernel, in_specs=[pl.BlockSpec(memory_space=pltpu....  7.79 us
    ppermute x1, waiting for transfers between devices, on_device(): theirs = lax.ppermute(chip[0], 'ka', across)  6.29 us
    all_to_all x1, starting transfers between devices, on_device(): electrons = lax.all_to_all(copies, 'pb', 0, 0, tiled=True)  4.6 us
    pallas_call x1, Pallas kernels, widths(): pl.pallas_call(width_kernel, in_specs=[vmem] * 6, out_specs=[vmem] * 2, o...  3.1 us
    ppermute x1, waiting for transfers between devices, on_device(): chip = added(keep, lax.ppermute(send, 'ka', beside))  2.08 us
    ppermute x1, starting transfers between devices, on_device(): theirs = lax.ppermute(chip[0], 'ka', across)  2.05 us
  transfers between devices with their start and end apart: 6, of which 5 were waited for; matrix products, arithmetic and copies ran while one was open for 1% of the time, Pallas kernels for 2%

profile of v3, /device:TPU:32, one launch (start us, length us, event | category | flops | bytes accessed | tf_op | source)
XLA Modules:
  0.0 71.6 jit_solution(16995571619474745341)
XLA Ops:
  0.6 7.8 %shard_map.140 = (bf16[2,256,640]{2,1,0:T(8,128)(2,1)S(1)}, bf16[2,256,640]{2,1,0:T(8,128)(2,1)S(1)}) custom-call(s32[3,16]{1,0:T(4,128)} %kpt_hbm.1, s32[3,256]{1,0:T(4,128)} %qpt_hbm.1, s32[3,320]{1,0:T(4,128)} %ecell_hbm.1, s32[3,320]{1,0:T(4,128)} %pcell_hbm.1, bf16[2,75,80,320]{3,2,1,0:T(8,128)(2,1)} %bitcast.14), custom_call_target="tpu_custom_call" | custom-call | tf_op jit(solution)/shard_map/pallas_call | solution.py:144
  8.4 0.1 collective-permute-start
  8.5 2.1 %collective-permute-done = bf16[2,256,640]{2,1,0:T(8,128)(2,1)S(1)} collective-permute-done((bf16[2,256,640]{2,1,0:T(8,128)(2,1)S(1)}, bf16[2,256,640]{2,1,0:T(8,128)(2,1)S(1)}, u32[]{:S(2)}, u32[]{:S(2)}) %collective-permute-start) | collective-permute-done | bytes 655392 | tf_op jit(solution)/shard_map/ppermute | solution.py:339
  10.6 0.0 copy-start.5
  10.6 0.0 copy-start.6
  10.7 0.0 copy-start.7
  10.7 0.2 add_convert_fusion
  10.9 2.1 %collective-permute-start.1 = (bf16[256,640]{1,0:T(8,128)(2,1)S(1)}, bf16[256,640]{1,0:T(8,128)(2,1)S(1)}, u32[]{:S(2)}, u32[]{:S(2)}) collective-permute-start(bf16[256,640]{1,0:T(8,128)(2,1)S(1)} %slice_bitcast_fusion), channel_id=1, source_target_pairs={{0,2},{1,3},{2,0},{3,1},{4,6},{5,7},{6,4},{7,5},{8,10},{9,11},{10,... | collective-permute-start | bytes 983048 | tf_op jit(solution)/shard_map/ppermute | solution.py:340
  12.9 0.0 copy-done
  12.9 0.0 copy-done.2
  12.9 0.0 copy-done.3
  12.9 0.0 copy-done.4
  12.9 0.0 copy-done.5
  12.9 0.0 copy-done.6
  13.0 1.6 %shard_map.141 = (f32[16,40,120]{2,1,0:T(8,128)S(1)}, f32[16,40,120]{2,1,0:T(8,128)S(1)}, bf16[16,80,40]{2,1,0:T(8,128)(2,1)S(1)}, bf16[640,1024]{1,0:T(8,128)(2,1)S(1)}) custom-call(f32[16,40]{1,0:T(8,128)S(1)} %bitcast.12, f32[16,40]{1,0:T(8,128)S(1)} %bitcast.13, f32[4,120]{1,0:T(4,128)S(1)} %copy-done.4, f32[4,120]{1,0:T(4,128)S(1)} %copy-done.5, ...), custom_call_target="tpu_custom_call" | custom-call | tf_op jit(solution)/shard_map/pallas_call | solution.py:201
  14.6 0.0 copy-start.1
  14.6 6.3 %collective-permute-done.1 = bf16[256,640]{1,0:T(8,128)(2,1)S(1)} collective-permute-done((bf16[256,640]{1,0:T(8,128)(2,1)S(1)}, bf16[256,640]{1,0:T(8,128)(2,1)S(1)}, u32[]{:S(2)}, u32[]{:S(2)}) %collective-permute-start.1) | collective-permute-done | bytes 327712 | tf_op jit(solution)/shard_map/ppermute | solution.py:340
  20.9 0.1 fusion
  21.0 0.1 reshape.21
  21.1 29.4 %all_to_all.10 = bf16[64,4,640]{2,1,0:T(4,128)(2,1)S(1)} all-to-all(bf16[64,4,640]{2,1,0:T(4,128)(2,1)S(1)} %reshape.21), channel_id=1, replica_groups=mesh['pb'=64,'ka'=4] {'pb'}, dimensions={0} | all-to-all | bytes 655360 | tf_op jit(solution)/shard_map/all_to_all | solution.py:353
  50.5 0.1 reshape.25.block_ref
  50.6 3.1 %shard_map.142 = (f32[64,4,120]{2,1,0:T(4,128)}, f32[4,120]{1,0:T(4,128)S(1)}) custom-call(bf16[256,640]{1,0:T(8,128)(2,1)S(1)} %reshape.25.block_ref, bf16[4,2,120,120]{3,2,1,0:T(8,128)(2,1)S(1)} %copy-done.1, bf16[16,80,40]{2,1,0:T(8,128)(2,1)S(1)} %get-tuple-element.24.turned_ref, f32[16,40,120]{2,1,0:T(8,128)S(1)} %get-tuple-element.25.absorb_ref, ...), custom_call_target="tpu_custom_call" | custom-call | tf_op jit(solution)/shard_map/pallas_call | solution.py:297
  53.7 4.6 %all-to-all-start.1 = ((f32[64,4,120]{2,1,0:T(4,128)}), f32[64,4,120]{2,1,0:T(4,128)S(1)}, u32[]{:S(2)}, u32[]{:S(2)}) async-start(f32[64,4,120]{2,1,0:T(4,128)} %get-tuple-element.28), calls=%async_computation.1 | async-start | bytes 262144 | tf_op jit(solution)/shard_map/all_to_all | solution.py:368
  58.3 0.1 collective-permute-start.4
  58.4 1.0 %collective-permute-start.3 = (f32[4,120]{1,0:T(4,128)S(1)}, f32[4,120]{1,0:T(4,128)S(1)}, u32[]{:S(2)}, u32[]{:S(2)}) collective-permute-start(f32[4,120]{1,0:T(4,128)S(1)} %get-tuple-element.29), channel_id=1, source_target_pairs={{0,2},{1,3},{2,0},{3,1},{4,6},{5,7},{6,4},{7,5},{8,10},{9,11},{10,... | collective-permute-start | bytes 5768 | tf_op jit(solution)/shard_map/ppermute | solution.py:365
  59.4 0.9 %collective-permute-start.2 = (f32[4,120]{1,0:T(4,128)S(1)}, f32[4,120]{1,0:T(4,128)S(1)}, u32[]{:S(2)}, u32[]{:S(2)}) collective-permute-start(f32[4,120]{1,0:T(4,128)S(1)} %get-tuple-element.29), channel_id=1, source_target_pairs={{0,1},{1,0},{2,3},{3,2},{4,5},{5,4},{6,7},{7,6},{8,9},{9,8},{10,11... | collective-permute-start | bytes 5768 | tf_op jit(solution)/shard_map/ppermute | solution.py:365
  60.3 1.2 %collective-permute-done.4 = f32[4,120]{1,0:T(4,128)S(1)} collective-permute-done((f32[4,120]{1,0:T(4,128)S(1)}, f32[4,120]{1,0:T(4,128)S(1)}, u32[]{:S(2)}, u32[]{:S(2)}) %collective-permute-start.4) | collective-permute-done | bytes 1952 | tf_op jit(solution)/shard_map/ppermute | solution.py:365
  61.4 0.7 collective-permute-done.3
  62.1 0.0 collective-permute-done.2
  62.1 0.6 add_add_fusion
  62.7 8.3 %all-to-all-done.1 = f32[64,4,120]{2,1,0:T(4,128)S(1)} async-done(((f32[64,4,120]{2,1,0:T(4,128)}), f32[64,4,120]{2,1,0:T(4,128)S(1)}, u32[]{:S(2)}, u32[]{:S(2)}) %all-to-all-start.1) | async-done | bytes 122912 | tf_op jit(solution)/shard_map/all_to_all | solution.py:368
  70.9 0.7 reduce_sum.9
  (7 shorter events, 0.0 us)
Async XLA Ops:
  8.4 2.2 %collective-permute-start = (bf16[2,256,640]{2,1,0:T(8,128)(2,1)S(1)}, bf16[2,256,640]{2,1,0:T(8,128)(2,1)S(1)}, u32[]{:S(2)}, u32[]{:S(2)}) collective-permute-start(bf16[2,256,640]{2,1,0:T(8,128)(2,1)S(1)} %get-tuple-element.17), channel_id=1, source_target_pairs={{0,1},{1,0},{2,3},{3,2},{4,5},{5,4},{6,7},{7,6},{8,9},{9,8},{10,11... | collective-permute-start | bytes 1966088 | tf_op jit(solution)/shard_map/ppermute | solution.py:339
  10.6 2.3 %copy-start = (bf16[4,4,2,40,40]{4,3,2,1,0:T(8,128)(2,1)S(1)}, bf16[4,4,2,40,40]{4,3,2,1,0:T(8,128)(2,1)}, u32[]{:S(2)}) copy-start(bf16[4,4,2,40,40]{4,3,2,1,0:T(8,128)(2,1)} %param.19) | copy-start | bytes 307204
  10.6 2.3 %copy-start.2 = (f32[4,4,40]{2,1,0:T(4,128)S(1)}, f32[4,4,40]{2,1,0:T(4,128)}, u32[]{:S(2)}) copy-start(f32[4,4,40]{2,1,0:T(4,128)} %param.20) | copy-start | bytes 7684
  10.6 2.3 %copy-start.3 = (f32[4,4,40]{2,1,0:T(4,128)S(1)}, f32[4,4,40]{2,1,0:T(4,128)}, u32[]{:S(2)}) copy-start(f32[4,4,40]{2,1,0:T(4,128)} %param.21) | copy-start | bytes 7684
  10.6 2.3 %copy-start.4 = (f32[4,120]{1,0:T(4,128)S(1)}, f32[4,120]{1,0:T(4,128)}, u32[]{:S(2)}) copy-start(f32[4,120]{1,0:T(4,128)} %omega_ref.1) | copy-start | bytes 5764
  10.6 2.3 %copy-start.5 = (f32[4,120]{1,0:T(4,128)S(1)}, f32[4,120]{1,0:T(4,128)}, u32[]{:S(2)}) copy-start(f32[4,120]{1,0:T(4,128)} %bose_ref.1) | copy-start | bytes 5764
  10.6 2.3 %copy-start.6 = (f32[4]{0:T(128)S(1)}, f32[4]{0:T(128)}, u32[]{:S(2)}) copy-start(f32[4]{0:T(128)} %ek_ref.1) | copy-start | bytes 52
  10.7 2.3 %copy-start.7 = (f32[4]{0:T(128)S(1)}, f32[4]{0:T(128)}, u32[]{:S(2)}) copy-start(f32[4]{0:T(128)} %ok_ref.1) | copy-start | bytes 52
  10.9 10.1 %collective-permute-start.1 = (bf16[256,640]{1,0:T(8,128)(2,1)S(1)}, bf16[256,640]{1,0:T(8,128)(2,1)S(1)}, u32[]{:S(2)}, u32[]{:S(2)}) collective-permute-start(bf16[256,640]{1,0:T(8,128)(2,1)S(1)} %slice_bitcast_fusion), channel_id=1, source_target_pairs={{0,2},{1,3},{2,0},{3,1},{4,6},{5,7},{6,4},{7,5},{8,10},{9,11},{10,... | collective-permute-start | bytes 983048 | tf_op jit(solution)/shard_map/ppermute | solution.py:340
  14.6 36.0 %copy-start.1 = (bf16[4,2,120,120]{3,2,1,0:T(8,128)(2,1)S(1)}, bf16[4,2,120,120]{3,2,1,0:T(8,128)(2,1)}, u32[]{:S(2)}) copy-start(bf16[4,2,120,120]{3,2,1,0:T(8,128)(2,1)} %modes_ref) | copy-start | bytes 691204
  53.7 17.2 %all-to-all-start.1 = ((f32[64,4,120]{2,1,0:T(4,128)}), f32[64,4,120]{2,1,0:T(4,128)S(1)}, u32[]{:S(2)}, u32[]{:S(2)}) async-start(f32[64,4,120]{2,1,0:T(4,128)} %get-tuple-element.28), calls=%async_computation.1 | async-start | bytes 262144 | tf_op jit(solution)/shard_map/all_to_all | solution.py:368
  58.3 3.1 %collective-permute-start.4 = (f32[4,120]{1,0:T(4,128)S(1)}, f32[4,120]{1,0:T(4,128)S(1)}, u32[]{:S(2)}, u32[]{:S(2)}) collective-permute-start(f32[4,120]{1,0:T(4,128)S(1)} %get-tuple-element.29), channel_id=1, source_target_pairs={{0,3},{1,2},{2,1},{3,0},{4,7},{5,6},{6,5},{7,4},{8,11},{9,10},{10,... | collective-permute-start | bytes 5768 | tf_op jit(solution)/shard_map/ppermute | solution.py:365
  58.4 3.7 %collective-permute-start.3 = (f32[4,120]{1,0:T(4,128)S(1)}, f32[4,120]{1,0:T(4,128)S(1)}, u32[]{:S(2)}, u32[]{:S(2)}) collective-permute-start(f32[4,120]{1,0:T(4,128)S(1)} %get-tuple-element.29), channel_id=1, source_target_pairs={{0,2},{1,3},{2,0},{3,1},{4,6},{5,7},{6,4},{7,5},{8,10},{9,11},{10,... | collective-permute-start | bytes 5768 | tf_op jit(solution)/shard_map/ppermute | solution.py:365
  59.4 2.7 %collective-permute-start.2 = (f32[4,120]{1,0:T(4,128)S(1)}, f32[4,120]{1,0:T(4,128)S(1)}, u32[]{:S(2)}, u32[]{:S(2)}) collective-permute-start(f32[4,120]{1,0:T(4,128)S(1)} %get-tuple-element.29), channel_id=1, source_target_pairs={{0,1},{1,0},{2,3},{3,2},{4,5},{5,4},{6,7},{7,6},{8,9},{9,8},{10,11... | collective-permute-start | bytes 5768 | tf_op jit(solution)/shard_map/ppermute | solution.py:365

commit v4 on v3

--- a/solution.py
+++ b/solution.py
@@ -1,3 +1,4 @@
+import functools
 import math
 
 import jax
@@ -33,13 +34,13 @@
 
 def product_kernel(
     kpt_hbm, qpt_hbm, ecell_hbm, pcell_hbm, g_hbm, send_ref, keep_ref,
-    kpt_ref, qpt_ref, ecell_ref, pcell_ref, g_ref, table, rows, small_sem, strip_sem,
+    kpt_ref, qpt_ref, ecell_ref, pcell_ref, g_ref, table, rows, small_sem, strip_sem, *, flips,
 ):
     q_total = qpt_ref.shape[1]
     cells = g_ref.shape[2]
     pairs = g_hbm.shape[1]
     phonons = g_hbm.shape[3]
-    groups = kpt_ref.shape[1] // 4
+    groups = len(flips)
     pitch = table.shape[1] // 2
     f32 = jnp.float32
     bf16 = jnp.bfloat16
@@ -74,7 +75,8 @@
     height = 2 * PARTS * groups
     source = lax.broadcasted_iota(jnp.int32, (kpt.shape[1], height), 0)
     row = lax.broadcasted_iota(jnp.int32, (kpt.shape[1], height), 1)
-    wanted = jnp.bitwise_xor((row // PARTS) % groups, mine) * 4 + row % 4
+    flip = jnp.where((row // PARTS) % groups == 0, flips[0], flips[1])
+    wanted = jnp.bitwise_xor(flip, mine) * 4 + row % 4
     k_rows = small_dot(kpt, (source == wanted).astype(f32).astype(bf16), ((1,), (0,)))
     source = lax.broadcasted_iota(jnp.int32, (ecell.shape[1], 2 * cells), 0)
     col = lax.broadcasted_iota(jnp.int32, (ecell.shape[1], 2 * cells), 1)
@@ -116,10 +118,8 @@
     def turned_rows(s):
         turned = small_dot(table[...], rows[s % 2], ((1,), (1,)))
         to = pl.ds(s * LANES, LANES)
-        for ref, slot, g in (
-            (send_ref, 0, 3), (send_ref, 1, 1), (keep_ref, 0, 2), (keep_ref, 1, 0),
-        ):
-            ref[slot, :, to] = turned[:, g * LANES : (g + 1) * LANES].astype(bf16)
+        send_ref[:, to] = turned[:, :LANES].astype(bf16)
+        keep_ref[:, to] = turned[:, LANES:].astype(bf16)
 
     for s, strip in enumerate(strips):
         strip.wait()
@@ -129,20 +129,19 @@
     turned_rows(len(strips) - 1)
 
 
-def products(kpoints, qpoints, electron_cells, phonon_cells, coupling):
+def products(kpoints, qpoints, electron_cells, phonon_cells, coupling, flips):
     parts, cells, pairs, phonons = coupling.shape
-    k_total = kpoints.shape[1]
     q_total = qpoints.shape[1]
     steps = pl.cdiv(pairs, STRIP)
     pitch = pl.cdiv(phonons, LANES) * LANES
     by_pair = jnp.transpose(coupling, (0, 2, 1, 3))
-    out = jax.ShapeDtypeStruct((2, q_total, steps * LANES), jnp.bfloat16)
+    out = jax.ShapeDtypeStruct((q_total, steps * LANES), jnp.bfloat16)
     points = [
         pltpu.with_memory_space_constraint(a, pltpu.HBM)
         for a in (kpoints, qpoints, electron_cells, phonon_cells)
     ]
     return pl.pallas_call(
-        product_kernel,
+        functools.partial(product_kernel, flips=flips),
         in_specs=[pl.BlockSpec(memory_space=pltpu.HBM)] * 5,
         out_specs=[pl.BlockSpec(memory_space=pltpu.VMEM)] * 2,
         out_shape=[out, out],
@@ -150,7 +149,7 @@
         + [
             pltpu.VMEM(by_pair.shape, by_pair.dtype),
             pltpu.VMEM((q_total, 2 * pitch), jnp.bfloat16),
-            pltpu.VMEM((2, 2 * k_total * STRIP, 2 * pitch), jnp.bfloat16),
+            pltpu.VMEM((2, len(flips) * LANES, 2 * pitch), jnp.bfloat16),
             pltpu.SemaphoreType.DMA((4,)),
             pltpu.SemaphoreType.DMA((steps,)),
         ],
@@ -311,8 +310,8 @@
     )(block, phonon_modes, turned, absorb, count, pick)
 
 
-def added(left, right):
-    return (left.astype(jnp.float32) + right.astype(jnp.float32)).astype(jnp.bfloat16)
+def added(*arrays):
+    return sum(a.astype(jnp.float32) for a in arrays).astype(jnp.bfloat16)
 
 
 def on_device(
@@ -331,13 +330,16 @@
     bose_factors,
 ):
     q_local = frequencies.shape[0]
-    send, keep = products(kpoints, qpoints, electron_cells, phonon_cells, coupling)
-    q_total, width = send.shape[1:]
     members = lax.axis_size("ka")
     beside = [(i, i ^ 1) for i in range(members)]
     across = [(i, i ^ 2) for i in range(members)]
+    send, keep = products(kpoints, qpoints, electron_cells, phonon_cells, coupling, (3, 2))
+    q_total, width = send.shape
     chip = added(keep, lax.ppermute(send, "ka", beside))
-    theirs = lax.ppermute(chip[0], "ka", across)
+    chip, kpoints, energy_k = lax.optimization_barrier((chip, kpoints, energy_k))
+    theirs = lax.ppermute(chip, "ka", across)
+    send, keep = products(kpoints, qpoints, electron_cells, phonon_cells, coupling, (1, 0))
+    near = lax.ppermute(send, "ka", beside)
     prepared = tables(
         energies_kq,
         occupations_kq,
@@ -348,7 +350,7 @@
         occupation_k,
         width,
     )
-    chunks = added(chip[1], theirs).reshape(q_total // q_local, q_local, width)
+    chunks = added(keep, near, theirs).reshape(q_total // q_local, q_local, width)
     chunks, prepared, phonon_modes = lax.optimization_barrier((chunks, prepared, phonon_modes))
     arrived = lax.all_to_all(chunks, "pb", 0, 0, tiled=True)
     absorb, count, turned, pick = prepared

time: 71.8 us -> 72.6 us (1.011)
  Pallas kernels: 12.5 us -> 19.3 us
  waiting for transfers between devices: 18.5 us -> 12 us
    pallas_call x1 -> x2, Pallas kernels: 7.79 us -> 14.6 us  [products(): pl.pallas_call(functools.partial(product_kernel, flips=flips), in_specs=[...]
    ppermute x1 -> x2, waiting for transfers between devices: 6.29 us -> 0.01 us  [the longest x1 0.01 us: on_device(): theirs = lax.ppermute(chip, 'ka', across)]
    ppermute x1 -> x2, starting transfers between devices: 2.05 us -> 2.06 us  [the longest x1 1.97 us: on_device(): theirs = lax.ppermute(chip, 'ka', across)]
  transfers between devices with their start and end apart: 6 -> 7, of which waited for: 5 -> 4; matrix products, arithmetic and copies ran while one was open for 1% -> 1% of each run, Pallas kernels for 2% -> 12%
where the time goes in v4:
time: 72.6 us; the launch traced here: 72.2 us
  blocking collectives  29.6 us (41%)
  Pallas kernels  19.3 us (27%)
  waiting for transfers between devices  12 us (17%)
  starting transfers between devices  8.71 us (12%)
  other arithmetic  1.44 us (2%)
  between operations  0.86 us (1%)
    all_to_all x1, blocking collectives, on_device(): arrived = lax.all_to_all(chunks, 'pb', 0, 0, tiled=True)  29.6 us
    pallas_call x2, Pallas kernels, products(): pl.pallas_call(functools.partial(product_kernel, flips=flips), in_specs=[...  14.6 us
    all_to_all x1, waiting for transfers between devices, on_device(): electrons = lax.all_to_all(copies, 'pb', 0, 0, tiled=True)  8.01 us
    all_to_all x1, starting transfers between devices, on_device(): electrons = lax.all_to_all(copies, 'pb', 0, 0, tiled=True)  4.62 us
    pallas_call x1, Pallas kernels, widths(): pl.pallas_call(width_kernel, in_specs=[vmem] * 6, out_specs=[vmem] * 2, o...  3.09 us
    ppermute x3, waiting for transfers between devices, on_device(): lax.ppermute(phonon, 'ka', [(i, i ^ flip) for i in range(members)])  2.38 us
    ppermute x1, starting transfers between devices, on_device(): theirs = lax.ppermute(chip, 'ka', across)  1.97 us
    ppermute x3, starting transfers between devices, on_device(): lax.ppermute(phonon, 'ka', [(i, i ^ flip) for i in range(members)])  1.94 us
  transfers between devices with their start and end apart: 7, of which 4 were waited for; matrix products, arithmetic and copies ran while one was open for 1% of the time, Pallas kernels for 12%

profile of v4, /device:TPU:32, one launch (start us, length us, event | category | flops | bytes accessed | tf_op | source)
XLA Modules:
  0.0 72.2 jit_solution(15632460277841671725)
XLA Ops:
  0.6 0.0 copy-start
  0.6 0.0 copy-start.2
  0.7 0.0 copy-start.3
  0.7 0.0 copy-start.4
  0.7 0.0 copy-start.5
  0.7 0.0 copy-start.6
  0.7 7.3 %shard_map.140 = (bf16[256,640]{1,0:T(8,128)(2,1)S(1)}, bf16[256,640]{1,0:T(8,128)(2,1)S(1)}) custom-call(s32[3,16]{1,0:T(4,128)} %kpt_hbm.2, s32[3,256]{1,0:T(4,128)} %qpt_hbm.3, s32[3,320]{1,0:T(4,128)} %ecell_hbm.3, s32[3,320]{1,0:T(4,128)} %pcell_hbm.3, bf16[2,75,80,320]{3,2,1,0:T(8,128)(2,1)} %bitcast.7), custom_call_target="tpu_custom_call" | custom-call | tf_op jit(solution)/shard_map/pallas_call | solution.py:143
  8.1 0.0 copy-start.1
  8.1 0.1 collective-permute-start
  8.2 1.6 %collective-permute-done = bf16[256,640]{1,0:T(8,128)(2,1)S(1)} collective-permute-done((bf16[256,640]{1,0:T(8,128)(2,1)S(1)}, bf16[256,640]{1,0:T(8,128)(2,1)S(1)}, u32[]{:S(2)}, u32[]{:S(2)}) %collective-permute-start) | collective-permute-done | bytes 327712 | tf_op jit(solution)/shard_map/ppermute | solution.py:338
  9.8 0.1 add_convert_fusion.1
  9.9 2.0 %collective-permute-start.2 = (bf16[256,640]{1,0:T(8,128)(2,1)S(1)}, bf16[256,640]{1,0:T(8,128)(2,1)S(1)}, u32[]{:S(2)}, u32[]{:S(2)}) collective-permute-start(bf16[256,640]{1,0:T(8,128)(2,1)S(1)} %add_convert_fusion.1), channel_id=1, source_target_pairs={{0,2},{1,3},{2,0},{3,1},{4,6},{5,7},{6,4},{7,5},{8,10},{9,11},{10,... | collective-permute-start | bytes 983048 | tf_op jit(solution)/shard_map/ppermute | solution.py:340
  11.8 7.3 %shard_map.141 = (bf16[256,640]{1,0:T(8,128)(2,1)S(1)}, bf16[256,640]{1,0:T(8,128)(2,1)S(1)}) custom-call(s32[3,16]{1,0:T(4,128)} %kpt_hbm.2, s32[3,256]{1,0:T(4,128)} %qpt_hbm.3, s32[3,320]{1,0:T(4,128)} %ecell_hbm.3, s32[3,320]{1,0:T(4,128)} %pcell_hbm.3, bf16[2,75,80,320]{3,2,1,0:T(8,128)(2,1)} %bitcast.8), custom_call_target="tpu_custom_call" | custom-call | tf_op jit(solution)/shard_map/pallas_call | solution.py:143
  19.1 0.1 collective-permute-start.1
  19.3 1.6 %shard_map.142 = (f32[16,40,120]{2,1,0:T(8,128)S(1)}, f32[16,40,120]{2,1,0:T(8,128)S(1)}, bf16[16,80,40]{2,1,0:T(8,128)(2,1)S(1)}, bf16[640,1024]{1,0:T(8,128)(2,1)S(1)}) custom-call(f32[16,40]{1,0:T(8,128)S(1)} %bitcast.5, f32[16,40]{1,0:T(8,128)S(1)} %bitcast.6, f32[4,120]{1,0:T(4,128)S(1)} %copy-done.4, f32[4,120]{1,0:T(4,128)S(1)} %copy-done.5, ...), custom_call_target="tpu_custom_call" | custom-call | tf_op jit(solution)/shard_map/pallas_call | solution.py:200
  20.9 0.0 collective-permute-done.2
  20.9 0.0 collective-permute-done.1
  20.9 0.1 add_convert_fusion
  21.1 0.1 reshape.19
  21.2 29.6 %all_to_all.10 = bf16[64,4,640]{2,1,0:T(4,128)(2,1)S(1)} all-to-all(bf16[64,4,640]{2,1,0:T(4,128)(2,1)S(1)} %reshape.19), channel_id=1, replica_groups=mesh['pb'=64,'ka'=4] {'pb'}, dimensions={0} | all-to-all | bytes 655360 | tf_op jit(solution)/shard_map/all_to_all | solution.py:355
  50.8 0.1 reshape.23.block_ref
  50.9 3.1 %shard_map.143 = (f32[64,4,120]{2,1,0:T(4,128)}, f32[4,120]{1,0:T(4,128)S(1)}) custom-call(bf16[256,640]{1,0:T(8,128)(2,1)S(1)} %reshape.23.block_ref, bf16[4,2,120,120]{3,2,1,0:T(8,128)(2,1)S(1)} %copy-done.1, bf16[16,80,40]{2,1,0:T(8,128)(2,1)S(1)} %get-tuple-element.34.turned_ref, f32[16,40,120]{2,1,0:T(8,128)S(1)} %get-tuple-element.35.absorb_ref, ...), custom_call_target="tpu_custom_call" | custom-call | tf_op jit(solution)/shard_map/pallas_call | solution.py:296
  54.0 4.6 %all-to-all-start.1 = ((f32[64,4,120]{2,1,0:T(4,128)}), f32[64,4,120]{2,1,0:T(4,128)S(1)}, u32[]{:S(2)}, u32[]{:S(2)}) async-start(f32[64,4,120]{2,1,0:T(4,128)} %get-tuple-element.38), calls=%async_computation.1 | async-start | bytes 262144 | tf_op jit(solution)/shard_map/all_to_all | solution.py:370
  58.6 0.1 collective-permute-start.5
  58.7 1.7 %collective-permute-start.4 = (f32[4,120]{1,0:T(4,128)S(1)}, f32[4,120]{1,0:T(4,128)S(1)}, u32[]{:S(2)}, u32[]{:S(2)}) collective-permute-start(f32[4,120]{1,0:T(4,128)S(1)} %get-tuple-element.39), channel_id=1, source_target_pairs={{0,2},{1,3},{2,0},{3,1},{4,6},{5,7},{6,4},{7,5},{8,10},{9,11},{10,... | collective-permute-start | bytes 5768 | tf_op jit(solution)/shard_map/ppermute | solution.py:367
  60.4 0.2 collective-permute-start.3
  60.6 1.5 %collective-permute-done.5 = f32[4,120]{1,0:T(4,128)S(1)} collective-permute-done((f32[4,120]{1,0:T(4,128)S(1)}, f32[4,120]{1,0:T(4,128)S(1)}, u32[]{:S(2)}, u32[]{:S(2)}) %collective-permute-start.5) | collective-permute-done | bytes 1952 | tf_op jit(solution)/shard_map/ppermute | solution.py:367
  62.0 0.9 %collective-permute-done.4 = f32[4,120]{1,0:T(4,128)S(1)} collective-permute-done((f32[4,120]{1,0:T(4,128)S(1)}, f32[4,120]{1,0:T(4,128)S(1)}, u32[]{:S(2)}, u32[]{:S(2)}) %collective-permute-start.4) | collective-permute-done | bytes 1952 | tf_op jit(solution)/shard_map/ppermute | solution.py:367
  62.9 0.0 collective-permute-done.3
  63.0 0.6 add_add_fusion
  63.5 8.0 %all-to-all-done.1 = f32[64,4,120]{2,1,0:T(4,128)S(1)} async-done(((f32[64,4,120]{2,1,0:T(4,128)}), f32[64,4,120]{2,1,0:T(4,128)S(1)}, u32[]{:S(2)}, u32[]{:S(2)}) %all-to-all-start.1) | async-done | bytes 122912 | tf_op jit(solution)/shard_map/all_to_all | solution.py:370
  71.5 0.7 reduce_sum.9
  (9 shorter events, 0.0 us)
Async XLA Ops:
  0.6 18.6 %copy-start = (bf16[4,4,2,40,40]{4,3,2,1,0:T(8,128)(2,1)S(1)}, bf16[4,4,2,40,40]{4,3,2,1,0:T(8,128)(2,1)}, u32[]{:S(2)}) copy-start(bf16[4,4,2,40,40]{4,3,2,1,0:T(8,128)(2,1)} %param.19) | copy-start | bytes 307204
  0.6 18.6 %copy-start.2 = (f32[4,4,40]{2,1,0:T(4,128)S(1)}, f32[4,4,40]{2,1,0:T(4,128)}, u32[]{:S(2)}) copy-start(f32[4,4,40]{2,1,0:T(4,128)} %param.20) | copy-start | bytes 7684
  0.7 18.6 %copy-start.3 = (f32[4,4,40]{2,1,0:T(4,128)S(1)}, f32[4,4,40]{2,1,0:T(4,128)}, u32[]{:S(2)}) copy-start(f32[4,4,40]{2,1,0:T(4,128)} %param.21) | copy-start | bytes 7684
  0.7 18.6 %copy-start.4 = (f32[4,120]{1,0:T(4,128)S(1)}, f32[4,120]{1,0:T(4,128)}, u32[]{:S(2)}) copy-start(f32[4,120]{1,0:T(4,128)} %omega_ref.1) | copy-start | bytes 5764
  0.7 18.6 %copy-start.5 = (f32[4,120]{1,0:T(4,128)S(1)}, f32[4,120]{1,0:T(4,128)}, u32[]{:S(2)}) copy-start(f32[4,120]{1,0:T(4,128)} %bose_ref.1) | copy-start | bytes 5764
  0.7 18.6 %copy-start.6 = (f32[4]{0:T(128)S(1)}, f32[4]{0:T(128)}, u32[]{:S(2)}) copy-start(f32[4]{0:T(128)} %ek_ref) | copy-start | bytes 52
  0.7 18.6 %copy-start.7 = (f32[4]{0:T(128)S(1)}, f32[4]{0:T(128)}, u32[]{:S(2)}) copy-start(f32[4]{0:T(128)} %ok_ref.1) | copy-start | bytes 52
  8.1 42.8 %copy-start.1 = (bf16[4,2,120,120]{3,2,1,0:T(8,128)(2,1)S(1)}, bf16[4,2,120,120]{3,2,1,0:T(8,128)(2,1)}, u32[]{:S(2)}) copy-start(bf16[4,2,120,120]{3,2,1,0:T(8,128)(2,1)} %modes_ref) | copy-start | bytes 691204
  8.1 1.7 %collective-permute-start = (bf16[256,640]{1,0:T(8,128)(2,1)S(1)}, bf16[256,640]{1,0:T(8,128)(2,1)S(1)}, u32[]{:S(2)}, u32[]{:S(2)}) collective-permute-start(bf16[256,640]{1,0:T(8,128)(2,1)S(1)} %get-tuple-element.22), channel_id=1, source_target_pairs={{0,1},{1,0},{2,3},{3,2},{4,5},{5,4},{6,7},{7,6},{8,9},{9,8},{10,11... | collective-permute-start | bytes 983048 | tf_op jit(solution)/shard_map/ppermute | solution.py:338
  9.9 11.1 %collective-permute-start.2 = (bf16[256,640]{1,0:T(8,128)(2,1)S(1)}, bf16[256,640]{1,0:T(8,128)(2,1)S(1)}, u32[]{:S(2)}, u32[]{:S(2)}) collective-permute-start(bf16[256,640]{1,0:T(8,128)(2,1)S(1)} %add_convert_fusion.1), channel_id=1, source_target_pairs={{0,2},{1,3},{2,0},{3,1},{4,6},{5,7},{6,4},{7,5},{8,10},{9,11},{10,... | collective-permute-start | bytes 983048 | tf_op jit(solution)/shard_map/ppermute | solution.py:340
  19.1 1.8 %collective-permute-start.1 = (bf16[256,640]{1,0:T(8,128)(2,1)S(1)}, bf16[256,640]{1,0:T(8,128)(2,1)S(1)}, u32[]{:S(2)}, u32[]{:S(2)}) collective-permute-start(bf16[256,640]{1,0:T(8,128)(2,1)S(1)} %get-tuple-element.25), channel_id=1, source_target_pairs={{0,1},{1,0},{2,3},{3,2},{4,5},{5,4},{6,7},{7,6},{8,9},{9,8},{10,11... | collective-permute-start | bytes 983048 | tf_op jit(solution)/shard_map/ppermute | solution.py:342
  54.0 17.5 %all-to-all-start.1 = ((f32[64,4,120]{2,1,0:T(4,128)}), f32[64,4,120]{2,1,0:T(4,128)S(1)}, u32[]{:S(2)}, u32[]{:S(2)}) async-start(f32[64,4,120]{2,1,0:T(4,128)} %get-tuple-element.38), calls=%async_computation.1 | async-start | bytes 262144 | tf_op jit(solution)/shard_map/all_to_all | solution.py:370
  58.6 3.4 %collective-permute-start.5 = (f32[4,120]{1,0:T(4,128)S(1)}, f32[4,120]{1,0:T(4,128)S(1)}, u32[]{:S(2)}, u32[]{:S(2)}) collective-permute-start(f32[4,120]{1,0:T(4,128)S(1)} %get-tuple-element.39), channel_id=1, source_target_pairs={{0,3},{1,2},{2,1},{3,0},{4,7},{5,6},{6,5},{7,4},{8,11},{9,10},{10,... | collective-permute-start | bytes 5768 | tf_op jit(solution)/shard_map/ppermute | solution.py:367
  58.7 4.2 %collective-permute-start.4 = (f32[4,120]{1,0:T(4,128)S(1)}, f32[4,120]{1,0:T(4,128)S(1)}, u32[]{:S(2)}, u32[]{:S(2)}) collective-permute-start(f32[4,120]{1,0:T(4,128)S(1)} %get-tuple-element.39), channel_id=1, source_target_pairs={{0,2},{1,3},{2,0},{3,1},{4,6},{5,7},{6,4},{7,5},{8,10},{9,11},{10,... | collective-permute-start | bytes 5768 | tf_op jit(solution)/shard_map/ppermute | solution.py:367
  60.4 2.5 %collective-permute-start.3 = (f32[4,120]{1,0:T(4,128)S(1)}, f32[4,120]{1,0:T(4,128)S(1)}, u32[]{:S(2)}, u32[]{:S(2)}) collective-permute-start(f32[4,120]{1,0:T(4,128)S(1)} %get-tuple-element.39), channel_id=1, source_target_pairs={{0,1},{1,0},{2,3},{3,2},{4,5},{5,4},{6,7},{7,6},{8,9},{9,8},{10,11... | collective-permute-start | bytes 5768 | tf_op jit(solution)/shard_map/ppermute | solution.py:367

commit v5 on v3

--- a/solution.py
+++ b/solution.py
@@ -32,7 +32,7 @@
 
 
 def product_kernel(
-    kpt_hbm, qpt_hbm, ecell_hbm, pcell_hbm, g_hbm, send_ref, keep_ref,
+    kpt_hbm, qpt_hbm, ecell_hbm, pcell_hbm, g_hbm, near_keep, near_send, far_keep, far_send,
     kpt_ref, qpt_ref, ecell_ref, pcell_ref, g_ref, table, rows, small_sem, strip_sem,
 ):
     q_total = qpt_ref.shape[1]
@@ -51,6 +51,8 @@
     ]
     for copy in small:
         copy.start()
+    for copy in small:
+        copy.wait()
     strips = []
     for first in range(0, pairs, STRIP):
         part = pl.ds(first, min(STRIP, pairs - first))
@@ -64,8 +66,6 @@
         for slot in range(2):
             for g in range(0, rows.shape[1], table.shape[0]):
                 rows[slot, g : g + table.shape[0], part * pitch + phonons : (part + 1) * pitch] = blank
-    for copy in small:
-        copy.wait()
     mine = lax.axis_index("ka")
     kpt = kpt_ref[...].astype(f32).astype(bf16)
     qpt = qpt_ref[...].astype(f32).astype(bf16)
@@ -116,10 +116,8 @@
     def turned_rows(s):
         turned = small_dot(table[...], rows[s % 2], ((1,), (1,)))
         to = pl.ds(s * LANES, LANES)
-        for ref, slot, g in (
-            (send_ref, 0, 3), (send_ref, 1, 1), (keep_ref, 0, 2), (keep_ref, 1, 0),
-        ):
-            ref[slot, :, to] = turned[:, g * LANES : (g + 1) * LANES].astype(bf16)
+        for g, ref in enumerate((near_keep, near_send, far_keep, far_send)):
+            ref[:, to] = turned[:, g * LANES : (g + 1) * LANES].astype(bf16)
 
     for s, strip in enumerate(strips):
         strip.wait()
@@ -136,7 +134,7 @@
     steps = pl.cdiv(pairs, STRIP)
     pitch = pl.cdiv(phonons, LANES) * LANES
     by_pair = jnp.transpose(coupling, (0, 2, 1, 3))
-    out = jax.ShapeDtypeStruct((2, q_total, steps * LANES), jnp.bfloat16)
+    out = jax.ShapeDtypeStruct((q_total, steps * LANES), jnp.bfloat16)
     points = [
         pltpu.with_memory_space_constraint(a, pltpu.HBM)
         for a in (kpoints, qpoints, electron_cells, phonon_cells)
@@ -144,8 +142,8 @@
     return pl.pallas_call(
         product_kernel,
         in_specs=[pl.BlockSpec(memory_space=pltpu.HBM)] * 5,
-        out_specs=[pl.BlockSpec(memory_space=pltpu.VMEM)] * 2,
-        out_shape=[out, out],
+        out_specs=[pl.BlockSpec(memory_space=pltpu.VMEM)] * 4,
+        out_shape=[out] * 4,
         scratch_shapes=[pltpu.VMEM(a.shape, a.dtype) for a in points]
         + [
             pltpu.VMEM(by_pair.shape, by_pair.dtype),
@@ -243,8 +241,8 @@
     for q in range(q_local):
         for part in range(2):
             m = modes_ref[q, part].astype(f32)
-            cycle[0:MODES, part * LANES : part * LANES + MODES] = m
-            cycle[MODES : 2 * MODES, part * LANES : part * LANES + MODES] = m
+            cycle[q, 0:MODES, part * LANES : part * LANES + MODES] = m
+            cycle[q, MODES : 2 * MODES, part * LANES : part * LANES + MODES] = m
         sums = [None] * 5
         for phase in range(phases):
             start = (per_source * phase) % MODES
@@ -256,7 +254,7 @@
                 ],
                 axis=0,
             )[:, :depth].astype(bf16)
-            right = cycle[pl.ds(start, depth), :]
+            right = cycle[q, pl.ds(start, depth), :]
             at = lax.broadcasted_iota(jnp.int32, right.shape, 0)
             until = min(MODES - start, per_source)
             pieces = [(first, jnp.where(at < until, right, 0.0))]
@@ -272,12 +270,12 @@
             real = sums[n][:half, :LANES] - sums[n][half:, LANES:]
             imag = sums[n][:half, LANES:] + sums[n][half:, :LANES]
             for k in range(k_local):
-                moded[k, 0, pl.ds(n, runs, stride=5), :] = real[k * runs : (k + 1) * runs]
-                moded[k, 1, pl.ds(n, runs, stride=5), :] = imag[k * runs : (k + 1) * runs]
+                moded[q * k_local + k, 0, pl.ds(n, runs, stride=5), :] = real[k * runs : (k + 1) * runs]
+                moded[q * k_local + k, 1, pl.ds(n, runs, stride=5), :] = imag[k * runs : (k + 1) * runs]
         phonon = None
         for k in range(k_local):
             i = q * k_local + k
-            right = jnp.concatenate([moded[k, 0], moded[k, 1]], axis=1).astype(bf16)
+            right = jnp.concatenate([moded[i, 0], moded[i, 1]], axis=1).astype(bf16)
             both = jnp.dot(turned_ref[i], right, preferred_element_type=f32)
             real = both[:NB, :MODES] + both[NB:, LANES : LANES + MODES]
             imag = both[:NB, LANES : LANES + MODES] - both[NB:, :MODES]
@@ -304,15 +302,15 @@
         ],
         scratch_shapes=[
             pltpu.VMEM((PARTS, rows, LANES), jnp.float32),
-            pltpu.VMEM((2 * modes, 2 * LANES), jnp.float32),
-            pltpu.VMEM((PARTS // 2, 2, NB, LANES), jnp.float32),
+            pltpu.VMEM((q_local, 2 * modes, 2 * LANES), jnp.float32),
+            pltpu.VMEM((q_local * PARTS // 2, 2, NB, LANES), jnp.float32),
         ],
         compiler_params=pltpu.CompilerParams(vmem_limit_bytes=48 << 20),
     )(block, phonon_modes, turned, absorb, count, pick)
 
 
-def added(left, right):
-    return (left.astype(jnp.float32) + right.astype(jnp.float32)).astype(jnp.bfloat16)
+def added(*arrays):
+    return sum(a.astype(jnp.float32) for a in arrays).astype(jnp.bfloat16)
 
 
 def on_device(
@@ -331,13 +329,17 @@
     bose_factors,
 ):
     q_local = frequencies.shape[0]
-    send, keep = products(kpoints, qpoints, electron_cells, phonon_cells, coupling)
-    q_total, width = send.shape[1:]
     members = lax.axis_size("ka")
     beside = [(i, i ^ 1) for i in range(members)]
     across = [(i, i ^ 2) for i in range(members)]
-    chip = added(keep, lax.ppermute(send, "ka", beside))
-    theirs = lax.ppermute(chip[0], "ka", across)
+    near_keep, near_send, far_keep, far_send = products(
+        kpoints, qpoints, electron_cells, phonon_cells, coupling
+    )
+    q_total, width = far_send.shape
+    chip = added(far_keep, lax.ppermute(far_send, "ka", beside))
+    chip, near_send, energy_k = lax.optimization_barrier((chip, near_send, energy_k))
+    theirs = lax.ppermute(chip, "ka", across)
+    near = lax.ppermute(near_send, "ka", beside)
     prepared = tables(
         energies_kq,
         occupations_kq,
@@ -348,7 +350,7 @@
         occupation_k,
         width,
     )
-    chunks = added(chip[1], theirs).reshape(q_total // q_local, q_local, width)
+    chunks = added(near_keep, near, theirs).reshape(q_total // q_local, q_local, width)
     chunks, prepared, phonon_modes = lax.optimization_barrier((chunks, prepared, phonon_modes))
     arrived = lax.all_to_all(chunks, "pb", 0, 0, tiled=True)
     absorb, count, turned, pick = prepared

time: 71.8 us -> 70.2 us (0.978)
  Pallas kernels: 12.5 us -> 11 us
    pallas_call x1, Pallas kernels: 7.79 us -> 6.28 us  [products(): pl.pallas_call(product_kernel, in_specs=[pl.BlockSpec(memory_space=pltpu....]
    ppermute x2 -> x3, waiting for transfers between devices: 8.38 us -> 8.14 us  [the longest x1 6.52 us: on_device(): theirs = lax.ppermute(chip, 'ka', across)]
    ppermute x2 -> x3, starting transfers between devices: 2.14 us -> 2.16 us  [the longest x1 1.85 us: on_device(): theirs = lax.ppermute(chip, 'ka', across)]
  transfers between devices with their start and end apart: 6 -> 7, of which waited for: 5 -> 5; matrix products, arithmetic and copies ran while one was open for 1% -> 1% of each run, Pallas kernels for 2% -> 2%
where the time goes in v5:
time: 70.2 us; the launch traced here: 70 us
  blocking collectives  29.6 us (42%)
  waiting for transfers between devices  18.2 us (26%)
  Pallas kernels  11 us (16%)
  starting transfers between devices  8.71 us (12%)
  other arithmetic  1.44 us (2%)
  between operations  0.81 us (1%)
    all_to_all x1, blocking collectives, on_device(): arrived = lax.all_to_all(chunks, 'pb', 0, 0, tiled=True)  29.6 us
    all_to_all x1, waiting for transfers between devices, on_device(): electrons = lax.all_to_all(copies, 'pb', 0, 0, tiled=True)  8.25 us
    ppermute x1, waiting for transfers between devices, on_device(): theirs = lax.ppermute(chip, 'ka', across)  6.52 us
    pallas_call x1, Pallas kernels, products(): pl.pallas_call(product_kernel, in_specs=[pl.BlockSpec(memory_space=pltpu....  6.28 us
    all_to_all x1, starting transfers between devices, on_device(): electrons = lax.all_to_all(copies, 'pb', 0, 0, tiled=True)  4.6 us
    pallas_call x1, Pallas kernels, widths(): pl.pallas_call(width_kernel, in_specs=[vmem] * 6, out_specs=[vmem] * 2, o...  3.07 us
    ppermute x3, starting transfers between devices, on_device(): lax.ppermute(phonon, 'ka', [(i, i ^ flip) for i in range(members)])  1.94 us
    ppermute x1, starting transfers between devices, on_device(): theirs = lax.ppermute(chip, 'ka', across)  1.85 us
  transfers between devices with their start and end apart: 7, of which 5 were waited for; matrix products, arithmetic and copies ran while one was open for 1% of the time, Pallas kernels for 2%

profile of v5, /device:TPU:32, one launch (start us, length us, event | category | flops | bytes accessed | tf_op | source)
XLA Modules:
  0.0 70.0 jit_solution(16549886155505736315)
XLA Ops:
  0.6 0.0 copy-start.6
  0.6 0.0 copy-start.5
  0.7 0.0 copy-start.4
  0.7 0.0 copy-start.7
  0.7 0.0 copy-start.3
  0.7 0.0 copy-start.2
  0.7 6.3 %shard_map.140 = (bf16[256,640]{1,0:T(8,128)(2,1)S(1)}, bf16[256,640]{1,0:T(8,128)(2,1)S(1)}, bf16[256,640]{1,0:T(8,128)(2,1)S(1)}, bf16[256,640]{1,0:T(8,128)(2,1)S(1)}) custom-call(s32[3,16]{1,0:T(4,128)} %kpt_hbm.1, s32[3,256]{1,0:T(4,128)} %qpt_hbm.1, s32[3,320]{1,0:T(4,128)} %ecell_hbm.1, s32[3,320]{1,0:T(4,128)} %pcell_hbm.1, ...), custom_call_target="tpu_custom_call" | custom-call | tf_op jit(solution)/shard_map/pallas_call | solution.py:142
  7.0 0.1 collective-permute-start
  7.1 1.6 %collective-permute-done = bf16[256,640]{1,0:T(8,128)(2,1)S(1)} collective-permute-done((bf16[256,640]{1,0:T(8,128)(2,1)S(1)}, bf16[256,640]{1,0:T(8,128)(2,1)S(1)}, u32[]{:S(2)}, u32[]{:S(2)}) %collective-permute-start) | collective-permute-done | bytes 327712 | tf_op jit(solution)/shard_map/ppermute | solution.py:339
  8.7 0.1 add_convert_fusion.1
  8.8 0.2 collective-permute-start.1
  9.0 1.8 %collective-permute-start.2 = (bf16[256,640]{1,0:T(8,128)(2,1)S(1)}, bf16[256,640]{1,0:T(8,128)(2,1)S(1)}, u32[]{:S(2)}, u32[]{:S(2)}) collective-permute-start(bf16[256,640]{1,0:T(8,128)(2,1)S(1)} %add_convert_fusion.1), channel_id=1, source_target_pairs={{0,2},{1,3},{2,0},{3,1},{4,6},{5,7},{6,4},{7,5},{8,10},{9,11},{10,... | collective-permute-start | bytes 983048 | tf_op jit(solution)/shard_map/ppermute | solution.py:341
  10.9 0.0 copy-done.7
  10.9 1.6 %shard_map.141 = (f32[16,40,120]{2,1,0:T(8,128)S(1)}, f32[16,40,120]{2,1,0:T(8,128)S(1)}, bf16[16,80,40]{2,1,0:T(8,128)(2,1)S(1)}, bf16[640,1024]{1,0:T(8,128)(2,1)S(1)}) custom-call(f32[16,40]{1,0:T(8,128)S(1)} %bitcast.5, f32[16,40]{1,0:T(8,128)S(1)} %bitcast.6, f32[4,120]{1,0:T(4,128)S(1)} %copy-done.4, f32[4,120]{1,0:T(4,128)S(1)} %copy-done.5, ...), custom_call_target="tpu_custom_call" | custom-call | tf_op jit(solution)/shard_map/pallas_call | solution.py:199
  12.6 0.0 collective-permute-done.1
  12.6 6.5 %collective-permute-done.2 = bf16[256,640]{1,0:T(8,128)(2,1)S(1)} collective-permute-done((bf16[256,640]{1,0:T(8,128)(2,1)S(1)}, bf16[256,640]{1,0:T(8,128)(2,1)S(1)}, u32[]{:S(2)}, u32[]{:S(2)}) %collective-permute-start.2) | collective-permute-done | bytes 327712 | tf_op jit(solution)/shard_map/ppermute | solution.py:341
  19.1 0.1 add_convert_fusion
  19.2 0.1 reshape.19
  19.3 29.6 %all_to_all.10 = bf16[64,4,640]{2,1,0:T(4,128)(2,1)S(1)} all-to-all(bf16[64,4,640]{2,1,0:T(4,128)(2,1)S(1)} %reshape.19), channel_id=1, replica_groups=mesh['pb'=64,'ka'=4] {'pb'}, dimensions={0} | all-to-all | bytes 655360 | tf_op jit(solution)/shard_map/all_to_all | solution.py:355
  49.0 0.1 reshape.23.block_ref
  49.0 0.0 copy-done.1
  49.1 3.1 %shard_map.142 = (f32[64,4,120]{2,1,0:T(4,128)}, f32[4,120]{1,0:T(4,128)S(1)}) custom-call(bf16[256,640]{1,0:T(8,128)(2,1)S(1)} %reshape.23.block_ref, bf16[4,2,120,120]{3,2,1,0:T(8,128)(2,1)S(1)} %copy-done.1, bf16[16,80,40]{2,1,0:T(8,128)(2,1)S(1)} %get-tuple-element.34.turned_ref, f32[16,40,120]{2,1,0:T(8,128)S(1)} %get-tuple-element.35.absorb_ref, ...), custom_call_target="tpu_custom_call" | custom-call | tf_op jit(solution)/shard_map/pallas_call | solution.py:295
  52.1 4.6 %all-to-all-start.1 = ((f32[64,4,120]{2,1,0:T(4,128)}), f32[64,4,120]{2,1,0:T(4,128)S(1)}, u32[]{:S(2)}, u32[]{:S(2)}) async-start(f32[64,4,120]{2,1,0:T(4,128)} %get-tuple-element.38), calls=%async_computation.1 | async-start | bytes 262144 | tf_op jit(solution)/shard_map/all_to_all | solution.py:370
  56.7 0.1 collective-permute-start.5
  56.8 1.1 %collective-permute-start.4 = (f32[4,120]{1,0:T(4,128)S(1)}, f32[4,120]{1,0:T(4,128)S(1)}, u32[]{:S(2)}, u32[]{:S(2)}) collective-permute-start(f32[4,120]{1,0:T(4,128)S(1)} %get-tuple-element.39), channel_id=1, source_target_pairs={{0,2},{1,3},{2,0},{3,1},{4,6},{5,7},{6,4},{7,5},{8,10},{9,11},{10,... | collective-permute-start | bytes 5768 | tf_op jit(solution)/shard_map/ppermute | solution.py:367
  57.9 0.8 %collective-permute-start.3 = (f32[4,120]{1,0:T(4,128)S(1)}, f32[4,120]{1,0:T(4,128)S(1)}, u32[]{:S(2)}, u32[]{:S(2)}) collective-permute-start(f32[4,120]{1,0:T(4,128)S(1)} %get-tuple-element.39), channel_id=1, source_target_pairs={{0,1},{1,0},{2,3},{3,2},{4,5},{5,4},{6,7},{7,6},{8,9},{9,8},{10,11... | collective-permute-start | bytes 5768 | tf_op jit(solution)/shard_map/ppermute | solution.py:367
  58.7 1.2 %collective-permute-done.5 = f32[4,120]{1,0:T(4,128)S(1)} collective-permute-done((f32[4,120]{1,0:T(4,128)S(1)}, f32[4,120]{1,0:T(4,128)S(1)}, u32[]{:S(2)}, u32[]{:S(2)}) %collective-permute-start.5) | collective-permute-done | bytes 1952 | tf_op jit(solution)/shard_map/ppermute | solution.py:367
  59.9 0.6 collective-permute-done.4
  60.5 0.0 collective-permute-done.3
  60.5 0.6 add_add_fusion
  61.1 8.3 %all-to-all-done.1 = f32[64,4,120]{2,1,0:T(4,128)S(1)} async-done(((f32[64,4,120]{2,1,0:T(4,128)}), f32[64,4,120]{2,1,0:T(4,128)S(1)}, u32[]{:S(2)}, u32[]{:S(2)}) %all-to-all-start.1) | async-done | bytes 122912 | tf_op jit(solution)/shard_map/all_to_all | solution.py:370
  69.4 0.7 reduce_sum.9
  (8 shorter events, 0.0 us)
Async XLA Ops:
  0.6 10.2 %copy-start.6 = (f32[4]{0:T(128)S(1)}, f32[4]{0:T(128)}, u32[]{:S(2)}) copy-start(f32[4]{0:T(128)} %ek_ref) | copy-start | bytes 52
  0.6 10.2 %copy-start.5 = (f32[4,120]{1,0:T(4,128)S(1)}, f32[4,120]{1,0:T(4,128)}, u32[]{:S(2)}) copy-start(f32[4,120]{1,0:T(4,128)} %bose_ref.1) | copy-start | bytes 5764
  0.7 10.2 %copy-start.4 = (f32[4,120]{1,0:T(4,128)S(1)}, f32[4,120]{1,0:T(4,128)}, u32[]{:S(2)}) copy-start(f32[4,120]{1,0:T(4,128)} %omega_ref.1) | copy-start | bytes 5764
  0.7 10.2 %copy-start.7 = (f32[4]{0:T(128)S(1)}, f32[4]{0:T(128)}, u32[]{:S(2)}) copy-start(f32[4]{0:T(128)} %ok_ref.1) | copy-start | bytes 52
  0.7 10.2 %copy-start.3 = (f32[4,4,40]{2,1,0:T(4,128)S(1)}, f32[4,4,40]{2,1,0:T(4,128)}, u32[]{:S(2)}) copy-start(f32[4,4,40]{2,1,0:T(4,128)} %param.21) | copy-start | bytes 7684
  0.7 10.2 %copy-start.2 = (f32[4,4,40]{2,1,0:T(4,128)S(1)}, f32[4,4,40]{2,1,0:T(4,128)}, u32[]{:S(2)}) copy-start(f32[4,4,40]{2,1,0:T(4,128)} %param.20) | copy-start | bytes 7684
  0.7 10.2 %copy-start = (bf16[4,4,2,40,40]{4,3,2,1,0:T(8,128)(2,1)S(1)}, bf16[4,4,2,40,40]{4,3,2,1,0:T(8,128)(2,1)}, u32[]{:S(2)}) copy-start(bf16[4,4,2,40,40]{4,3,2,1,0:T(8,128)(2,1)} %param.19) | copy-start | bytes 307204
  0.7 48.3 %copy-start.1 = (bf16[4,2,120,120]{3,2,1,0:T(8,128)(2,1)S(1)}, bf16[4,2,120,120]{3,2,1,0:T(8,128)(2,1)}, u32[]{:S(2)}) copy-start(bf16[4,2,120,120]{3,2,1,0:T(8,128)(2,1)} %modes_ref) | copy-start | bytes 691204
  7.0 1.7 %collective-permute-start = (bf16[256,640]{1,0:T(8,128)(2,1)S(1)}, bf16[256,640]{1,0:T(8,128)(2,1)S(1)}, u32[]{:S(2)}, u32[]{:S(2)}) collective-permute-start(bf16[256,640]{1,0:T(8,128)(2,1)S(1)} %get-tuple-element.23), channel_id=1, source_target_pairs={{0,1},{1,0},{2,3},{3,2},{4,5},{5,4},{6,7},{7,6},{8,9},{9,8},{10,11... | collective-permute-start | bytes 983048 | tf_op jit(solution)/shard_map/ppermute | solution.py:339
  8.8 3.8 %collective-permute-start.1 = (bf16[256,640]{1,0:T(8,128)(2,1)S(1)}, bf16[256,640]{1,0:T(8,128)(2,1)S(1)}, u32[]{:S(2)}, u32[]{:S(2)}) collective-permute-start(bf16[256,640]{1,0:T(8,128)(2,1)S(1)} %get-tuple-element.25), channel_id=1, source_target_pairs={{0,1},{1,0},{2,3},{3,2},{4,5},{5,4},{6,7},{7,6},{8,9},{9,8},{10,11... | collective-permute-start | bytes 983048 | tf_op jit(solution)/shard_map/ppermute | solution.py:342
  9.0 10.1 %collective-permute-start.2 = (bf16[256,640]{1,0:T(8,128)(2,1)S(1)}, bf16[256,640]{1,0:T(8,128)(2,1)S(1)}, u32[]{:S(2)}, u32[]{:S(2)}) collective-permute-start(bf16[256,640]{1,0:T(8,128)(2,1)S(1)} %add_convert_fusion.1), channel_id=1, source_target_pairs={{0,2},{1,3},{2,0},{3,1},{4,6},{5,7},{6,4},{7,5},{8,10},{9,11},{10,... | collective-permute-start | bytes 983048 | tf_op jit(solution)/shard_map/ppermute | solution.py:341
  52.1 17.2 %all-to-all-start.1 = ((f32[64,4,120]{2,1,0:T(4,128)}), f32[64,4,120]{2,1,0:T(4,128)S(1)}, u32[]{:S(2)}, u32[]{:S(2)}) async-start(f32[64,4,120]{2,1,0:T(4,128)} %get-tuple-element.38), calls=%async_computation.1 | async-start | bytes 262144 | tf_op jit(solution)/shard_map/all_to_all | solution.py:370
  56.7 3.2 %collective-permute-start.5 = (f32[4,120]{1,0:T(4,128)S(1)}, f32[4,120]{1,0:T(4,128)S(1)}, u32[]{:S(2)}, u32[]{:S(2)}) collective-permute-start(f32[4,120]{1,0:T(4,128)S(1)} %get-tuple-element.39), channel_id=1, source_target_pairs={{0,3},{1,2},{2,1},{3,0},{4,7},{5,6},{6,5},{7,4},{8,11},{9,10},{10,... | collective-permute-start | bytes 5768 | tf_op jit(solution)/shard_map/ppermute | solution.py:367
  56.8 3.7 %collective-permute-start.4 = (f32[4,120]{1,0:T(4,128)S(1)}, f32[4,120]{1,0:T(4,128)S(1)}, u32[]{:S(2)}, u32[]{:S(2)}) collective-permute-start(f32[4,120]{1,0:T(4,128)S(1)} %get-tuple-element.39), channel_id=1, source_target_pairs={{0,2},{1,3},{2,0},{3,1},{4,6},{5,7},{6,4},{7,5},{8,10},{9,11},{10,... | collective-permute-start | bytes 5768 | tf_op jit(solution)/shard_map/ppermute | solution.py:367
  57.9 2.6 %collective-permute-start.3 = (f32[4,120]{1,0:T(4,128)S(1)}, f32[4,120]{1,0:T(4,128)S(1)}, u32[]{:S(2)}, u32[]{:S(2)}) collective-permute-start(f32[4,120]{1,0:T(4,128)S(1)} %get-tuple-element.39), channel_id=1, source_target_pairs={{0,1},{1,0},{2,3},{3,2},{4,5},{5,4},{6,7},{7,6},{8,9},{9,8},{10,11... | collective-permute-start | bytes 5768 | tf_op jit(solution)/shard_map/ppermute | solution.py:367

commit v6 on v5

--- a/solution.py
+++ b/solution.py
@@ -1,3 +1,4 @@
+import functools
 import math
 
 import jax
@@ -15,6 +16,7 @@
 STRIP = 16
 LANES = 128
 PARTS = 8
+AHEAD = 3
 
 
 def whole_turn_cosine(ticks):
@@ -33,12 +35,12 @@
 
 def product_kernel(
     kpt_hbm, qpt_hbm, ecell_hbm, pcell_hbm, g_hbm, near_keep, near_send, far_keep, far_send,
-    kpt_ref, qpt_ref, ecell_ref, pcell_ref, g_ref, table, rows, small_sem, strip_sem,
+    kpt_ref, qpt_ref, ecell_ref, pcell_ref, g_ref, table, rows, small_sem, strip_sem, *, first_pair,
 ):
     q_total = qpt_ref.shape[1]
     cells = g_ref.shape[2]
-    pairs = g_hbm.shape[1]
-    phonons = g_hbm.shape[3]
+    pairs = g_ref.shape[1]
+    phonons = g_ref.shape[3]
     groups = kpt_ref.shape[1] // 4
     pitch = table.shape[1] // 2
     f32 = jnp.float32
@@ -55,9 +57,13 @@
         copy.wait()
     strips = []
     for first in range(0, pairs, STRIP):
-        part = pl.ds(first, min(STRIP, pairs - first))
+        size = min(STRIP, pairs - first)
         strips.append(
-            pltpu.make_async_copy(g_hbm.at[:, part], g_ref.at[:, part], strip_sem.at[len(strips)])
+            pltpu.make_async_copy(
+                g_hbm.at[:, pl.ds(first_pair + first, size)],
+                g_ref.at[:, pl.ds(first, size)],
+                strip_sem.at[len(strips)],
+            )
         )
         strips[-1].start()
     blank = jnp.zeros((table.shape[0], pitch - phonons), bf16)
@@ -127,8 +133,8 @@
     turned_rows(len(strips) - 1)
 
 
-def products(kpoints, qpoints, electron_cells, phonon_cells, coupling):
-    parts, cells, pairs, phonons = coupling.shape
+def products(kpoints, qpoints, electron_cells, phonon_cells, coupling, first_pair, pairs):
+    parts, cells, _, phonons = coupling.shape
     k_total = kpoints.shape[1]
     q_total = qpoints.shape[1]
     steps = pl.cdiv(pairs, STRIP)
@@ -140,13 +146,13 @@
         for a in (kpoints, qpoints, electron_cells, phonon_cells)
     ]
     return pl.pallas_call(
-        product_kernel,
+        functools.partial(product_kernel, first_pair=first_pair),
         in_specs=[pl.BlockSpec(memory_space=pltpu.HBM)] * 5,
         out_specs=[pl.BlockSpec(memory_space=pltpu.VMEM)] * 4,
         out_shape=[out] * 4,
         scratch_shapes=[pltpu.VMEM(a.shape, a.dtype) for a in points]
         + [
-            pltpu.VMEM(by_pair.shape, by_pair.dtype),
+            pltpu.VMEM((parts, pairs, cells, phonons), by_pair.dtype),
             pltpu.VMEM((q_total, 2 * pitch), jnp.bfloat16),
             pltpu.VMEM((2, 2 * k_total * STRIP, 2 * pitch), jnp.bfloat16),
             pltpu.SemaphoreType.DMA((4,)),
@@ -332,14 +338,27 @@
     members = lax.axis_size("ka")
     beside = [(i, i ^ 1) for i in range(members)]
     across = [(i, i ^ 2) for i in range(members)]
-    near_keep, near_send, far_keep, far_send = products(
-        kpoints, qpoints, electron_cells, phonon_cells, coupling
-    )
-    q_total, width = far_send.shape
-    chip = added(far_keep, lax.ppermute(far_send, "ka", beside))
-    chip, near_send, energy_k = lax.optimization_barrier((chip, near_send, energy_k))
-    theirs = lax.ppermute(chip, "ka", across)
-    near = lax.ppermute(near_send, "ka", beside)
+    pairs = coupling.shape[2]
+    ahead = min(AHEAD * STRIP, pairs)
+    near_parts = []
+    far_parts = []
+    for first, count in ((0, ahead), (ahead, pairs - ahead)):
+        near_keep, near_send, far_keep, far_send = products(
+            kpoints, qpoints, electron_cells, phonon_cells, coupling, first, count
+        )
+        chip = added(far_keep, lax.ppermute(far_send, "ka", beside))
+        near_parts.append((near_keep, near_send))
+        chip, kpoints, energy_k, near_parts = lax.optimization_barrier(
+            (chip, kpoints, energy_k, near_parts)
+        )
+        far_parts.append(lax.ppermute(chip, "ka", across))
+    q_total = qpoints.shape[1]
+    sums = [
+        added(near_keep, lax.ppermute(near_send, "ka", beside), theirs)
+        for (near_keep, near_send), theirs in zip(near_parts, far_parts)
+    ]
+    whole = jnp.concatenate(sums, axis=1)
+    width = whole.shape[1]
     prepared = tables(
         energies_kq,
         occupations_kq,
@@ -350,7 +369,7 @@
         occupation_k,
         width,
     )
-    chunks = added(near_keep, near, theirs).reshape(q_total // q_local, q_local, width)
+    chunks = whole.reshape(q_total // q_local, q_local, width)
     chunks, prepared, phonon_modes = lax.optimization_barrier((chunks, prepared, phonon_modes))
     arrived = lax.all_to_all(chunks, "pb", 0, 0, tiled=True)
     absorb, count, turned, pick = prepared

time: 70.2 us -> 74.2 us (1.057)
  Pallas kernels: 11 us -> 13.3 us
  waiting for transfers between devices: 18.2 us -> 19.2 us
    pallas_call x1 -> x2, Pallas kernels: 6.28 us -> 8.63 us  [products(): pl.pallas_call(functools.partial(product_kernel, first_pair=first_pair),...]
    ppermute x1 -> x2, waiting for transfers between devices: 1.62 us -> 2.64 us  [on_device(): chip = added(far_keep, lax.ppermute(far_send, 'ka', beside))]
    ppermute x2 -> x4, waiting for transfers between devices: 6.53 us -> 6.19 us  [the longest x2 6.19 us: on_device(): far_parts.append(lax.ppermute(chip, 'ka', across))]
    ppermute x2 -> x4, starting transfers between devices: 2.07 us -> 2.28 us  [the longest x2 2.04 us: on_device(): far_parts.append(lax.ppermute(chip, 'ka', across))]
  transfers between devices with their start and end apart: 7 -> 10, of which waited for: 5 -> 7; matrix products, arithmetic and copies ran while one was open for 1% -> 1% of each run, Pallas kernels for 2% -> 2%
where the time goes in v6:
time: 74.2 us; the launch traced here: 73.6 us
  blocking collectives  29.4 us (40%)
  waiting for transfers between devices  19.2 us (26%)
  Pallas kernels  13.3 us (18%)
  starting transfers between devices  9.15 us (12%)
  other arithmetic  1.49 us (2%)
  between operations  0.84 us (1%)
    all_to_all x1, blocking collectives, on_device(): arrived = lax.all_to_all(chunks, 'pb', 0, 0, tiled=True)  29.4 us
    pallas_call x2, Pallas kernels, products(): pl.pallas_call(functools.partial(product_kernel, first_pair=first_pair),...  8.63 us
    all_to_all x1, waiting for transfers between devices, on_device(): electrons = lax.all_to_all(copies, 'pb', 0, 0, tiled=True)  8.4 us
    ppermute x2, waiting for transfers between devices, on_device(): far_parts.append(lax.ppermute(chip, 'ka', across))  6.19 us
    all_to_all x1, starting transfers between devices, on_device(): electrons = lax.all_to_all(copies, 'pb', 0, 0, tiled=True)  4.61 us
    pallas_call x1, Pallas kernels, widths(): pl.pallas_call(width_kernel, in_specs=[vmem] * 6, out_specs=[vmem] * 2, o...  3.06 us
    ppermute x2, waiting for transfers between devices, on_device(): chip = added(far_keep, lax.ppermute(far_send, 'ka', beside))  2.64 us
    ppermute x2, starting transfers between devices, on_device(): far_parts.append(lax.ppermute(chip, 'ka', across))  2.04 us
  transfers between devices with their start and end apart: 10, of which 7 were waited for; matrix products, arithmetic and copies ran while one was open for 1% of the time, Pallas kernels for 2%

profile of v6, /device:TPU:32, one launch (start us, length us, event | category | flops | bytes accessed | tf_op | source)
XLA Modules:
  0.0 73.6 jit_solution(15108710652600298228)
XLA Ops:
  0.7 4.9 %shard_map.140 = (bf16[256,384]{1,0:T(8,128)(2,1)S(1)}, bf16[256,384]{1,0:T(8,128)(2,1)S(1)}, bf16[256,384]{1,0:T(8,128)(2,1)S(1)}, bf16[256,384]{1,0:T(8,128)(2,1)S(1)}) custom-call(s32[3,16]{1,0:T(4,128)} %kpt_hbm.2, s32[3,256]{1,0:T(4,128)} %qpt_hbm.3, s32[3,320]{1,0:T(4,128)} %ecell_hbm.3, s32[3,320]{1,0:T(4,128)} %pcell_hbm.3, ...), custom_call_target="tpu_custom_call" | custom-call | tf_op jit(solution)/shard_map/pallas_call | solution.py:148
  5.6 0.0 copy-start.1
  5.6 0.1 collective-permute-start
  5.7 1.4 %collective-permute-done = bf16[256,384]{1,0:T(8,128)(2,1)S(1)} collective-permute-done((bf16[256,384]{1,0:T(8,128)(2,1)S(1)}, bf16[256,384]{1,0:T(8,128)(2,1)S(1)}, u32[]{:S(2)}, u32[]{:S(2)}) %collective-permute-start) | collective-permute-done | bytes 196640 | tf_op jit(solution)/shard_map/ppermute | solution.py:349
  7.1 0.1 add_convert_fusion.1
  7.2 3.8 %shard_map.141 = (bf16[256,256]{1,0:T(8,128)(2,1)S(1)}, bf16[256,256]{1,0:T(8,128)(2,1)S(1)}, bf16[256,256]{1,0:T(8,128)(2,1)S(1)}, bf16[256,256]{1,0:T(8,128)(2,1)S(1)}) custom-call(s32[3,16]{1,0:T(4,128)} %kpt_hbm.2, s32[3,256]{1,0:T(4,128)} %qpt_hbm.3, s32[3,320]{1,0:T(4,128)} %ecell_hbm.3, s32[3,320]{1,0:T(4,128)} %pcell_hbm.3, ...), custom_call_target="tpu_custom_call" | custom-call | tf_op jit(solution)/shard_map/pallas_call | solution.py:148
  10.9 0.2 collective-permute-start.1
  11.2 1.2 %collective-permute-done.1 = bf16[256,256]{1,0:T(8,128)(2,1)S(1)} collective-permute-done((bf16[256,256]{1,0:T(8,128)(2,1)S(1)}, bf16[256,256]{1,0:T(8,128)(2,1)S(1)}, u32[]{:S(2)}, u32[]{:S(2)}) %collective-permute-start.1) | collective-permute-done | bytes 131104 | tf_op jit(solution)/shard_map/ppermute | solution.py:349
  12.4 0.2 collective-permute-start.4
  12.7 1.8 %collective-permute-start.5 = (bf16[256,256]{1,0:T(8,128)(2,1)S(1)}, bf16[256,256]{1,0:T(8,128)(2,1)S(1)}, u32[]{:S(2)}, u32[]{:S(2)}) collective-permute-start(bf16[256,256]{1,0:T(8,128)(2,1)S(1)} %add_convert_fusion.3), channel_id=1, source_target_pairs={{0,2},{1,3},{2,0},{3,1},{4,6},{5,7},{6,4},{7,5},{8,10},{9,11},{10,... | collective-permute-start | bytes 393224 | tf_op jit(solution)/shard_map/ppermute | solution.py:354
  14.5 0.2 collective-permute-start.3
  14.7 0.0 collective-permute-start.2
  14.8 1.6 %shard_map.142 = (f32[16,40,120]{2,1,0:T(8,128)S(1)}, f32[16,40,120]{2,1,0:T(8,128)S(1)}, bf16[16,80,40]{2,1,0:T(8,128)(2,1)S(1)}, bf16[640,1024]{1,0:T(8,128)(2,1)S(1)}) custom-call(f32[16,40]{1,0:T(8,128)S(1)} %bitcast.5, f32[16,40]{1,0:T(8,128)S(1)} %bitcast.6, f32[4,120]{1,0:T(4,128)S(1)} %copy-done.4, f32[4,120]{1,0:T(4,128)S(1)} %copy-done.5, ...), custom_call_target="tpu_custom_call" | custom-call | tf_op jit(solution)/shard_map/pallas_call | solution.py:205
  16.4 0.0 collective-permute-done.4
  16.4 2.6 %collective-permute-done.5 = bf16[256,256]{1,0:T(8,128)(2,1)S(1)} collective-permute-done((bf16[256,256]{1,0:T(8,128)(2,1)S(1)}, bf16[256,256]{1,0:T(8,128)(2,1)S(1)}, u32[]{:S(2)}, u32[]{:S(2)}) %collective-permute-start.5) | collective-permute-done | bytes 131104 | tf_op jit(solution)/shard_map/ppermute | solution.py:354
  19.0 0.1 add_convert_fusion.2
  19.0 3.6 %collective-permute-done.3 = bf16[256,384]{1,0:T(8,128)(2,1)S(1)} collective-permute-done((bf16[256,384]{1,0:T(8,128)(2,1)S(1)}, bf16[256,384]{1,0:T(8,128)(2,1)S(1)}, u32[]{:S(2)}, u32[]{:S(2)}) %collective-permute-start.3) | collective-permute-done | bytes 196640 | tf_op jit(solution)/shard_map/ppermute | solution.py:354
  22.7 0.1 add_convert_fusion
  22.8 0.1 reshape.19
  22.9 29.4 %all_to_all.10 = bf16[64,4,640]{2,1,0:T(4,128)(2,1)S(1)} all-to-all(bf16[64,4,640]{2,1,0:T(4,128)(2,1)S(1)} %reshape.19), channel_id=1, replica_groups=mesh['pb'=64,'ka'=4] {'pb'}, dimensions={0} | all-to-all | bytes 655360 | tf_op jit(solution)/shard_map/all_to_all | solution.py:374
  52.3 0.1 reshape.23.block_ref
  52.4 3.1 %shard_map.143 = (f32[64,4,120]{2,1,0:T(4,128)}, f32[4,120]{1,0:T(4,128)S(1)}) custom-call(bf16[256,640]{1,0:T(8,128)(2,1)S(1)} %reshape.23.block_ref, bf16[4,2,120,120]{3,2,1,0:T(8,128)(2,1)S(1)} %copy-done.1, bf16[16,80,40]{2,1,0:T(8,128)(2,1)S(1)} %get-tuple-element.58.turned_ref, f32[16,40,120]{2,1,0:T(8,128)S(1)} %get-tuple-element.59.absorb_ref, ...), custom_call_target="tpu_custom_call" | custom-call | tf_op jit(solution)/shard_map/pallas_call | solution.py:301
  55.4 4.6 %all-to-all-start.1 = ((f32[64,4,120]{2,1,0:T(4,128)}), f32[64,4,120]{2,1,0:T(4,128)S(1)}, u32[]{:S(2)}, u32[]{:S(2)}) async-start(f32[64,4,120]{2,1,0:T(4,128)} %get-tuple-element.62), calls=%async_computation.1 | async-start | bytes 262144 | tf_op jit(solution)/shard_map/all_to_all | solution.py:389
  60.0 0.1 collective-permute-start.8
  60.1 1.8 %collective-permute-start.7 = (f32[4,120]{1,0:T(4,128)S(1)}, f32[4,120]{1,0:T(4,128)S(1)}, u32[]{:S(2)}, u32[]{:S(2)}) collective-permute-start(f32[4,120]{1,0:T(4,128)S(1)} %get-tuple-element.63), channel_id=1, source_target_pairs={{0,2},{1,3},{2,0},{3,1},{4,6},{5,7},{6,4},{7,5},{8,10},{9,11},{10,... | collective-permute-start | bytes 5768 | tf_op jit(solution)/shard_map/ppermute | solution.py:386
  61.9 0.1 collective-permute-start.6
  62.0 1.2 %collective-permute-done.8 = f32[4,120]{1,0:T(4,128)S(1)} collective-permute-done((f32[4,120]{1,0:T(4,128)S(1)}, f32[4,120]{1,0:T(4,128)S(1)}, u32[]{:S(2)}, u32[]{:S(2)}) %collective-permute-start.8) | collective-permute-done | bytes 1952 | tf_op jit(solution)/shard_map/ppermute | solution.py:386
  63.2 0.8 %collective-permute-done.7 = f32[4,120]{1,0:T(4,128)S(1)} collective-permute-done((f32[4,120]{1,0:T(4,128)S(1)}, f32[4,120]{1,0:T(4,128)S(1)}, u32[]{:S(2)}, u32[]{:S(2)}) %collective-permute-start.7) | collective-permute-done | bytes 1952 | tf_op jit(solution)/shard_map/ppermute | solution.py:386
  64.0 0.0 collective-permute-done.6
  64.0 0.6 add_add_fusion
  64.6 8.4 %all-to-all-done.1 = f32[64,4,120]{2,1,0:T(4,128)S(1)} async-done(((f32[64,4,120]{2,1,0:T(4,128)}), f32[64,4,120]{2,1,0:T(4,128)S(1)}, u32[]{:S(2)}, u32[]{:S(2)}) %all-to-all-start.1) | async-done | bytes 122912 | tf_op jit(solution)/shard_map/all_to_all | solution.py:389
  73.0 0.7 reduce_sum.9
  (18 shorter events, 0.1 us)
Async XLA Ops:
  0.6 14.1 %copy-start = (bf16[4,4,2,40,40]{4,3,2,1,0:T(8,128)(2,1)S(1)}, bf16[4,4,2,40,40]{4,3,2,1,0:T(8,128)(2,1)}, u32[]{:S(2)}) copy-start(bf16[4,4,2,40,40]{4,3,2,1,0:T(8,128)(2,1)} %param.19) | copy-start | bytes 307204
  0.6 14.1 %copy-start.2 = (f32[4,4,40]{2,1,0:T(4,128)S(1)}, f32[4,4,40]{2,1,0:T(4,128)}, u32[]{:S(2)}) copy-start(f32[4,4,40]{2,1,0:T(4,128)} %param.20) | copy-start | bytes 7684
  0.7 14.1 %copy-start.3 = (f32[4,4,40]{2,1,0:T(4,128)S(1)}, f32[4,4,40]{2,1,0:T(4,128)}, u32[]{:S(2)}) copy-start(f32[4,4,40]{2,1,0:T(4,128)} %param.21) | copy-start | bytes 7684
  0.7 14.1 %copy-start.4 = (f32[4,120]{1,0:T(4,128)S(1)}, f32[4,120]{1,0:T(4,128)}, u32[]{:S(2)}) copy-start(f32[4,120]{1,0:T(4,128)} %omega_ref.1) | copy-start | bytes 5764
  0.7 14.1 %copy-start.5 = (f32[4,120]{1,0:T(4,128)S(1)}, f32[4,120]{1,0:T(4,128)}, u32[]{:S(2)}) copy-start(f32[4,120]{1,0:T(4,128)} %bose_ref.1) | copy-start | bytes 5764
  0.7 14.1 %copy-start.6 = (f32[4]{0:T(128)S(1)}, f32[4]{0:T(128)}, u32[]{:S(2)}) copy-start(f32[4]{0:T(128)} %ek_ref) | copy-start | bytes 52
  0.7 14.1 %copy-start.7 = (f32[4]{0:T(128)S(1)}, f32[4]{0:T(128)}, u32[]{:S(2)}) copy-start(f32[4]{0:T(128)} %ok_ref.1) | copy-start | bytes 52
  5.6 46.8 %copy-start.1 = (bf16[4,2,120,120]{3,2,1,0:T(8,128)(2,1)S(1)}, bf16[4,2,120,120]{3,2,1,0:T(8,128)(2,1)}, u32[]{:S(2)}) copy-start(bf16[4,2,120,120]{3,2,1,0:T(8,128)(2,1)} %modes_ref) | copy-start | bytes 691204
  5.6 1.5 %collective-permute-start = (bf16[256,384]{1,0:T(8,128)(2,1)S(1)}, bf16[256,384]{1,0:T(8,128)(2,1)S(1)}, u32[]{:S(2)}, u32[]{:S(2)}) collective-permute-start(bf16[256,384]{1,0:T(8,128)(2,1)S(1)} %get-tuple-element.34), channel_id=1, source_target_pairs={{0,1},{1,0},{2,3},{3,2},{4,5},{5,4},{6,7},{7,6},{8,9},{9,8},{10,11... | collective-permute-start | bytes 589832 | tf_op jit(solution)/shard_map/ppermute | solution.py:349
  10.9 1.4 %collective-permute-start.1 = (bf16[256,256]{1,0:T(8,128)(2,1)S(1)}, bf16[256,256]{1,0:T(8,128)(2,1)S(1)}, u32[]{:S(2)}, u32[]{:S(2)}) collective-permute-start(bf16[256,256]{1,0:T(8,128)(2,1)S(1)} %get-tuple-element.39), channel_id=1, source_target_pairs={{0,1},{1,0},{2,3},{3,2},{4,5},{5,4},{6,7},{7,6},{8,9},{9,8},{10,11... | collective-permute-start | bytes 393224 | tf_op jit(solution)/shard_map/ppermute | solution.py:349
  12.4 4.0 %collective-permute-start.4 = (bf16[256,256]{1,0:T(8,128)(2,1)S(1)}, bf16[256,256]{1,0:T(8,128)(2,1)S(1)}, u32[]{:S(2)}, u32[]{:S(2)}) collective-permute-start(bf16[256,256]{1,0:T(8,128)(2,1)S(1)} %get-tuple-element.49), channel_id=1, source_target_pairs={{0,1},{1,0},{2,3},{3,2},{4,5},{5,4},{6,7},{7,6},{8,9},{9,8},{10,11... | collective-permute-start | bytes 393224 | tf_op jit(solution)/shard_map/ppermute | solution.py:357
  12.7 6.3 %collective-permute-start.5 = (bf16[256,256]{1,0:T(8,128)(2,1)S(1)}, bf16[256,256]{1,0:T(8,128)(2,1)S(1)}, u32[]{:S(2)}, u32[]{:S(2)}) collective-permute-start(bf16[256,256]{1,0:T(8,128)(2,1)S(1)} %add_convert_fusion.3), channel_id=1, source_target_pairs={{0,2},{1,3},{2,0},{3,1},{4,6},{5,7},{6,4},{7,5},{8,10},{9,11},{10,... | collective-permute-start | bytes 393224 | tf_op jit(solution)/shard_map/ppermute | solution.py:354
  14.5 8.2 %collective-permute-start.3 = (bf16[256,384]{1,0:T(8,128)(2,1)S(1)}, bf16[256,384]{1,0:T(8,128)(2,1)S(1)}, u32[]{:S(2)}, u32[]{:S(2)}) collective-permute-start(bf16[256,384]{1,0:T(8,128)(2,1)S(1)} %add_convert_fusion.1), channel_id=1, source_target_pairs={{0,2},{1,3},{2,0},{3,1},{4,6},{5,7},{6,4},{7,5},{8,10},{9,11},{10,... | collective-permute-start | bytes 589832 | tf_op jit(solution)/shard_map/ppermute | solution.py:354
  14.7 8.0 %collective-permute-start.2 = (bf16[256,384]{1,0:T(8,128)(2,1)S(1)}, bf16[256,384]{1,0:T(8,128)(2,1)S(1)}, u32[]{:S(2)}, u32[]{:S(2)}) collective-permute-start(bf16[256,384]{1,0:T(8,128)(2,1)S(1)} %get-tuple-element.46), channel_id=1, source_target_pairs={{0,1},{1,0},{2,3},{3,2},{4,5},{5,4},{6,7},{7,6},{8,9},{9,8},{10,11... | collective-permute-start | bytes 589832 | tf_op jit(solution)/shard_map/ppermute | solution.py:357
  55.4 17.6 %all-to-all-start.1 = ((f32[64,4,120]{2,1,0:T(4,128)}), f32[64,4,120]{2,1,0:T(4,128)S(1)}, u32[]{:S(2)}, u32[]{:S(2)}) async-start(f32[64,4,120]{2,1,0:T(4,128)} %get-tuple-element.62), calls=%async_computation.1 | async-start | bytes 262144 | tf_op jit(solution)/shard_map/all_to_all | solution.py:389
  60.0 3.1 %collective-permute-start.8 = (f32[4,120]{1,0:T(4,128)S(1)}, f32[4,120]{1,0:T(4,128)S(1)}, u32[]{:S(2)}, u32[]{:S(2)}) collective-permute-start(f32[4,120]{1,0:T(4,128)S(1)} %get-tuple-element.63), channel_id=1, source_target_pairs={{0,3},{1,2},{2,1},{3,0},{4,7},{5,6},{6,5},{7,4},{8,11},{9,10},{10,... | collective-permute-start | bytes 5768 | tf_op jit(solution)/shard_map/ppermute | solution.py:386
  60.1 3.9 %collective-permute-start.7 = (f32[4,120]{1,0:T(4,128)S(1)}, f32[4,120]{1,0:T(4,128)S(1)}, u32[]{:S(2)}, u32[]{:S(2)}) collective-permute-start(f32[4,120]{1,0:T(4,128)S(1)} %get-tuple-element.63), channel_id=1, source_target_pairs={{0,2},{1,3},{2,0},{3,1},{4,6},{5,7},{6,4},{7,5},{8,10},{9,11},{10,... | collective-permute-start | bytes 5768 | tf_op jit(solution)/shard_map/ppermute | solution.py:386
  61.9 2.1 %collective-permute-start.6 = (f32[4,120]{1,0:T(4,128)S(1)}, f32[4,120]{1,0:T(4,128)S(1)}, u32[]{:S(2)}, u32[]{:S(2)}) collective-permute-start(f32[4,120]{1,0:T(4,128)S(1)} %get-tuple-element.63), channel_id=1, source_target_pairs={{0,1},{1,0},{2,3},{3,2},{4,5},{5,4},{6,7},{7,6},{8,9},{9,8},{10,11... | collective-permute-start | bytes 5768 | tf_op jit(solution)/shard_map/ppermute | solution.py:386

commit v7 on v5

--- a/solution.py
+++ b/solution.py
@@ -163,6 +163,9 @@
     f32 = jnp.float32
     points = level_ref.shape[0]
     q_local = omega_ref.shape[0]
+    n = lax.broadcasted_iota(jnp.int32, (NB, NB), 0)
+    at = lax.broadcasted_iota(jnp.int32, (NB, NB), 1)
+    order = (n == (at % 8) * (NB // 8) + at // 8).astype(f32).astype(jnp.bfloat16)
     level = jnp.transpose(level_ref[...])
     filled = jnp.transpose(filled_ref[...])
     scale = 1.0 / (SMEARING * math.sqrt(2.0 * math.pi))
@@ -179,8 +182,8 @@
         absorb_ref[i] = ((n + f) * up + (n + 1.0 - f) * down) * electron_scale
         count_ref[i] = (ok_ref[k] - f) * up * phonon_scale
         for part in range(2):
-            turned_ref[i, part * NB : (part + 1) * NB, :] = jnp.transpose(
-                vector_ref[i, part].astype(f32)
+            turned_ref[i, part * NB : (part + 1) * NB, :] = small_dot(
+                vector_ref[i, part], order, ((0,), (0,))
             ).astype(jnp.bfloat16)
     lane = lax.broadcasted_iota(jnp.int32, pick_ref.shape, 0)
     col = lax.broadcasted_iota(jnp.int32, pick_ref.shape, 1)
@@ -232,11 +235,18 @@
     sources = rows // q_local
     phases = 8
     runs = sources // phases
-    block = block_ref[...]
-    for part in range(PARTS):
-        spread[part] = jnp.dot(
-            block, pick_ref[:, part * LANES : (part + 1) * LANES], preferred_element_type=f32
+    to = lax.broadcasted_iota(jnp.int32, (rows, rows), 0)
+    source = lax.broadcasted_iota(jnp.int32, (rows, rows), 1)
+    wanted = (to % runs) * (phases * q_local) + (to // runs) % phases * q_local
+    wanted = wanted + to // (runs * phases)
+    order = (source == wanted).astype(f32).astype(bf16)
+    block = jnp.dot(order, block_ref[...], preferred_element_type=f32).astype(bf16)
+    for part in range(0, PARTS, 2):
+        two = jnp.dot(
+            block, pick_ref[:, part * LANES : (part + 2) * LANES], preferred_element_type=f32
         )
+        spread[part] = two[:, :LANES]
+        spread[part + 1] = two[:, LANES:]
     electron = [None] * k_local
     for q in range(q_local):
         for part in range(2):
@@ -249,7 +259,7 @@
             first = (per_source * phase) // MODES
             left = jnp.concatenate(
                 [
-                    spread[part, pl.ds(phase * q_local + q, runs, stride=phases * q_local), :]
+                    spread[part, (q * phases + phase) * runs : (q * phases + phase + 1) * runs, :]
                     for part in range(PARTS)
                 ],
                 axis=0,
@@ -270,8 +280,8 @@
             real = sums[n][:half, :LANES] - sums[n][half:, LANES:]
             imag = sums[n][:half, LANES:] + sums[n][half:, :LANES]
             for k in range(k_local):
-                moded[q * k_local + k, 0, pl.ds(n, runs, stride=5), :] = real[k * runs : (k + 1) * runs]
-                moded[q * k_local + k, 1, pl.ds(n, runs, stride=5), :] = imag[k * runs : (k + 1) * runs]
+                moded[q * k_local + k, 0, n * runs : (n + 1) * runs, :] = real[k * runs : (k + 1) * runs]
+                moded[q * k_local + k, 1, n * runs : (n + 1) * runs, :] = imag[k * runs : (k + 1) * runs]
         phonon = None
         for k in range(k_local):
             i = q * k_local + k
@@ -337,9 +347,8 @@
     )
     q_total, width = far_send.shape
     chip = added(far_keep, lax.ppermute(far_send, "ka", beside))
-    chip, near_send, energy_k = lax.optimization_barrier((chip, near_send, energy_k))
+    chip, energy_k = lax.optimization_barrier((chip, energy_k))
     theirs = lax.ppermute(chip, "ka", across)
-    near = lax.ppermute(near_send, "ka", beside)
     prepared = tables(
         energies_kq,
         occupations_kq,
@@ -350,6 +359,8 @@
         occupation_k,
         width,
     )
+    near_send, prepared = lax.optimization_barrier((near_send, prepared))
+    near = lax.ppermute(near_send, "ka", beside)
     chunks = added(near_keep, near, theirs).reshape(q_total // q_local, q_local, width)
     chunks, prepared, phonon_modes = lax.optimization_barrier((chunks, prepared, phonon_modes))
     arrived = lax.all_to_all(chunks, "pb", 0, 0, tiled=True)

time: 70.2 us -> 69.3 us (0.987)
  no operation moved by 1% of the time
where the time goes in v7:
time: 69.3 us; the launch traced here: 69 us
  blocking collectives  29.5 us (43%)
  waiting for transfers between devices  18 us (26%)
  Pallas kernels  10.5 us (15%)
  starting transfers between devices  8.65 us (12%)
  other arithmetic  1.44 us (2%)
  between operations  0.81 us (1%)
    all_to_all x1, blocking collectives, on_device(): arrived = lax.all_to_all(chunks, 'pb', 0, 0, tiled=True)  29.5 us
    all_to_all x1, waiting for transfers between devices, on_device(): electrons = lax.all_to_all(copies, 'pb', 0, 0, tiled=True)  8.25 us
    pallas_call x1, Pallas kernels, products(): pl.pallas_call(product_kernel, in_specs=[pl.BlockSpec(memory_space=pltpu....  6.28 us
    ppermute x1, waiting for transfers between devices, on_device(): theirs = lax.ppermute(chip, 'ka', across)  6.26 us
    all_to_all x1, starting transfers between devices, on_device(): electrons = lax.all_to_all(copies, 'pb', 0, 0, tiled=True)  4.6 us
    pallas_call x1, Pallas kernels, widths(): pl.pallas_call(width_kernel, in_specs=[vmem] * 6, out_specs=[vmem] * 2, o...  2.59 us
    ppermute x3, starting transfers between devices, on_device(): lax.ppermute(phonon, 'ka', [(i, i ^ flip) for i in range(members)])  1.94 us
    ppermute x1, starting transfers between devices, on_device(): theirs = lax.ppermute(chip, 'ka', across)  1.92 us
  transfers between devices with their start and end apart: 7, of which 5 were waited for; matrix products, arithmetic and copies ran while one was open for 1% of the time, Pallas kernels for 2%

profile of v7, /device:TPU:32, one launch (start us, length us, event | category | flops | bytes accessed | tf_op | source)
XLA Modules:
  0.0 69.0 jit_solution(7024831896211381510)
XLA Ops:
  0.6 0.0 copy-start.6
  0.6 0.0 copy-start.5
  0.7 0.0 copy-start.4
  0.7 0.0 copy-start.7
  0.7 0.0 copy-start.3
  0.7 6.3 %shard_map.140 = (bf16[256,640]{1,0:T(8,128)(2,1)S(1)}, bf16[256,640]{1,0:T(8,128)(2,1)S(1)}, bf16[256,640]{1,0:T(8,128)(2,1)S(1)}, bf16[256,640]{1,0:T(8,128)(2,1)S(1)}) custom-call(s32[3,16]{1,0:T(4,128)} %kpt_hbm.1, s32[3,256]{1,0:T(4,128)} %qpt_hbm.1, s32[3,320]{1,0:T(4,128)} %ecell_hbm.1, s32[3,320]{1,0:T(4,128)} %pcell_hbm.1, ...), custom_call_target="tpu_custom_call" | custom-call | tf_op jit(solution)/shard_map/pallas_call | solution.py:142
  7.0 0.1 collective-permute-start
  7.1 1.6 %collective-permute-done = bf16[256,640]{1,0:T(8,128)(2,1)S(1)} collective-permute-done((bf16[256,640]{1,0:T(8,128)(2,1)S(1)}, bf16[256,640]{1,0:T(8,128)(2,1)S(1)}, u32[]{:S(2)}, u32[]{:S(2)}) %collective-permute-start) | collective-permute-done | bytes 327712 | tf_op jit(solution)/shard_map/ppermute | solution.py:349
  8.7 0.1 add_convert_fusion.1
  8.8 1.9 %collective-permute-start.2 = (bf16[256,640]{1,0:T(8,128)(2,1)S(1)}, bf16[256,640]{1,0:T(8,128)(2,1)S(1)}, u32[]{:S(2)}, u32[]{:S(2)}) collective-permute-start(bf16[256,640]{1,0:T(8,128)(2,1)S(1)} %add_convert_fusion.1), channel_id=1, source_target_pairs={{0,2},{1,3},{2,0},{3,1},{4,6},{5,7},{6,4},{7,5},{8,10},{9,11},{10,... | collective-permute-start | bytes 983048 | tf_op jit(solution)/shard_map/ppermute | solution.py:351
  10.7 0.0 copy-done.6
  10.7 0.0 copy-done.4
  10.8 1.6 %shard_map.141 = (f32[16,40,120]{2,1,0:T(8,128)S(1)}, f32[16,40,120]{2,1,0:T(8,128)S(1)}, bf16[16,80,40]{2,1,0:T(8,128)(2,1)S(1)}, bf16[640,1024]{1,0:T(8,128)(2,1)S(1)}) custom-call(f32[16,40]{1,0:T(8,128)S(1)} %bitcast.5, f32[16,40]{1,0:T(8,128)S(1)} %bitcast.6, f32[4,120]{1,0:T(4,128)S(1)} %copy-done.4, f32[4,120]{1,0:T(4,128)S(1)} %copy-done.5, ...), custom_call_target="tpu_custom_call" | custom-call | tf_op jit(solution)/shard_map/pallas_call | solution.py:202
  12.4 0.1 collective-permute-start.1
  12.5 6.3 %collective-permute-done.2 = bf16[256,640]{1,0:T(8,128)(2,1)S(1)} collective-permute-done((bf16[256,640]{1,0:T(8,128)(2,1)S(1)}, bf16[256,640]{1,0:T(8,128)(2,1)S(1)}, u32[]{:S(2)}, u32[]{:S(2)}) %collective-permute-start.2) | collective-permute-done | bytes 327712 | tf_op jit(solution)/shard_map/ppermute | solution.py:351
  18.7 0.0 collective-permute-done.1
  18.7 0.1 add_convert_fusion
  18.9 0.1 reshape.22
  18.9 29.5 %all_to_all.10 = bf16[64,4,640]{2,1,0:T(4,128)(2,1)S(1)} all-to-all(bf16[64,4,640]{2,1,0:T(4,128)(2,1)S(1)} %reshape.22), channel_id=1, replica_groups=mesh['pb'=64,'ka'=4] {'pb'}, dimensions={0} | all-to-all | bytes 655360 | tf_op jit(solution)/shard_map/all_to_all | solution.py:366
  48.5 0.1 reshape.23.block_ref
  48.5 0.0 copy-done.1
  48.6 2.6 %shard_map.142 = (f32[64,4,120]{2,1,0:T(4,128)}, f32[4,120]{1,0:T(4,128)S(1)}) custom-call(bf16[256,640]{1,0:T(8,128)(2,1)S(1)} %reshape.23.block_ref, bf16[4,2,120,120]{3,2,1,0:T(8,128)(2,1)S(1)} %copy-done.1, bf16[16,80,40]{2,1,0:T(8,128)(2,1)S(1)} %get-tuple-element.42.turned_ref, f32[16,40,120]{2,1,0:T(8,128)S(1)} %get-tuple-element.43.absorb_ref, ...), custom_call_target="tpu_custom_call" | custom-call | tf_op jit(solution)/shard_map/pallas_call | solution.py:305
  51.1 4.6 %all-to-all-start.1 = ((f32[64,4,120]{2,1,0:T(4,128)}), f32[64,4,120]{2,1,0:T(4,128)S(1)}, u32[]{:S(2)}, u32[]{:S(2)}) async-start(f32[64,4,120]{2,1,0:T(4,128)} %get-tuple-element.46), calls=%async_computation.1 | async-start | bytes 262144 | tf_op jit(solution)/shard_map/all_to_all | solution.py:381
  55.8 0.1 collective-permute-start.5
  55.9 1.0 %collective-permute-start.4 = (f32[4,120]{1,0:T(4,128)S(1)}, f32[4,120]{1,0:T(4,128)S(1)}, u32[]{:S(2)}, u32[]{:S(2)}) collective-permute-start(f32[4,120]{1,0:T(4,128)S(1)} %get-tuple-element.47), channel_id=1, source_target_pairs={{0,2},{1,3},{2,0},{3,1},{4,6},{5,7},{6,4},{7,5},{8,10},{9,11},{10,... | collective-permute-start | bytes 5768 | tf_op jit(solution)/shard_map/ppermute | solution.py:378
  56.8 0.9 %collective-permute-start.3 = (f32[4,120]{1,0:T(4,128)S(1)}, f32[4,120]{1,0:T(4,128)S(1)}, u32[]{:S(2)}, u32[]{:S(2)}) collective-permute-start(f32[4,120]{1,0:T(4,128)S(1)} %get-tuple-element.47), channel_id=1, source_target_pairs={{0,1},{1,0},{2,3},{3,2},{4,5},{5,4},{6,7},{7,6},{8,9},{9,8},{10,11... | collective-permute-start | bytes 5768 | tf_op jit(solution)/shard_map/ppermute | solution.py:378
  57.7 1.2 %collective-permute-done.5 = f32[4,120]{1,0:T(4,128)S(1)} collective-permute-done((f32[4,120]{1,0:T(4,128)S(1)}, f32[4,120]{1,0:T(4,128)S(1)}, u32[]{:S(2)}, u32[]{:S(2)}) %collective-permute-start.5) | collective-permute-done | bytes 1952 | tf_op jit(solution)/shard_map/ppermute | solution.py:378
  58.9 0.6 collective-permute-done.4
  59.5 0.0 collective-permute-done.3
  59.5 0.6 add_add_fusion
  60.1 8.3 %all-to-all-done.1 = f32[64,4,120]{2,1,0:T(4,128)S(1)} async-done(((f32[64,4,120]{2,1,0:T(4,128)}), f32[64,4,120]{2,1,0:T(4,128)S(1)}, u32[]{:S(2)}, u32[]{:S(2)}) %all-to-all-start.1) | async-done | bytes 122912 | tf_op jit(solution)/shard_map/all_to_all | solution.py:381
  68.4 0.7 reduce_sum.9
  (8 shorter events, 0.0 us)
Async XLA Ops:
  0.6 10.1 %copy-start.6 = (f32[4]{0:T(128)S(1)}, f32[4]{0:T(128)}, u32[]{:S(2)}) copy-start(f32[4]{0:T(128)} %ek_ref) | copy-start | bytes 52
  0.6 10.1 %copy-start.5 = (f32[4,120]{1,0:T(4,128)S(1)}, f32[4,120]{1,0:T(4,128)}, u32[]{:S(2)}) copy-start(f32[4,120]{1,0:T(4,128)} %bose_ref.1) | copy-start | bytes 5764
  0.7 10.1 %copy-start.4 = (f32[4,120]{1,0:T(4,128)S(1)}, f32[4,120]{1,0:T(4,128)}, u32[]{:S(2)}) copy-start(f32[4,120]{1,0:T(4,128)} %omega_ref.1) | copy-start | bytes 5764
  0.7 10.1 %copy-start.7 = (f32[4]{0:T(128)S(1)}, f32[4]{0:T(128)}, u32[]{:S(2)}) copy-start(f32[4]{0:T(128)} %ok_ref.1) | copy-start | bytes 52
  0.7 10.1 %copy-start.3 = (f32[4,4,40]{2,1,0:T(4,128)S(1)}, f32[4,4,40]{2,1,0:T(4,128)}, u32[]{:S(2)}) copy-start(f32[4,4,40]{2,1,0:T(4,128)} %param.21) | copy-start | bytes 7684
  0.7 10.1 %copy-start.2 = (f32[4,4,40]{2,1,0:T(4,128)S(1)}, f32[4,4,40]{2,1,0:T(4,128)}, u32[]{:S(2)}) copy-start(f32[4,4,40]{2,1,0:T(4,128)} %param.20) | copy-start | bytes 7684
  0.7 10.1 %copy-start = (bf16[4,4,2,40,40]{4,3,2,1,0:T(8,128)(2,1)S(1)}, bf16[4,4,2,40,40]{4,3,2,1,0:T(8,128)(2,1)}, u32[]{:S(2)}) copy-start(bf16[4,4,2,40,40]{4,3,2,1,0:T(8,128)(2,1)} %param.19) | copy-start | bytes 307204
  0.7 47.8 %copy-start.1 = (bf16[4,2,120,120]{3,2,1,0:T(8,128)(2,1)S(1)}, bf16[4,2,120,120]{3,2,1,0:T(8,128)(2,1)}, u32[]{:S(2)}) copy-start(bf16[4,2,120,120]{3,2,1,0:T(8,128)(2,1)} %modes_ref) | copy-start | bytes 691204
  7.0 1.7 %collective-permute-start = (bf16[256,640]{1,0:T(8,128)(2,1)S(1)}, bf16[256,640]{1,0:T(8,128)(2,1)S(1)}, u32[]{:S(2)}, u32[]{:S(2)}) collective-permute-start(bf16[256,640]{1,0:T(8,128)(2,1)S(1)} %get-tuple-element.28), channel_id=1, source_target_pairs={{0,1},{1,0},{2,3},{3,2},{4,5},{5,4},{6,7},{7,6},{8,9},{9,8},{10,11... | collective-permute-start | bytes 983048 | tf_op jit(solution)/shard_map/ppermute | solution.py:349
  8.8 9.9 %collective-permute-start.2 = (bf16[256,640]{1,0:T(8,128)(2,1)S(1)}, bf16[256,640]{1,0:T(8,128)(2,1)S(1)}, u32[]{:S(2)}, u32[]{:S(2)}) collective-permute-start(bf16[256,640]{1,0:T(8,128)(2,1)S(1)} %add_convert_fusion.1), channel_id=1, source_target_pairs={{0,2},{1,3},{2,0},{3,1},{4,6},{5,7},{6,4},{7,5},{8,10},{9,11},{10,... | collective-permute-start | bytes 983048 | tf_op jit(solution)/shard_map/ppermute | solution.py:351
  12.4 6.4 %collective-permute-start.1 = (bf16[256,640]{1,0:T(8,128)(2,1)S(1)}, bf16[256,640]{1,0:T(8,128)(2,1)S(1)}, u32[]{:S(2)}, u32[]{:S(2)}) collective-permute-start(bf16[256,640]{1,0:T(8,128)(2,1)S(1)} %get-tuple-element.34), channel_id=1, source_target_pairs={{0,1},{1,0},{2,3},{3,2},{4,5},{5,4},{6,7},{7,6},{8,9},{9,8},{10,11... | collective-permute-start | bytes 983048 | tf_op jit(solution)/shard_map/ppermute | solution.py:363
  51.1 17.2 %all-to-all-start.1 = ((f32[64,4,120]{2,1,0:T(4,128)}), f32[64,4,120]{2,1,0:T(4,128)S(1)}, u32[]{:S(2)}, u32[]{:S(2)}) async-start(f32[64,4,120]{2,1,0:T(4,128)} %get-tuple-element.46), calls=%async_computation.1 | async-start | bytes 262144 | tf_op jit(solution)/shard_map/all_to_all | solution.py:381
  55.8 3.1 %collective-permute-start.5 = (f32[4,120]{1,0:T(4,128)S(1)}, f32[4,120]{1,0:T(4,128)S(1)}, u32[]{:S(2)}, u32[]{:S(2)}) collective-permute-start(f32[4,120]{1,0:T(4,128)S(1)} %get-tuple-element.47), channel_id=1, source_target_pairs={{0,3},{1,2},{2,1},{3,0},{4,7},{5,6},{6,5},{7,4},{8,11},{9,10},{10,... | collective-permute-start | bytes 5768 | tf_op jit(solution)/shard_map/ppermute | solution.py:378
  55.9 3.7 %collective-permute-start.4 = (f32[4,120]{1,0:T(4,128)S(1)}, f32[4,120]{1,0:T(4,128)S(1)}, u32[]{:S(2)}, u32[]{:S(2)}) collective-permute-start(f32[4,120]{1,0:T(4,128)S(1)} %get-tuple-element.47), channel_id=1, source_target_pairs={{0,2},{1,3},{2,0},{3,1},{4,6},{5,7},{6,4},{7,5},{8,10},{9,11},{10,... | collective-permute-start | bytes 5768 | tf_op jit(solution)/shard_map/ppermute | solution.py:378
  56.8 2.7 %collective-permute-start.3 = (f32[4,120]{1,0:T(4,128)S(1)}, f32[4,120]{1,0:T(4,128)S(1)}, u32[]{:S(2)}, u32[]{:S(2)}) collective-permute-start(f32[4,120]{1,0:T(4,128)S(1)} %get-tuple-element.47), channel_id=1, source_target_pairs={{0,1},{1,0},{2,3},{3,2},{4,5},{5,4},{6,7},{7,6},{8,9},{9,8},{10,11... | collective-permute-start | bytes 5768 | tf_op jit(solution)/shard_map/ppermute | solution.py:378

commit v8 on v7

--- a/solution.py
+++ b/solution.py
@@ -51,21 +51,23 @@
     ]
     for copy in small:
         copy.start()
-    for copy in small:
-        copy.wait()
     strips = []
     for first in range(0, pairs, STRIP):
         part = pl.ds(first, min(STRIP, pairs - first))
         strips.append(
             pltpu.make_async_copy(g_hbm.at[:, part], g_ref.at[:, part], strip_sem.at[len(strips)])
         )
-        strips[-1].start()
+    strips[0].start()
     blank = jnp.zeros((table.shape[0], pitch - phonons), bf16)
     for part in range(2):
         table[:, part * pitch + phonons : (part + 1) * pitch] = blank
         for slot in range(2):
             for g in range(0, rows.shape[1], table.shape[0]):
                 rows[slot, g : g + table.shape[0], part * pitch + phonons : (part + 1) * pitch] = blank
+    for copy in small:
+        copy.wait()
+    for strip in strips[1:]:
+        strip.start()
     mine = lax.axis_index("ka")
     kpt = kpt_ref[...].astype(f32).astype(bf16)
     qpt = qpt_ref[...].astype(f32).astype(bf16)

time: 69.3 us -> 68.7 us (level)
  no operation moved by 1% of the time
where the time goes in v8:
time: 68.7 us; the launch traced here: 68.5 us
  blocking collectives  29.4 us (43%)
  waiting for transfers between devices  18 us (26%)
  Pallas kernels  10.1 us (15%)
  starting transfers between devices  8.62 us (13%)
  other arithmetic  1.44 us (2%)
  between operations  0.81 us (1%)
    all_to_all x1, blocking collectives, on_device(): arrived = lax.all_to_all(chunks, 'pb', 0, 0, tiled=True)  29.4 us
    all_to_all x1, waiting for transfers between devices, on_device(): electrons = lax.all_to_all(copies, 'pb', 0, 0, tiled=True)  8.25 us
    ppermute x1, waiting for transfers between devices, on_device(): theirs = lax.ppermute(chip, 'ka', across)  6.26 us
    pallas_call x1, Pallas kernels, products(): pl.pallas_call(product_kernel, in_specs=[pl.BlockSpec(memory_space=pltpu....  5.93 us
    all_to_all x1, starting transfers between devices, on_device(): electrons = lax.all_to_all(copies, 'pb', 0, 0, tiled=True)  4.6 us
    pallas_call x1, Pallas kernels, widths(): pl.pallas_call(width_kernel, in_specs=[vmem] * 6, out_specs=[vmem] * 2, o...  2.59 us
    ppermute x3, starting transfers between devices, on_device(): lax.ppermute(phonon, 'ka', [(i, i ^ flip) for i in range(members)])  1.94 us
    ppermute x1, starting transfers between devices, on_device(): theirs = lax.ppermute(chip, 'ka', across)  1.89 us
  transfers between devices with their start and end apart: 7, of which 5 were waited for; matrix products, arithmetic and copies ran while one was open for 1% of the time, Pallas kernels for 2%

profile of v8, /device:TPU:32, one launch (start us, length us, event | category | flops | bytes accessed | tf_op | source)
XLA Modules:
  0.0 68.5 jit_solution(16030239891072408927)
XLA Ops:
  0.6 0.0 copy-start.6
  0.6 0.0 copy-start.5
  0.7 0.0 copy-start.4
  0.7 0.0 copy-start.7
  0.7 0.0 copy-start.3
  0.7 0.0 copy-start.2
  0.7 0.0 copy-start
  0.7 0.0 copy-start.1
  0.7 5.9 %shard_map.140 = (bf16[256,640]{1,0:T(8,128)(2,1)S(1)}, bf16[256,640]{1,0:T(8,128)(2,1)S(1)}, bf16[256,640]{1,0:T(8,128)(2,1)S(1)}, bf16[256,640]{1,0:T(8,128)(2,1)S(1)}) custom-call(s32[3,16]{1,0:T(4,128)} %kpt_hbm.1, s32[3,256]{1,0:T(4,128)} %qpt_hbm.1, s32[3,320]{1,0:T(4,128)} %ecell_hbm.1, s32[3,320]{1,0:T(4,128)} %pcell_hbm.1, ...), custom_call_target="tpu_custom_call" | custom-call | tf_op jit(solution)/shard_map/pallas_call | solution.py:144
  6.7 0.1 collective-permute-start
  6.8 1.6 %collective-permute-done = bf16[256,640]{1,0:T(8,128)(2,1)S(1)} collective-permute-done((bf16[256,640]{1,0:T(8,128)(2,1)S(1)}, bf16[256,640]{1,0:T(8,128)(2,1)S(1)}, u32[]{:S(2)}, u32[]{:S(2)}) %collective-permute-start) | collective-permute-done | bytes 327712 | tf_op jit(solution)/shard_map/ppermute | solution.py:351
  8.4 0.1 add_convert_fusion.1
  8.5 1.9 %collective-permute-start.2 = (bf16[256,640]{1,0:T(8,128)(2,1)S(1)}, bf16[256,640]{1,0:T(8,128)(2,1)S(1)}, u32[]{:S(2)}, u32[]{:S(2)}) collective-permute-start(bf16[256,640]{1,0:T(8,128)(2,1)S(1)} %add_convert_fusion.1), channel_id=1, source_target_pairs={{0,2},{1,3},{2,0},{3,1},{4,6},{5,7},{6,4},{7,5},{8,10},{9,11},{10,... | collective-permute-start | bytes 983048 | tf_op jit(solution)/shard_map/ppermute | solution.py:353
  10.4 1.6 %shard_map.141 = (f32[16,40,120]{2,1,0:T(8,128)S(1)}, f32[16,40,120]{2,1,0:T(8,128)S(1)}, bf16[16,80,40]{2,1,0:T(8,128)(2,1)S(1)}, bf16[640,1024]{1,0:T(8,128)(2,1)S(1)}) custom-call(f32[16,40]{1,0:T(8,128)S(1)} %bitcast.5, f32[16,40]{1,0:T(8,128)S(1)} %bitcast.6, f32[4,120]{1,0:T(4,128)S(1)} %copy-done.4, f32[4,120]{1,0:T(4,128)S(1)} %copy-done.5, ...), custom_call_target="tpu_custom_call" | custom-call | tf_op jit(solution)/shard_map/pallas_call | solution.py:204
  12.0 0.1 collective-permute-start.1
  12.1 6.3 %collective-permute-done.2 = bf16[256,640]{1,0:T(8,128)(2,1)S(1)} collective-permute-done((bf16[256,640]{1,0:T(8,128)(2,1)S(1)}, bf16[256,640]{1,0:T(8,128)(2,1)S(1)}, u32[]{:S(2)}, u32[]{:S(2)}) %collective-permute-start.2) | collective-permute-done | bytes 327712 | tf_op jit(solution)/shard_map/ppermute | solution.py:353
  18.4 0.0 collective-permute-done.1
  18.4 0.1 add_convert_fusion
  18.5 0.1 reshape.22
  18.6 29.4 %all_to_all.10 = bf16[64,4,640]{2,1,0:T(4,128)(2,1)S(1)} all-to-all(bf16[64,4,640]{2,1,0:T(4,128)(2,1)S(1)} %reshape.22), channel_id=1, replica_groups=mesh['pb'=64,'ka'=4] {'pb'}, dimensions={0} | all-to-all | bytes 655360 | tf_op jit(solution)/shard_map/all_to_all | solution.py:368
  47.9 0.1 reshape.23.block_ref
  48.0 2.6 %shard_map.142 = (f32[64,4,120]{2,1,0:T(4,128)}, f32[4,120]{1,0:T(4,128)S(1)}) custom-call(bf16[256,640]{1,0:T(8,128)(2,1)S(1)} %reshape.23.block_ref, bf16[4,2,120,120]{3,2,1,0:T(8,128)(2,1)S(1)} %copy-done.1, bf16[16,80,40]{2,1,0:T(8,128)(2,1)S(1)} %get-tuple-element.42.turned_ref, f32[16,40,120]{2,1,0:T(8,128)S(1)} %get-tuple-element.43.absorb_ref, ...), custom_call_target="tpu_custom_call" | custom-call | tf_op jit(solution)/shard_map/pallas_call | solution.py:307
  50.6 4.6 %all-to-all-start.1 = ((f32[64,4,120]{2,1,0:T(4,128)}), f32[64,4,120]{2,1,0:T(4,128)S(1)}, u32[]{:S(2)}, u32[]{:S(2)}) async-start(f32[64,4,120]{2,1,0:T(4,128)} %get-tuple-element.46), calls=%async_computation.1 | async-start | bytes 262144 | tf_op jit(solution)/shard_map/all_to_all | solution.py:383
  55.2 0.1 collective-permute-start.5
  55.3 1.1 %collective-permute-start.4 = (f32[4,120]{1,0:T(4,128)S(1)}, f32[4,120]{1,0:T(4,128)S(1)}, u32[]{:S(2)}, u32[]{:S(2)}) collective-permute-start(f32[4,120]{1,0:T(4,128)S(1)} %get-tuple-element.47), channel_id=1, source_target_pairs={{0,2},{1,3},{2,0},{3,1},{4,6},{5,7},{6,4},{7,5},{8,10},{9,11},{10,... | collective-permute-start | bytes 5768 | tf_op jit(solution)/shard_map/ppermute | solution.py:380
  56.4 0.7 %collective-permute-start.3 = (f32[4,120]{1,0:T(4,128)S(1)}, f32[4,120]{1,0:T(4,128)S(1)}, u32[]{:S(2)}, u32[]{:S(2)}) collective-permute-start(f32[4,120]{1,0:T(4,128)S(1)} %get-tuple-element.47), channel_id=1, source_target_pairs={{0,1},{1,0},{2,3},{3,2},{4,5},{5,4},{6,7},{7,6},{8,9},{9,8},{10,11... | collective-permute-start | bytes 5768 | tf_op jit(solution)/shard_map/ppermute | solution.py:380
  57.2 1.2 %collective-permute-done.5 = f32[4,120]{1,0:T(4,128)S(1)} collective-permute-done((f32[4,120]{1,0:T(4,128)S(1)}, f32[4,120]{1,0:T(4,128)S(1)}, u32[]{:S(2)}, u32[]{:S(2)}) %collective-permute-start.5) | collective-permute-done | bytes 1952 | tf_op jit(solution)/shard_map/ppermute | solution.py:380
  58.4 0.6 collective-permute-done.4
  59.0 0.0 collective-permute-done.3
  59.0 0.6 add_add_fusion
  59.6 8.3 %all-to-all-done.1 = f32[64,4,120]{2,1,0:T(4,128)S(1)} async-done(((f32[64,4,120]{2,1,0:T(4,128)}), f32[64,4,120]{2,1,0:T(4,128)S(1)}, u32[]{:S(2)}, u32[]{:S(2)}) %all-to-all-start.1) | async-done | bytes 122912 | tf_op jit(solution)/shard_map/all_to_all | solution.py:383
  67.8 0.7 reduce_sum.9
  (8 shorter events, 0.0 us)
Async XLA Ops:
  0.6 9.7 %copy-start.6 = (f32[4]{0:T(128)S(1)}, f32[4]{0:T(128)}, u32[]{:S(2)}) copy-start(f32[4]{0:T(128)} %ek_ref) | copy-start | bytes 52
  0.6 9.7 %copy-start.5 = (f32[4,120]{1,0:T(4,128)S(1)}, f32[4,120]{1,0:T(4,128)}, u32[]{:S(2)}) copy-start(f32[4,120]{1,0:T(4,128)} %bose_ref.1) | copy-start | bytes 5764
  0.7 9.7 %copy-start.4 = (f32[4,120]{1,0:T(4,128)S(1)}, f32[4,120]{1,0:T(4,128)}, u32[]{:S(2)}) copy-start(f32[4,120]{1,0:T(4,128)} %omega_ref.1) | copy-start | bytes 5764
  0.7 9.7 %copy-start.7 = (f32[4]{0:T(128)S(1)}, f32[4]{0:T(128)}, u32[]{:S(2)}) copy-start(f32[4]{0:T(128)} %ok_ref.1) | copy-start | bytes 52
  0.7 9.7 %copy-start.3 = (f32[4,4,40]{2,1,0:T(4,128)S(1)}, f32[4,4,40]{2,1,0:T(4,128)}, u32[]{:S(2)}) copy-start(f32[4,4,40]{2,1,0:T(4,128)} %param.21) | copy-start | bytes 7684
  0.7 9.7 %copy-start.2 = (f32[4,4,40]{2,1,0:T(4,128)S(1)}, f32[4,4,40]{2,1,0:T(4,128)}, u32[]{:S(2)}) copy-start(f32[4,4,40]{2,1,0:T(4,128)} %param.20) | copy-start | bytes 7684
  0.7 9.7 %copy-start = (bf16[4,4,2,40,40]{4,3,2,1,0:T(8,128)(2,1)S(1)}, bf16[4,4,2,40,40]{4,3,2,1,0:T(8,128)(2,1)}, u32[]{:S(2)}) copy-start(bf16[4,4,2,40,40]{4,3,2,1,0:T(8,128)(2,1)} %param.19) | copy-start | bytes 307204
  0.7 47.3 %copy-start.1 = (bf16[4,2,120,120]{3,2,1,0:T(8,128)(2,1)S(1)}, bf16[4,2,120,120]{3,2,1,0:T(8,128)(2,1)}, u32[]{:S(2)}) copy-start(bf16[4,2,120,120]{3,2,1,0:T(8,128)(2,1)} %modes_ref) | copy-start | bytes 691204
  6.7 1.7 %collective-permute-start = (bf16[256,640]{1,0:T(8,128)(2,1)S(1)}, bf16[256,640]{1,0:T(8,128)(2,1)S(1)}, u32[]{:S(2)}, u32[]{:S(2)}) collective-permute-start(bf16[256,640]{1,0:T(8,128)(2,1)S(1)} %get-tuple-element.28), channel_id=1, source_target_pairs={{0,1},{1,0},{2,3},{3,2},{4,5},{5,4},{6,7},{7,6},{8,9},{9,8},{10,11... | collective-permute-start | bytes 983048 | tf_op jit(solution)/shard_map/ppermute | solution.py:351
  8.5 9.9 %collective-permute-start.2 = (bf16[256,640]{1,0:T(8,128)(2,1)S(1)}, bf16[256,640]{1,0:T(8,128)(2,1)S(1)}, u32[]{:S(2)}, u32[]{:S(2)}) collective-permute-start(bf16[256,640]{1,0:T(8,128)(2,1)S(1)} %add_convert_fusion.1), channel_id=1, source_target_pairs={{0,2},{1,3},{2,0},{3,1},{4,6},{5,7},{6,4},{7,5},{8,10},{9,11},{10,... | collective-permute-start | bytes 983048 | tf_op jit(solution)/shard_map/ppermute | solution.py:353
  12.0 6.4 %collective-permute-start.1 = (bf16[256,640]{1,0:T(8,128)(2,1)S(1)}, bf16[256,640]{1,0:T(8,128)(2,1)S(1)}, u32[]{:S(2)}, u32[]{:S(2)}) collective-permute-start(bf16[256,640]{1,0:T(8,128)(2,1)S(1)} %get-tuple-element.34), channel_id=1, source_target_pairs={{0,1},{1,0},{2,3},{3,2},{4,5},{5,4},{6,7},{7,6},{8,9},{9,8},{10,11... | collective-permute-start | bytes 983048 | tf_op jit(solution)/shard_map/ppermute | solution.py:365
  50.6 17.2 %all-to-all-start.1 = ((f32[64,4,120]{2,1,0:T(4,128)}), f32[64,4,120]{2,1,0:T(4,128)S(1)}, u32[]{:S(2)}, u32[]{:S(2)}) async-start(f32[64,4,120]{2,1,0:T(4,128)} %get-tuple-element.46), calls=%async_computation.1 | async-start | bytes 262144 | tf_op jit(solution)/shard_map/all_to_all | solution.py:383
  55.2 3.2 %collective-permute-start.5 = (f32[4,120]{1,0:T(4,128)S(1)}, f32[4,120]{1,0:T(4,128)S(1)}, u32[]{:S(2)}, u32[]{:S(2)}) collective-permute-start(f32[4,120]{1,0:T(4,128)S(1)} %get-tuple-element.47), channel_id=1, source_target_pairs={{0,3},{1,2},{2,1},{3,0},{4,7},{5,6},{6,5},{7,4},{8,11},{9,10},{10,... | collective-permute-start | bytes 5768 | tf_op jit(solution)/shard_map/ppermute | solution.py:380
  55.3 3.7 %collective-permute-start.4 = (f32[4,120]{1,0:T(4,128)S(1)}, f32[4,120]{1,0:T(4,128)S(1)}, u32[]{:S(2)}, u32[]{:S(2)}) collective-permute-start(f32[4,120]{1,0:T(4,128)S(1)} %get-tuple-element.47), channel_id=1, source_target_pairs={{0,2},{1,3},{2,0},{3,1},{4,6},{5,7},{6,4},{7,5},{8,10},{9,11},{10,... | collective-permute-start | bytes 5768 | tf_op jit(solution)/shard_map/ppermute | solution.py:380
  56.4 2.6 %collective-permute-start.3 = (f32[4,120]{1,0:T(4,128)S(1)}, f32[4,120]{1,0:T(4,128)S(1)}, u32[]{:S(2)}, u32[]{:S(2)}) collective-permute-start(f32[4,120]{1,0:T(4,128)S(1)} %get-tuple-element.47), channel_id=1, source_target_pairs={{0,1},{1,0},{2,3},{3,2},{4,5},{5,4},{6,7},{7,6},{8,9},{9,8},{10,11... | collective-permute-start | bytes 5768 | tf_op jit(solution)/shard_map/ppermute | solution.py:380

commit v9 on v8

--- a/solution.py
+++ b/solution.py
@@ -160,7 +160,7 @@
 
 def table_kernel(
     level_ref, filled_ref, omega_ref, bose_ref, vector_ref, ek_ref, ok_ref,
-    absorb_ref, count_ref, turned_ref, pick_ref,
+    absorb_ref, count_ref, turned_ref, pick_ref, order_ref,
 ):
     f32 = jnp.float32
     points = level_ref.shape[0]
@@ -192,9 +192,17 @@
     place = col % LANES
     wanted = (place // STRIP) * LANES + (place % STRIP) * PARTS + col // LANES
     pick_ref[...] = (lane == wanted).astype(f32).astype(jnp.bfloat16)
-
-
-def tables(levels, filled, frequencies, bose, vectors, energy_k, occupation_k, width):
+    rows = order_ref.shape[0]
+    phases = 8
+    runs = rows // q_local // phases
+    to = lax.broadcasted_iota(jnp.int32, (rows, rows), 0)
+    source = lax.broadcasted_iota(jnp.int32, (rows, rows), 1)
+    wanted = (to % runs) * (phases * q_local) + (to // runs) % phases * q_local
+    wanted = wanted + to // (runs * phases)
+    order_ref[...] = (source == wanted).astype(f32).astype(jnp.bfloat16)
+
+
+def tables(levels, filled, frequencies, bose, vectors, energy_k, occupation_k, width, q_total):
     q_local, k_local, bands = levels.shape
     points = q_local * k_local
     modes = frequencies.shape[1]
@@ -204,12 +212,13 @@
     return pl.pallas_call(
         table_kernel,
         in_specs=[vmem] * 5 + [smem] * 2,
-        out_specs=[vmem] * 4,
+        out_specs=[vmem] * 5,
         out_shape=[
             weight,
             weight,
             jax.ShapeDtypeStruct((points, 2 * bands, bands), jnp.bfloat16),
             jax.ShapeDtypeStruct((width, PARTS * LANES), jnp.bfloat16),
+            jax.ShapeDtypeStruct((q_total, q_total), jnp.bfloat16),
         ],
         compiler_params=pltpu.CompilerParams(vmem_limit_bytes=48 << 20),
     )(
@@ -224,7 +233,7 @@
 
 
 def width_kernel(
-    block_ref, modes_ref, turned_ref, absorb_ref, count_ref, pick_ref,
+    block_ref, modes_ref, turned_ref, absorb_ref, count_ref, pick_ref, order_ref,
     copies_ref, phonon_ref, spread, cycle, moded,
 ):
     f32 = jnp.float32
@@ -237,12 +246,7 @@
     sources = rows // q_local
     phases = 8
     runs = sources // phases
-    to = lax.broadcasted_iota(jnp.int32, (rows, rows), 0)
-    source = lax.broadcasted_iota(jnp.int32, (rows, rows), 1)
-    wanted = (to % runs) * (phases * q_local) + (to // runs) % phases * q_local
-    wanted = wanted + to // (runs * phases)
-    order = (source == wanted).astype(f32).astype(bf16)
-    block = jnp.dot(order, block_ref[...], preferred_element_type=f32).astype(bf16)
+    block = jnp.dot(order_ref[...], block_ref[...], preferred_element_type=f32).astype(bf16)
     for part in range(0, PARTS, 2):
         two = jnp.dot(
             block, pick_ref[:, part * LANES : (part + 2) * LANES], preferred_element_type=f32
@@ -300,13 +304,13 @@
     copies_ref[...] = jnp.broadcast_to(jnp.concatenate(electron, axis=0)[None], copies_ref.shape)
 
 
-def widths(block, phonon_modes, turned, absorb, count, pick, members):
+def widths(block, phonon_modes, turned, absorb, count, pick, order, members):
     q_local, _, modes, _ = phonon_modes.shape
     rows = block.shape[0]
     vmem = pl.BlockSpec(memory_space=pltpu.VMEM)
     return pl.pallas_call(
         width_kernel,
-        in_specs=[vmem] * 6,
+        in_specs=[vmem] * 7,
         out_specs=[vmem] * 2,
         out_shape=[
             jax.ShapeDtypeStruct((members, PARTS // 2, modes), jnp.float32),
@@ -318,7 +322,7 @@
             pltpu.VMEM((q_local * PARTS // 2, 2, NB, LANES), jnp.float32),
         ],
         compiler_params=pltpu.CompilerParams(vmem_limit_bytes=48 << 20),
-    )(block, phonon_modes, turned, absorb, count, pick)
+    )(block, phonon_modes, turned, absorb, count, pick, order)
 
 
 def added(*arrays):
@@ -360,13 +364,14 @@
         energy_k,
         occupation_k,
         width,
+        q_total,
     )
     near_send, prepared = lax.optimization_barrier((near_send, prepared))
     near = lax.ppermute(near_send, "ka", beside)
     chunks = added(near_keep, near, theirs).reshape(q_total // q_local, q_local, width)
     chunks, prepared, phonon_modes = lax.optimization_barrier((chunks, prepared, phonon_modes))
     arrived = lax.all_to_all(chunks, "pb", 0, 0, tiled=True)
-    absorb, count, turned, pick = prepared
+    absorb, count, turned, pick, order = prepared
     copies, phonon = widths(
         arrived.reshape(q_total, width),
         phonon_modes,
@@ -374,6 +379,7 @@
         absorb,
         count,
         pick,
+        order,
         q_total // q_local,
     )
     phonons = [phonon] + [

time: 68.7 us -> 68.7 us (level)
  no operation moved by 1% of the time
where the time goes in v9:
time: 68.7 us; the launch traced here: 68.5 us
  blocking collectives  29.4 us (43%)
  waiting for transfers between devices  17.9 us (26%)
  Pallas kernels  10.2 us (15%)
  starting transfers between devices  8.62 us (13%)
  other arithmetic  1.45 us (2%)
  between operations  0.81 us (1%)
    all_to_all x1, blocking collectives, on_device(): arrived = lax.all_to_all(chunks, 'pb', 0, 0, tiled=True)  29.4 us
    all_to_all x1, waiting for transfers between devices, on_device(): electrons = lax.all_to_all(copies, 'pb', 0, 0, tiled=True)  8.25 us
    ppermute x1, waiting for transfers between devices, on_device(): theirs = lax.ppermute(chip, 'ka', across)  6.18 us
    pallas_call x1, Pallas kernels, products(): pl.pallas_call(product_kernel, in_specs=[pl.BlockSpec(memory_space=pltpu....  5.93 us
    all_to_all x1, starting transfers between devices, on_device(): electrons = lax.all_to_all(copies, 'pb', 0, 0, tiled=True)  4.6 us
    pallas_call x1, Pallas kernels, widths(): pl.pallas_call(width_kernel, in_specs=[vmem] * 7, out_specs=[vmem] * 2, o...  2.61 us
    ppermute x3, starting transfers between devices, on_device(): lax.ppermute(phonon, 'ka', [(i, i ^ flip) for i in range(members)])  1.94 us
    ppermute x1, starting transfers between devices, on_device(): theirs = lax.ppermute(chip, 'ka', across)  1.89 us
  transfers between devices with their start and end apart: 7, of which 5 were waited for; matrix products, arithmetic and copies ran while one was open for 1% of the time, Pallas kernels for 2%

profile of v9, /device:TPU:32, one launch (start us, length us, event | category | flops | bytes accessed | tf_op | source)
XLA Modules:
  0.0 68.5 jit_solution(8865112313329206408)
XLA Ops:
  0.6 0.0 copy-start.6
  0.6 0.0 copy-start.5
  0.7 0.0 copy-start.4
  0.7 0.0 copy-start.7
  0.7 5.9 %shard_map.140 = (bf16[256,640]{1,0:T(8,128)(2,1)S(1)}, bf16[256,640]{1,0:T(8,128)(2,1)S(1)}, bf16[256,640]{1,0:T(8,128)(2,1)S(1)}, bf16[256,640]{1,0:T(8,128)(2,1)S(1)}) custom-call(s32[3,16]{1,0:T(4,128)} %kpt_hbm.1, s32[3,256]{1,0:T(4,128)} %qpt_hbm.1, s32[3,320]{1,0:T(4,128)} %ecell_hbm.1, s32[3,320]{1,0:T(4,128)} %pcell_hbm.1, ...), custom_call_target="tpu_custom_call" | custom-call | tf_op jit(solution)/shard_map/pallas_call | solution.py:144
  6.7 0.1 collective-permute-start
  6.8 1.6 %collective-permute-done = bf16[256,640]{1,0:T(8,128)(2,1)S(1)} collective-permute-done((bf16[256,640]{1,0:T(8,128)(2,1)S(1)}, bf16[256,640]{1,0:T(8,128)(2,1)S(1)}, u32[]{:S(2)}, u32[]{:S(2)}) %collective-permute-start) | collective-permute-done | bytes 327712 | tf_op jit(solution)/shard_map/ppermute | solution.py:355
  8.4 0.1 add_convert_fusion.1
  8.5 1.9 %collective-permute-start.2 = (bf16[256,640]{1,0:T(8,128)(2,1)S(1)}, bf16[256,640]{1,0:T(8,128)(2,1)S(1)}, u32[]{:S(2)}, u32[]{:S(2)}) collective-permute-start(bf16[256,640]{1,0:T(8,128)(2,1)S(1)} %add_convert_fusion.1), channel_id=1, source_target_pairs={{0,2},{1,3},{2,0},{3,1},{4,6},{5,7},{6,4},{7,5},{8,10},{9,11},{10,... | collective-permute-start | bytes 983048 | tf_op jit(solution)/shard_map/ppermute | solution.py:357
  10.3 0.0 copy-done.6
  10.4 0.0 copy-done.3
  10.4 0.0 copy-done.2
  10.4 0.0 copy-done
  10.4 1.7 %shard_map.141 = (f32[16,40,120]{2,1,0:T(8,128)S(1)}, f32[16,40,120]{2,1,0:T(8,128)S(1)}, bf16[16,80,40]{2,1,0:T(8,128)(2,1)S(1)}, bf16[640,1024]{1,0:T(8,128)(2,1)S(1)}, bf16[256,256]{1,0:T(8,128)(2,1)S(1)}) custom-call(f32[16,40]{1,0:T(8,128)S(1)} %bitcast.5, f32[16,40]{1,0:T(8,128)S(1)} %bitcast.6, f32[4,120]{1,0:T(4,128)S(1)} %copy-done.4, ...), custom_call_target="tpu_custom_call" | custom-call | tf_op jit(solution)/shard_map/pallas_call | solution.py:212
  12.1 0.1 collective-permute-start.1
  12.2 6.2 %collective-permute-done.2 = bf16[256,640]{1,0:T(8,128)(2,1)S(1)} collective-permute-done((bf16[256,640]{1,0:T(8,128)(2,1)S(1)}, bf16[256,640]{1,0:T(8,128)(2,1)S(1)}, u32[]{:S(2)}, u32[]{:S(2)}) %collective-permute-start.2) | collective-permute-done | bytes 327712 | tf_op jit(solution)/shard_map/ppermute | solution.py:357
  18.4 0.0 collective-permute-done.1
  18.4 0.1 add_convert_fusion
  18.5 0.1 reshape.22
  18.6 29.4 %all_to_all.10 = bf16[64,4,640]{2,1,0:T(4,128)(2,1)S(1)} all-to-all(bf16[64,4,640]{2,1,0:T(4,128)(2,1)S(1)} %reshape.22), channel_id=1, replica_groups=mesh['pb'=64,'ka'=4] {'pb'}, dimensions={0} | all-to-all | bytes 655360 | tf_op jit(solution)/shard_map/all_to_all | solution.py:373
  47.9 0.1 reshape.23.block_ref
  48.0 2.6 %shard_map.142 = (f32[64,4,120]{2,1,0:T(4,128)}, f32[4,120]{1,0:T(4,128)S(1)}) custom-call(bf16[256,640]{1,0:T(8,128)(2,1)S(1)} %reshape.23.block_ref, bf16[4,2,120,120]{3,2,1,0:T(8,128)(2,1)S(1)} %copy-done.1, bf16[16,80,40]{2,1,0:T(8,128)(2,1)S(1)} %get-tuple-element.47.turned_ref, f32[16,40,120]{2,1,0:T(8,128)S(1)} %get-tuple-element.48.absorb_ref, ...), custom_call_target="tpu_custom_call" | custom-call | tf_op jit(solution)/shard_map/pallas_call | solution.py:311
  50.6 4.6 %all-to-all-start.1 = ((f32[64,4,120]{2,1,0:T(4,128)}), f32[64,4,120]{2,1,0:T(4,128)S(1)}, u32[]{:S(2)}, u32[]{:S(2)}) async-start(f32[64,4,120]{2,1,0:T(4,128)} %get-tuple-element.52), calls=%async_computation.1 | async-start | bytes 262144 | tf_op jit(solution)/shard_map/all_to_all | solution.py:389
  55.2 0.1 collective-permute-start.5
  55.3 1.1 %collective-permute-start.4 = (f32[4,120]{1,0:T(4,128)S(1)}, f32[4,120]{1,0:T(4,128)S(1)}, u32[]{:S(2)}, u32[]{:S(2)}) collective-permute-start(f32[4,120]{1,0:T(4,128)S(1)} %get-tuple-element.53), channel_id=1, source_target_pairs={{0,2},{1,3},{2,0},{3,1},{4,6},{5,7},{6,4},{7,5},{8,10},{9,11},{10,... | collective-permute-start | bytes 5768 | tf_op jit(solution)/shard_map/ppermute | solution.py:386
  56.5 0.7 %collective-permute-start.3 = (f32[4,120]{1,0:T(4,128)S(1)}, f32[4,120]{1,0:T(4,128)S(1)}, u32[]{:S(2)}, u32[]{:S(2)}) collective-permute-start(f32[4,120]{1,0:T(4,128)S(1)} %get-tuple-element.53), channel_id=1, source_target_pairs={{0,1},{1,0},{2,3},{3,2},{4,5},{5,4},{6,7},{7,6},{8,9},{9,8},{10,11... | collective-permute-start | bytes 5768 | tf_op jit(solution)/shard_map/ppermute | solution.py:386
  57.2 1.2 %collective-permute-done.5 = f32[4,120]{1,0:T(4,128)S(1)} collective-permute-done((f32[4,120]{1,0:T(4,128)S(1)}, f32[4,120]{1,0:T(4,128)S(1)}, u32[]{:S(2)}, u32[]{:S(2)}) %collective-permute-start.5) | collective-permute-done | bytes 1952 | tf_op jit(solution)/shard_map/ppermute | solution.py:386
  58.4 0.6 collective-permute-done.4
  59.0 0.0 collective-permute-done.3
  59.0 0.6 add_add_fusion
  59.6 8.3 %all-to-all-done.1 = f32[64,4,120]{2,1,0:T(4,128)S(1)} async-done(((f32[64,4,120]{2,1,0:T(4,128)}), f32[64,4,120]{2,1,0:T(4,128)S(1)}, u32[]{:S(2)}, u32[]{:S(2)}) %all-to-all-start.1) | async-done | bytes 122912 | tf_op jit(solution)/shard_map/all_to_all | solution.py:389
  67.9 0.7 reduce_sum.9
  (8 shorter events, 0.0 us)
Async XLA Ops:
  0.6 9.7 %copy-start.6 = (f32[4]{0:T(128)S(1)}, f32[4]{0:T(128)}, u32[]{:S(2)}) copy-start(f32[4]{0:T(128)} %ek_ref) | copy-start | bytes 52
  0.6 9.7 %copy-start.5 = (f32[4,120]{1,0:T(4,128)S(1)}, f32[4,120]{1,0:T(4,128)}, u32[]{:S(2)}) copy-start(f32[4,120]{1,0:T(4,128)} %bose_ref.1) | copy-start | bytes 5764
  0.7 9.7 %copy-start.4 = (f32[4,120]{1,0:T(4,128)S(1)}, f32[4,120]{1,0:T(4,128)}, u32[]{:S(2)}) copy-start(f32[4,120]{1,0:T(4,128)} %omega_ref.1) | copy-start | bytes 5764
  0.7 9.7 %copy-start.7 = (f32[4]{0:T(128)S(1)}, f32[4]{0:T(128)}, u32[]{:S(2)}) copy-start(f32[4]{0:T(128)} %ok_ref.1) | copy-start | bytes 52
  0.7 9.7 %copy-start.3 = (f32[4,4,40]{2,1,0:T(4,128)S(1)}, f32[4,4,40]{2,1,0:T(4,128)}, u32[]{:S(2)}) copy-start(f32[4,4,40]{2,1,0:T(4,128)} %param.21) | copy-start | bytes 7684
  0.7 9.7 %copy-start.2 = (f32[4,4,40]{2,1,0:T(4,128)S(1)}, f32[4,4,40]{2,1,0:T(4,128)}, u32[]{:S(2)}) copy-start(f32[4,4,40]{2,1,0:T(4,128)} %param.20) | copy-start | bytes 7684
  0.7 9.7 %copy-start = (bf16[4,4,2,40,40]{4,3,2,1,0:T(8,128)(2,1)S(1)}, bf16[4,4,2,40,40]{4,3,2,1,0:T(8,128)(2,1)}, u32[]{:S(2)}) copy-start(bf16[4,4,2,40,40]{4,3,2,1,0:T(8,128)(2,1)} %param.19) | copy-start | bytes 307204
  0.7 47.3 %copy-start.1 = (bf16[4,2,120,120]{3,2,1,0:T(8,128)(2,1)S(1)}, bf16[4,2,120,120]{3,2,1,0:T(8,128)(2,1)}, u32[]{:S(2)}) copy-start(bf16[4,2,120,120]{3,2,1,0:T(8,128)(2,1)} %modes_ref) | copy-start | bytes 691204
  6.7 1.7 %collective-permute-start = (bf16[256,640]{1,0:T(8,128)(2,1)S(1)}, bf16[256,640]{1,0:T(8,128)(2,1)S(1)}, u32[]{:S(2)}, u32[]{:S(2)}) collective-permute-start(bf16[256,640]{1,0:T(8,128)(2,1)S(1)} %get-tuple-element.31), channel_id=1, source_target_pairs={{0,1},{1,0},{2,3},{3,2},{4,5},{5,4},{6,7},{7,6},{8,9},{9,8},{10,11... | collective-permute-start | bytes 983048 | tf_op jit(solution)/shard_map/ppermute | solution.py:355
  8.5 9.9 %collective-permute-start.2 = (bf16[256,640]{1,0:T(8,128)(2,1)S(1)}, bf16[256,640]{1,0:T(8,128)(2,1)S(1)}, u32[]{:S(2)}, u32[]{:S(2)}) collective-permute-start(bf16[256,640]{1,0:T(8,128)(2,1)S(1)} %add_convert_fusion.1), channel_id=1, source_target_pairs={{0,2},{1,3},{2,0},{3,1},{4,6},{5,7},{6,4},{7,5},{8,10},{9,11},{10,... | collective-permute-start | bytes 983048 | tf_op jit(solution)/shard_map/ppermute | solution.py:357
  12.1 6.3 %collective-permute-start.1 = (bf16[256,640]{1,0:T(8,128)(2,1)S(1)}, bf16[256,640]{1,0:T(8,128)(2,1)S(1)}, u32[]{:S(2)}, u32[]{:S(2)}) collective-permute-start(bf16[256,640]{1,0:T(8,128)(2,1)S(1)} %get-tuple-element.38), channel_id=1, source_target_pairs={{0,1},{1,0},{2,3},{3,2},{4,5},{5,4},{6,7},{7,6},{8,9},{9,8},{10,11... | collective-permute-start | bytes 983048 | tf_op jit(solution)/shard_map/ppermute | solution.py:370
  50.6 17.2 %all-to-all-start.1 = ((f32[64,4,120]{2,1,0:T(4,128)}), f32[64,4,120]{2,1,0:T(4,128)S(1)}, u32[]{:S(2)}, u32[]{:S(2)}) async-start(f32[64,4,120]{2,1,0:T(4,128)} %get-tuple-element.52), calls=%async_computation.1 | async-start | bytes 262144 | tf_op jit(solution)/shard_map/all_to_all | solution.py:389
  55.2 3.2 %collective-permute-start.5 = (f32[4,120]{1,0:T(4,128)S(1)}, f32[4,120]{1,0:T(4,128)S(1)}, u32[]{:S(2)}, u32[]{:S(2)}) collective-permute-start(f32[4,120]{1,0:T(4,128)S(1)} %get-tuple-element.53), channel_id=1, source_target_pairs={{0,3},{1,2},{2,1},{3,0},{4,7},{5,6},{6,5},{7,4},{8,11},{9,10},{10,... | collective-permute-start | bytes 5768 | tf_op jit(solution)/shard_map/ppermute | solution.py:386
  55.3 3.7 %collective-permute-start.4 = (f32[4,120]{1,0:T(4,128)S(1)}, f32[4,120]{1,0:T(4,128)S(1)}, u32[]{:S(2)}, u32[]{:S(2)}) collective-permute-start(f32[4,120]{1,0:T(4,128)S(1)} %get-tuple-element.53), channel_id=1, source_target_pairs={{0,2},{1,3},{2,0},{3,1},{4,6},{5,7},{6,4},{7,5},{8,10},{9,11},{10,... | collective-permute-start | bytes 5768 | tf_op jit(solution)/shard_map/ppermute | solution.py:386
  56.5 2.6 %collective-permute-start.3 = (f32[4,120]{1,0:T(4,128)S(1)}, f32[4,120]{1,0:T(4,128)S(1)}, u32[]{:S(2)}, u32[]{:S(2)}) collective-permute-start(f32[4,120]{1,0:T(4,128)S(1)} %get-tuple-element.53), channel_id=1, source_target_pairs={{0,1},{1,0},{2,3},{3,2},{4,5},{5,4},{6,7},{7,6},{8,9},{9,8},{10,11... | collective-permute-start | bytes 5768 | tf_op jit(solution)/shard_map/ppermute | solution.py:386
